TPU v7x, 256 devices: a whole 4x4x8 slice. The times are simulated.
256 devices in a mesh: ang: 64 (over x, y, z_hi), rad: 4 (over z_lo, core).
Axes of the slice: x: 4, y: 4, z: 8 (z_hi: 4, z_lo: 2; z = z_hi * 2 + z_lo), core: 2. Of those that a mesh axis runs over, the one named last changes fastest.
Arguments:
- coarse: float32 [1, 64, 32, 512], P(None, 'ang', None, 'rad'), may hold values from -6 to 6
- excite: float32 [1, 128, 64, 1024], P(None, 'ang', None, 'rad'), may hold values from -6 to 6
- kernels: float32 [27, 8, 512], replicated, may hold values from -0.875 to 0.875
- mixing: float32 [8, 8, 512], replicated, may hold values from -1.5 to 1.5
- star_bin: int32 [128, 64, 16], P('ang'), may hold values from 0 to 1023
- star_count: int32 [128, 64], P('ang'), may hold values from 1 to 16
- star_obs: float32 [128, 64, 16], P('ang'), may hold values from 0 to 3
- star_isig: float32 [128, 64, 16], P('ang'), may hold values from 1 to 10
Outputs:
- grad_excite: float32 [1, 128, 64, 1024], P(None, 'ang', None, 'rad')
- grad_coarse: float32 [1, 64, 32, 512], P(None, 'ang', None, 'rad')
All inputs are finite; a program needn't handle non-finite values.
Results may differ from a plain program's by a relative error of at most 0.0003.
Values sent between devices are 32-bit elements; how exact they have to be, the bound alone decides.
No kernel may reach another device: no remote copies, remote signals or barrier semaphores. Data moves between devices by JAX's collectives and lax.ppermute only.
A program may use at most 64 MiB of HBM per device.

v0:
```python
import jax
import jax.numpy as jnp
from jax import lax
from jax.sharding import PartitionSpec as P


def extended(block, sides, width):
    for axis, dim in sides:
        count = lax.axis_size(axis)
        forward = [(i, i + 1) for i in range(count - 1)]
        backward = [(target, source) for source, target in forward]
        low = lax.ppermute(
            lax.slice_in_dim(block, block.shape[dim] - width, None, axis=dim), axis, forward
        )
        high = lax.ppermute(lax.slice_in_dim(block, 0, width, axis=dim), axis, backward)
        block = jnp.concatenate([low, block, high], axis=dim)
    return block


def prefix(shard, axis, combine, identity, reverse):
    length, index = (lax.axis_size(axis), lax.axis_index(axis))
    everything = lax.all_gather(shard, axis)
    start = jnp.broadcast_to(jnp.asarray(identity, shard.dtype), shard.shape)

    def hop(k, before):
        at = length - 1 - k if reverse else k
        reached = at > index if reverse else at < index
        new = combine(before, everything[at])
        return jnp.where(reached, new, before)

    return lax.fori_loop(0, length, hop, start)


def to_blocks(field):
    samples, na, nb, nr = field.shape
    return (
        field.reshape(samples, na // 2, 2, nb // 2, 2, nr // 2, 2)
        .transpose(2, 4, 6, 0, 1, 3, 5)
        .reshape(8, samples, na // 2, nb // 2, nr // 2)
    )


def from_blocks(blocks):
    _, samples, na, nb, nr = blocks.shape
    return (
        blocks.reshape(2, 2, 2, samples, na, nb, nr)
        .transpose(3, 4, 0, 5, 1, 6, 2)
        .reshape(samples, 2 * na, 2 * nb, 2 * nr)
    )


def add_up(earlier, later):
    return earlier + later


def per_device(coarse, excite, kernels, mixing, star_bin, star_count, star_obs, star_isig):
    samples, rows_c, cols_c, depth_c = coarse.shape
    rows_f, cols_f, depth_f = (2 * rows_c, 2 * cols_c, 2 * depth_c)
    rad_index = lax.axis_index("rad")
    rad_count = lax.axis_size("rad")
    step_len = 1.0 / (depth_f * rad_count)
    kernel_pad = jnp.pad(kernels, ((0, 0), (0, 0), (1, 1)), mode="edge")
    kernel_wide = lax.dynamic_slice_in_dim(kernel_pad, rad_index * depth_c, depth_c + 2, 2)
    kernel_here = kernel_wide[:, :, 1:-1]
    mixing_here = lax.dynamic_slice_in_dim(mixing, rad_index * depth_c, depth_c, 2)
    framed = extended(coarse, (("ang", 1), ("rad", 3)), 1)
    framed = jnp.pad(framed, ((0, 0), (0, 0), (1, 1), (0, 0)))
    fine = jnp.zeros((8, samples, rows_c, cols_c, depth_c), jnp.float32)
    for offset in range(27):
        step_a, step_b, step_r = (offset // 9, offset // 3 % 3, offset % 3)
        window = framed[
            :, step_a : step_a + rows_c, step_b : step_b + cols_c, step_r : step_r + depth_c
        ]
        fine = fine + kernel_here[offset][:, None, None, None, :] * window[None]
    excite_blocks = to_blocks(excite)
    fine = fine + jnp.einsum(
        "qpr,psabr->qsabr", mixing_here, excite_blocks, precision=lax.Precision.HIGHEST
    )
    dens = jnp.exp(from_blocks(fine))
    ladder = jnp.arange(depth_f)
    upper = (ladder[:, None] <= ladder[None, :]).astype(jnp.float32)
    cumul = jnp.dot(dens.reshape(-1, depth_f), upper, precision=lax.Precision.HIGHEST).reshape(
        dens.shape
    )
    depth_sums = cumul[..., -1]
    nearer = prefix(depth_sums, "rad", add_up, jnp.zeros_like(depth_sums), False)
    extinction = step_len * (nearer[..., None] + cumul)
    local_bin = star_bin - rad_index * depth_f
    live = jnp.arange(star_bin.shape[2])[None, None, :] < star_count[:, :, None]
    inside = live & (local_bin >= 0) & (local_bin < depth_f)
    clipped = jnp.clip(local_bin, 0, depth_f - 1)
    pred = jnp.take_along_axis(extinction, clipped[None], axis=3)
    res = jnp.where(inside[None], (pred - star_obs[None]) * star_isig[None], 0.0)
    terms = res * star_isig[None]
    onehot = ((clipped[..., None] == ladder) & inside[..., None]).astype(jnp.float32)
    hits = jnp.einsum("sabm,abmr->sabr", terms, onehot, precision=lax.Precision.HIGHEST)
    suffix = jnp.dot(hits.reshape(-1, depth_f), upper.T, precision=lax.Precision.HIGHEST).reshape(
        hits.shape
    )
    star_sums = suffix[..., 0]
    farther = prefix(star_sums, "rad", add_up, jnp.zeros_like(star_sums), True)
    grad_fine = to_blocks(dens * step_len * (farther[..., None] + suffix))
    grad_excite = from_blocks(
        jnp.einsum("qpr,qsabr->psabr", mixing_here, grad_fine, precision=lax.Precision.HIGHEST)
        + excite_blocks
    )
    framed_grad = extended(grad_fine, (("ang", 2), ("rad", 4)), 1)
    framed_grad = jnp.pad(framed_grad, ((0, 0), (0, 0), (0, 0), (1, 1), (0, 0)))
    grad_coarse = jnp.zeros((samples, rows_c, cols_c, depth_c), jnp.float32)
    for offset in range(27):
        step_a, step_b, step_r = (offset // 9, offset // 3 % 3, offset % 3)
        piece = framed_grad[
            :,
            :,
            2 - step_a : 2 - step_a + rows_c,
            2 - step_b : 2 - step_b + cols_c,
            2 - step_r : 2 - step_r + depth_c,
        ]
        weights = kernel_wide[offset][:, 2 - step_r : 2 - step_r + depth_c]
        grad_coarse = grad_coarse + jnp.sum(weights[:, None, None, None, :] * piece, axis=0)
    return (grad_excite, grad_coarse)


def solution(mesh):
    in_specs = (
        P(None, "ang", None, "rad"),
        P(None, "ang", None, "rad"),
        P(),
        P(),
        P("ang", None, None),
        P("ang", None),
        P("ang", None, None),
        P("ang", None, None),
    )
    out_specs = (P(None, "ang", None, "rad"), P(None, "ang", None, "rad"))
    return jax.shard_map(
        per_device, mesh=mesh, in_specs=in_specs, out_specs=out_specs, check_vma=False
    )
```

profile of v0, /device:TPU:7, one launch (start us, length us, event | category | flops | bytes accessed | tf_op | source)
XLA Modules:
  0.0 224.0 jit_solution(10753498035399574054)
XLA Ops:
  0.6 10.8 %collective-permute-start.1 = (f32[1,1,32,128]{3,2,1,0:T(8,128)}, f32[1,1,32,128]{3,2,1,0:T(8,128)S(1)}, u32[]{:S(2)}, u32[]{:S(2)}) collective-permute-start(f32[1,1,32,128]{3,2,1,0:T(8,128)} %param.12), channel_id=1, source_target_pairs={{4,0},{8,4},{12,8},{16,12},{20,16},{24,20},{28,24},{32,28},{36,32}... | collective-permute-start | bytes 49160 | tf_op jit(solution)/shard_map/ppermute | solution.py:15
  11.4 1.9 collective-permute-start
  17.4 10.5 %reshape.827 = f32[1,1,2,32,2,128,2]{6,5,4,3,2,1,0:T(8,128)} reshape(f32[1,2,64,256]{3,2,1,0:T(8,128)} %param.13) | data formatting | bytes 262144 | tf_op jit(solution)/shard_map/reshape | solution.py:37
  27.9 5.3 %copy.295 = f32[2,2,2,1,1,32,128]{6,5,2,1,0,4,3:T(8,128)S(1)} copy(f32[2,2,2,1,1,32,128]{2,6,1,5,0,4,3:T(8,128)} %bitcast.278) | data formatting | bytes 262144 | tf_op jit(solution)/shard_map/transpose | solution.py:38
  33.2 8.4 %copy.310 = f32[2,2,2,1,1,32,128]{5,2,1,0,6,4,3:T(2,128)S(1)} copy(f32[2,2,2,1,1,32,128]{2,6,1,5,0,4,3:T(8,128)} %bitcast.279) | data formatting | bytes 262144 | tf_op jit(solution)/shard_map/transpose | solution.py:38
  61.9 3.4 %collective-permute-start.2 = (f32[1,3,32,1]{3,2,1,0:T(8,128)S(1)}, f32[1,3,32,1]{3,2,1,0:T(8,128)S(1)}, u32[]{:S(2)}, u32[]{:S(2)}) collective-permute-start(f32[1,3,32,1]{3,2,1,0:T(8,128)S(1)} %get-tuple-element.372), channel_id=1, source_target_pairs={{0,1},{1,2},{2,3},{4,5},{5,6},{6,7},{8,9},{9,10},{10,11},{12,13},{... | collective-permute-start | bytes 1160 | tf_op jit(solution)/shard_map/ppermute | solution.py:12
  65.3 1.9 collective-permute-start.3
  68.5 2.3 %collective-permute-done.3 = f32[1,3,32,1]{3,2,1,0:T(8,128)S(1)} collective-permute-done((f32[1,3,32,1]{3,2,1,0:T(8,128)S(1)}, f32[1,3,32,1]{3,2,1,0:T(8,128)S(1)}, u32[]{:S(2)}, u32[]{:S(2)}) %collective-permute-start.3) | collective-permute-done | bytes 416 | tf_op jit(solution)/shard_map/ppermute | solution.py:15
  86.5 7.6 %broadcast_multiply_fusion = (f32[8,1,1,32,128]{3,0,4,2,1:T(8,128)S(1)}, f32[8,1,1,32,128]{3,0,4,2,1:T(8,128)S(1)}) fusion(f32[8,8,128]{1,0,2:T(8,128)S(1)} %copy.317, f32[8,32,128]{1,0,2:T(8,128)} %copy.296, f32[32,128]{0,1:T(8,128)} %copy.293, f32[8,128]{0,1:T(8,128)} %copy.292, f32[32,128]{0,1:T(8,128)} %copy.291, f32[8,128]{0,1:T(8,128)} %copy.290, ...), kind=kOutput, calls=%fused_computation.30 | convolution fusion | flops 4947968 | bytes 978944 | tf_op jit(solution)/shard_map/qpr,psabr->qsabr/dot_general | solution.py:76
  94.1 8.0 %copy.299 = f32[2,2,2,1,1,32,128]{2,6,1,5,0,4,3:T(8,128)} copy(f32[2,2,2,1,1,32,128]{5,2,1,0,6,4,3:T(2,128)S(1)} %bitcast.296) | data formatting | bytes 262144 | tf_op jit(solution)/shard_map/exp | solution.py:79
  102.1 6.9 %exp.22 = f32[128,256]{1,0:T(8,128)S(1)} reshape(f32[1,1,2,32,2,128,2]{6,5,4,3,2,1,0:T(8,128)} %bitcast.280) | data formatting | bytes 262144 | tf_op jit(solution)/shard_map/exp | solution.py:79
  109.4 4.1 %all-gather = f32[4,2,64,1]{2,1,3,0:T(2,128)S(1)} all-gather(f32[1,2,64,1]{2,1,3,0:T(2,128)S(1)} %copy.300), channel_id=2, replica_groups=mesh['ang'=64,'rad'=4] {'rad'}, dimensions={0}, use_global_device_ids=true | all-gather | bytes 2560 | tf_op jit(solution)/shard_map/all_gather | solution.py:22
  113.7 20.6 %gather_fusion = f32[2048]{0:T(1024)S(1)} fusion(f32[2,64,256]{2,1,0:T(8,128)S(1)} %multiply_bitcast_fusion, s32[2048]{0:T(1024)S(1)} %reshape.844), kind=kCustom, calls=%fused_computation | custom fusion | bytes 40960 | tf_op jit(solution)/shard_map/jit(take_along_axis)/gather | solution.py:92
  136.1 9.7 %reshape.832 = f32[1,1,2,32,2,128,2]{6,5,4,3,2,1,0:T(8,128)} reshape(f32[128,256]{1,0:T(8,128)S(1)} %fusion.10) | data formatting | bytes 262144 | tf_op jit(solution)/shard_map/reshape | solution.py:97
  145.9 5.2 %all-gather.1 = f32[4,2,64,1]{2,1,3,0:T(2,128)S(1)} all-gather(f32[1,2,64,1]{2,1,3,0:T(2,128)S(1)} %copy.318), channel_id=3, replica_groups=mesh['ang'=64,'rad'=4] {'rad'}, dimensions={0}, use_global_device_ids=true | all-gather | bytes 2560 | tf_op jit(solution)/shard_map/all_gather | solution.py:22
  151.4 7.9 %copy.297 = f32[2,2,2,1,1,32,128]{2,6,1,5,0,4,3:T(8,128)} copy(f32[2,2,2,1,1,32,128]{5,2,1,0,6,4,3:T(2,128)S(1)} %bitcast.295) | data formatting | bytes 262144 | tf_op jit(solution)/shard_map/mul | solution.py:102
  159.3 10.0 %multiply_reduce_fusion = (f32[32,128]{1,0:T(8,128)S(1)}, f32[2,2,2,1,1,32,128]{2,6,1,5,0,4,3:T(8,128)}) fusion(f32[2,2,2,128]{2,3,1,0:T(8,128)S(1)} %copy.313, f32[1,1,2,32,2,128,2]{6,5,4,3,2,1,0:T(8,128)} %reshape.832, f32[2,32,2]{2,1,0:T(8,128)S(1)} %add.739, f32[2,2,2,1,1,32,128]{2,6,1,5,0,4,3:T(8,128)} %copy.297), kind=kLoop, calls=%fused_computation.5 | loop fusion | flops 126976 | bytes 414208 | tf_op jit(solution)/shard_map/reduce_sum | solution.py:120
  169.4 5.3 %copy.307 = f32[2,2,2,1,1,32,128]{6,5,2,1,0,4,3:T(8,128)S(1)} copy(f32[2,2,2,1,1,32,128]{2,6,1,5,0,4,3:T(8,128)} %get-tuple-element.282) | data formatting | bytes 262144 | tf_op jit(solution)/shard_map/transpose | solution.py:38
  174.7 8.8 %collective-permute-start.5 = (f32[8,1,1,32,128]{4,3,0,2,1:T(8,128)S(1)}, f32[8,1,1,32,128]{4,3,0,2,1:T(8,128)S(1)}, u32[]{:S(2)}, u32[]{:S(2)}) collective-permute-start(f32[8,1,1,32,128]{4,3,0,2,1:T(8,128)S(1)} %bitcast.282), channel_id=1, source_target_pairs={{4,0},{8,4},{12,8},{16,12},{20,16},{24,20},{28,24},{32,28},{36,32}... | collective-permute-start | bytes 393224 | tf_op jit(solution)/shard_map/ppermute | solution.py:15
  183.5 1.9 collective-permute-start.4
  193.5 2.6 %collective-permute-done.4 = f32[8,1,1,32,128]{4,3,0,2,1:T(8,128)S(1)} collective-permute-done((f32[8,1,1,32,128]{4,3,0,2,1:T(8,128)S(1)}, f32[8,1,1,32,128]{4,3,0,2,1:T(8,128)S(1)}, u32[]{:S(2)}, u32[]{:S(2)}) %collective-permute-start.4) | collective-permute-done | bytes 131104 | tf_op jit(solution)/shard_map/ppermute | solution.py:12
  197.2 5.9 %collective-permute-start.6 = (f32[8,1,3,32,1]{4,3,0,2,1:T(8,128)}, f32[8,1,3,32,1]{4,3,0,2,1:T(8,128)S(1)}, u32[]{:S(2)}, u32[]{:S(2)}) collective-permute-start(f32[8,1,3,32,1]{4,3,0,2,1:T(8,128)} %get-tuple-element.289), channel_id=1, source_target_pairs={{0,1},{1,2},{2,3},{4,5},{5,6},{6,7},{8,9},{9,10},{10,11},{12,13},{... | collective-permute-start | bytes 9224 | tf_op jit(solution)/shard_map/ppermute | solution.py:12
  206.3 8.0 %copy.311 = f32[2,2,2,1,1,32,128]{2,6,1,5,0,4,3:T(8,128)} copy(f32[2,2,2,1,1,32,128]{5,2,1,0,6,4,3:T(2,128)S(1)} %bitcast.290) | data formatting | bytes 262144 | tf_op jit(solution)/shard_map/reshape | solution.py:46
  214.3 7.5 %reshape.836 = f32[1,2,64,256]{3,2,1,0:T(8,128)} reshape(f32[1,1,2,32,2,128,2]{6,5,4,3,2,1,0:T(8,128)} %bitcast.281) | data formatting | bytes 262144 | tf_op jit(solution)/shard_map/reshape | solution.py:48
  (208 shorter events, 58.3 us)
Async XLA Ops:
  0.6 61.2 %collective-permute-start.1 = (f32[1,1,32,128]{3,2,1,0:T(8,128)}, f32[1,1,32,128]{3,2,1,0:T(8,128)S(1)}, u32[]{:S(2)}, u32[]{:S(2)}) collective-permute-start(f32[1,1,32,128]{3,2,1,0:T(8,128)} %param.12), channel_id=1, source_target_pairs={{4,0},{8,4},{12,8},{16,12},{20,16},{24,20},{28,24},{32,28},{36,32}... | collective-permute-start | bytes 49160 | tf_op jit(solution)/shard_map/ppermute | solution.py:15
  11.4 50.3 %collective-permute-start = (f32[1,1,32,128]{3,2,1,0:T(8,128)}, f32[1,1,32,128]{3,2,1,0:T(8,128)S(1)}, u32[]{:S(2)}, u32[]{:S(2)}) collective-permute-start(f32[1,1,32,128]{3,2,1,0:T(8,128)} %param.12), channel_id=1, source_target_pairs={{0,4},{4,8},{8,12},{12,16},{16,20},{20,24},{24,28},{28,32},{32,36}... | collective-permute-start | bytes 49160 | tf_op jit(solution)/shard_map/ppermute | solution.py:12
  61.9 6.6 %collective-permute-start.2 = (f32[1,3,32,1]{3,2,1,0:T(8,128)S(1)}, f32[1,3,32,1]{3,2,1,0:T(8,128)S(1)}, u32[]{:S(2)}, u32[]{:S(2)}) collective-permute-start(f32[1,3,32,1]{3,2,1,0:T(8,128)S(1)} %get-tuple-element.372), channel_id=1, source_target_pairs={{0,1},{1,2},{2,3},{4,5},{5,6},{6,7},{8,9},{9,10},{10,11},{12,13},{... | collective-permute-start | bytes 1160 | tf_op jit(solution)/shard_map/ppermute | solution.py:12
  65.3 5.4 %collective-permute-start.3 = (f32[1,3,32,1]{3,2,1,0:T(8,128)S(1)}, f32[1,3,32,1]{3,2,1,0:T(8,128)S(1)}, u32[]{:S(2)}, u32[]{:S(2)}) collective-permute-start(f32[1,3,32,1]{3,2,1,0:T(8,128)S(1)} %get-tuple-element.373), channel_id=1, source_target_pairs={{1,0},{2,1},{3,2},{5,4},{6,5},{7,6},{9,8},{10,9},{11,10},{13,12},{... | collective-permute-start | bytes 1160 | tf_op jit(solution)/shard_map/ppermute | solution.py:15
  169.2 21.3 %copy-start.17 = (f32[8,130]{1,0:T(8,128)S(1)}, f32[8,130]{1,0:T(8,128)}, u32[]{:S(2)}) copy-start(f32[8,130]{1,0:T(8,128)} %get-tuple-element.291) | copy-start | bytes 12484
  169.2 21.9 %copy-start.16 = (f32[8,130]{1,0:T(8,128)S(1)}, f32[8,130]{1,0:T(8,128)}, u32[]{:S(2)}) copy-start(f32[8,130]{1,0:T(8,128)} %get-tuple-element.292) | copy-start | bytes 12484
  169.2 22.6 %copy-start.15 = (f32[8,130]{1,0:T(8,128)S(1)}, f32[8,130]{1,0:T(8,128)}, u32[]{:S(2)}) copy-start(f32[8,130]{1,0:T(8,128)} %get-tuple-element.293) | copy-start | bytes 12484
  169.2 23.3 %copy-start.14 = (f32[8,130]{1,0:T(8,128)S(1)}, f32[8,130]{1,0:T(8,128)}, u32[]{:S(2)}) copy-start(f32[8,130]{1,0:T(8,128)} %get-tuple-element.294) | copy-start | bytes 12484
  169.3 23.3 %copy-start.13 = (f32[8,130]{1,0:T(8,128)S(1)}, f32[8,130]{1,0:T(8,128)}, u32[]{:S(2)}) copy-start(f32[8,130]{1,0:T(8,128)} %get-tuple-element.295) | copy-start | bytes 12484
  169.3 23.3 %copy-start.12 = (f32[8,130]{1,0:T(8,128)S(1)}, f32[8,130]{1,0:T(8,128)}, u32[]{:S(2)}) copy-start(f32[8,130]{1,0:T(8,128)} %get-tuple-element.296) | copy-start | bytes 12484
  169.3 23.4 %copy-start.11 = (f32[8,130]{1,0:T(8,128)S(1)}, f32[8,130]{1,0:T(8,128)}, u32[]{:S(2)}) copy-start(f32[8,130]{1,0:T(8,128)} %get-tuple-element.297) | copy-start | bytes 12484
  169.3 23.4 %copy-start.10 = (f32[8,130]{1,0:T(8,128)S(1)}, f32[8,130]{1,0:T(8,128)}, u32[]{:S(2)}) copy-start(f32[8,130]{1,0:T(8,128)} %get-tuple-element.298) | copy-start | bytes 12484
  169.3 23.4 %copy-start.9 = (f32[8,130]{1,0:T(8,128)S(1)}, f32[8,130]{1,0:T(8,128)}, u32[]{:S(2)}) copy-start(f32[8,130]{1,0:T(8,128)} %get-tuple-element.299) | copy-start | bytes 12484
  169.3 23.5 %copy-start.8 = (f32[8,130]{1,0:T(8,128)S(1)}, f32[8,130]{1,0:T(8,128)}, u32[]{:S(2)}) copy-start(f32[8,130]{1,0:T(8,128)} %get-tuple-element.300) | copy-start | bytes 12484
  169.3 23.5 %copy-start.7 = (f32[8,130]{1,0:T(8,128)S(1)}, f32[8,130]{1,0:T(8,128)}, u32[]{:S(2)}) copy-start(f32[8,130]{1,0:T(8,128)} %get-tuple-element.301) | copy-start | bytes 12484
  169.3 23.6 %copy-start.6 = (f32[8,130]{1,0:T(8,128)S(1)}, f32[8,130]{1,0:T(8,128)}, u32[]{:S(2)}) copy-start(f32[8,130]{1,0:T(8,128)} %get-tuple-element.302) | copy-start | bytes 12484
  169.3 23.6 %copy-start.5 = (f32[8,130]{1,0:T(8,128)S(1)}, f32[8,130]{1,0:T(8,128)}, u32[]{:S(2)}) copy-start(f32[8,130]{1,0:T(8,128)} %get-tuple-element.303) | copy-start | bytes 12484
  169.3 23.6 %copy-start.4 = (f32[8,130]{1,0:T(8,128)S(1)}, f32[8,130]{1,0:T(8,128)}, u32[]{:S(2)}) copy-start(f32[8,130]{1,0:T(8,128)} %get-tuple-element.305) | copy-start | bytes 12484
  169.4 23.7 %copy-start.3 = (f32[8,130]{1,0:T(8,128)S(1)}, f32[8,130]{1,0:T(8,128)}, u32[]{:S(2)}) copy-start(f32[8,130]{1,0:T(8,128)} %get-tuple-element.306) | copy-start | bytes 12484
  169.4 23.7 %copy-start.2 = (f32[8,130]{1,0:T(8,128)S(1)}, f32[8,130]{1,0:T(8,128)}, u32[]{:S(2)}) copy-start(f32[8,130]{1,0:T(8,128)} %get-tuple-element.307) | copy-start | bytes 12484
  174.7 18.7 %collective-permute-start.5 = (f32[8,1,1,32,128]{4,3,0,2,1:T(8,128)S(1)}, f32[8,1,1,32,128]{4,3,0,2,1:T(8,128)S(1)}, u32[]{:S(2)}, u32[]{:S(2)}) collective-permute-start(f32[8,1,1,32,128]{4,3,0,2,1:T(8,128)S(1)} %bitcast.282), channel_id=1, source_target_pairs={{4,0},{8,4},{12,8},{16,12},{20,16},{24,20},{28,24},{32,28},{36,32}... | collective-permute-start | bytes 393224 | tf_op jit(solution)/shard_map/ppermute | solution.py:15
  183.5 12.6 %collective-permute-start.4 = (f32[8,1,1,32,128]{4,3,0,2,1:T(8,128)S(1)}, f32[8,1,1,32,128]{4,3,0,2,1:T(8,128)S(1)}, u32[]{:S(2)}, u32[]{:S(2)}) collective-permute-start(f32[8,1,1,32,128]{4,3,0,2,1:T(8,128)S(1)} %bitcast.283), channel_id=1, source_target_pairs={{0,4},{4,8},{8,12},{12,16},{16,20},{20,24},{24,28},{28,32},{32,36}... | collective-permute-start | bytes 393224 | tf_op jit(solution)/shard_map/ppermute | solution.py:12
  197.2 24.6 %collective-permute-start.6 = (f32[8,1,3,32,1]{4,3,0,2,1:T(8,128)}, f32[8,1,3,32,1]{4,3,0,2,1:T(8,128)S(1)}, u32[]{:S(2)}, u32[]{:S(2)}) collective-permute-start(f32[8,1,3,32,1]{4,3,0,2,1:T(8,128)} %get-tuple-element.289), channel_id=1, source_target_pairs={{0,1},{1,2},{2,3},{4,5},{5,6},{6,7},{8,9},{9,10},{10,11},{12,13},{... | collective-permute-start | bytes 9224 | tf_op jit(solution)/shard_map/ppermute | solution.py:12
  203.1 18.7 %collective-permute-start.7 = (f32[8,1,3,32,1]{4,3,0,2,1:T(8,128)}, f32[8,1,3,32,1]{4,3,0,2,1:T(8,128)S(1)}, u32[]{:S(2)}, u32[]{:S(2)}) collective-permute-start(f32[8,1,3,32,1]{4,3,0,2,1:T(8,128)} %get-tuple-element.290), channel_id=1, source_target_pairs={{1,0},{2,1},{3,2},{5,4},{6,5},{7,6},{9,8},{10,9},{11,10},{13,12},{... | collective-permute-start | bytes 9224 | tf_op jit(solution)/shard_map/ppermute | solution.py:15
  (16 other events, 233.7 us)
where the time goes:
time: 225 us; the launch traced here: 224 us
  local copies, waits for them, and re-layouts  147 us (65%)
  starting transfers between devices  36.6 us (16%)
  other arithmetic  13.9 us (6%)
  matrix products  10.5 us (5%)
  blocking collectives  9.33 us (4%)
  waiting for transfers between devices  4.93 us (2%)
    mul x57, local copies, waits for them, and re-layouts, per_device(): fine = fine + kernel_here[offset][:, None, None, None, :] * window[None]  35.3 us
    ppermute x4, starting transfers between devices, extended(): lax.ppermute(lax.slice_in_dim(block, 0, width, axis=dim), axis, backward)  23.4 us
    gather x3, local copies, waits for them, and re-layouts, per_device(): pred = jnp.take_along_axis(extinction, clipped[None], axis=3)  20.7 us
    transpose x3, local copies, waits for them, and re-layouts, to_blocks(): return field.reshape(samples, na // 2, 2, nb // 2, 2, nr // 2, 2).transpo...  19 us
    exp x2, local copies, waits for them, and re-layouts, per_device(): dens = jnp.exp(from_blocks(fine))  14.9 us
    ppermute x4, starting transfers between devices, extended(): lax.ppermute(lax.slice_in_dim(block, block.shape[dim] - width, None, axis...  13.2 us
    reduce_sum x5, other arithmetic, per_device(): jnp.sum(weights[:, None, None, None, :] * piece, axis=0)  11 us
    reshape x1, local copies, waits for them, and re-layouts, to_blocks(): field.reshape(samples, na // 2, 2, nb // 2, 2, nr // 2, 2)  10.5 us
  transfers between devices with their start and end apart: 8, of which 2 were waited for; matrix products, arithmetic and copies ran while one was open for 33% of the time, Pallas kernels for 0%

commit v1 on v0

v1 whole, which is shorter than its diff:
```python
import jax
import jax.numpy as jnp
from jax import lax
from jax.experimental import pallas as pl
from jax.experimental.pallas import tpu as pltpu
from jax.sharding import PartitionSpec as P

F32 = jnp.float32
HI = lax.Precision.HIGHEST
VMEM = pl.BlockSpec(memory_space=pltpu.VMEM)


def lanes(shape):
    return lax.broadcasted_iota(jnp.int32, shape, 1)


def rows(shape):
    return lax.broadcasted_iota(jnp.int32, shape, 0)


def along(x, k, axis):
    if k == 0:
        return x
    n = x.shape[axis]
    at = lax.broadcasted_iota(jnp.int32, x.shape, axis)
    inside = at < n - k if k > 0 else at >= -k
    return jnp.where(inside, pltpu.roll(x, (-k) % n, axis), 0.0)


def pick(x, index):
    return jnp.take_along_axis(x, index, axis=1, mode="promise_in_bounds")


def wide(x):
    return jnp.concatenate([x, jnp.zeros((x.shape[0], 128 - x.shape[1]), x.dtype)], axis=1)


def split_pixels(ref, j):
    half = pl.ds(j, 32, stride=2)
    low, high = ref[0, half, :], ref[1, half, :]
    lane = lanes((32, 128))
    out = []
    for k in range(2):
        index = (2 * lane + k) & 127
        out.append(jnp.where(lane < 64, pick(low, index), pick(high, index)))
    return out


def taps(acc, row, weights, first, shard):
    here = pl.ds(pl.multiple_of(shard * 128, 128), 128)
    for w in range(3):
        moved = along(row, w - 1, 1)
        for v in range(3):
            window = along(moved, v - 1, 0)
            t = first + 3 * v + w
            block = weights[t, :, here]
            for q in range(8):
                acc[q] = acc[q] + block[q : q + 1, :] * window


def prepare(coarse, excite, kernels, mixing, star_bin, star_count, star_obs, star_isig,
            base, fields, rel_out, w_out, o_out, sums, count_t, halves, slots, bins):
    shard = lax.axis_index("rad")
    here = pl.ds(pl.multiple_of(shard * 128, 128), 128)
    parts = []
    for i in range(2):
        halves[i, 0] = excite[i, :, 0:128]
        halves[i, 1] = excite[i, :, 128:256]
        bins[i] = wide(star_bin[i])
        slots[i, 0] = wide(star_isig[i])
        slots[i, 1] = wide(star_obs[i])
    for i in range(2):
        for j in range(2):
            parts += split_pixels(halves.at[i], j)
    for p in range(8):
        fields[p] = parts[p]
    acc = []
    for q in range(8):
        block = mixing[q, :, here]
        total = block[0:1, :] * parts[0]
        for p in range(1, 8):
            total = total + block[p : p + 1, :] * parts[p]
        acc.append(total)
    taps(acc, coarse[...], kernels, 9, shard)
    for q in range(8):
        base[q] = acc[q]
    counts = jnp.concatenate([star_count[...].astype(F32), jnp.zeros((2, 64), F32)], axis=1)
    counts = jnp.concatenate([counts, jnp.zeros((126, 128), F32)], axis=0)
    count_t[...] = counts.T
    lane = lanes((32, 128))
    table = jnp.zeros((32, 128), F32)
    for i in range(2):
        for j in range(2):
            p = 2 * i + j
            half = pl.ds(j, 32, stride=2)
            count = count_t[half, :][:, i : i + 1]
            rel = bins[i, half, :] - 256 * shard
            live = (lane < 16) & (lane.astype(F32) < count) & (rel >= 0) & (rel < 256)
            isig = slots[i, 0, half, :]
            w = jnp.where(live, isig * isig, 0.0)
            o = w * slots[i, 1, half, :]
            rel = jnp.where(live, rel, -1)
            rel_out[p] = rel
            w_out[p] = w
            o_out[p] = o
            for k in range(2):
                for group, least in ((40, k), (48, 254 + k)):
                    deep = rel >= least
                    total = jnp.sum(jnp.where(deep, w, 0.0), axis=1, keepdims=True)
                    table = jnp.where(lane == group + 2 * p + k, total, table)
                    total = jnp.sum(jnp.where(deep, o, 0.0), axis=1, keepdims=True)
                    table = jnp.where(lane == group + 16 + 2 * p + k, total, table)
    sums[...] = table


def forward(coarse, low, high, base, kernels, rel_in, w_in, o_in, sums, dens, local, table):
    shard = lax.axis_index("rad")
    step = 1.0 / 1024
    acc = [base[q] for q in range(8)]
    taps(acc, low[...], kernels, 0, shard)
    taps(acc, high[...], kernels, 18, shard)
    lane = lanes((32, 128))
    out = sums[...]
    for q in range(8):
        out = jnp.where(lane == q, acc[q][:, 0:1], out)
        out = jnp.where(lane == 8 + q, acc[q][:, 127:128], out)
    for u, row in enumerate((low, coarse, high)):
        value = row[...]
        out = jnp.where(lane == 32 + u, value[:, 0:1], out)
        out = jnp.where(lane == 35 + u, value[:, 127:128], out)
    inner = (lane > 0) & (lane < 127)
    density = []
    for q in range(8):
        d = jnp.exp(acc[q])
        dens[q] = d
        density.append(jnp.where(inner, d, 0.0))
    pairs = jnp.concatenate([density[2 * p] + density[2 * p + 1] for p in range(4)], axis=0)
    strict = (rows((128, 128)) < lanes((128, 128))).astype(F32)
    before = jnp.dot(pairs, strict, precision=HI, preferred_element_type=F32)
    for p in range(4):
        first = before[32 * p : 32 * p + 32] + density[2 * p]
        second = first + density[2 * p + 1]
        rel = jnp.maximum(rel_in[p], 0)
        index = rel >> 1
        at = jnp.where((rel & 1) == 1, pick(second, index), pick(first, index))
        local[p] = at
        total = second[:, 127:128]
        share = jnp.sum(step * at * w_in[p] - o_in[p], axis=1, keepdims=True)
        for k in range(2):
            out = jnp.where(lane == 16 + 2 * p + k, total, out)
            out = jnp.where(lane == 24 + 2 * p + k, share, out)
    table[...] = out


def swap(x):
    even = (rows(x.shape) & 1) == 0
    return jnp.where(even, pltpu.roll(x, x.shape[0] - 1, 0), pltpu.roll(x, 1, 0))


def backward(table, dens, local, kernels, rel_in, w_in, o_in, grad, to_low, own, to_high):
    shard = lax.axis_index("rad")
    step = 1.0 / 1024
    even = (rows((8, 128)) & 1) == 0
    groups = []
    for s in range(4):
        full = jnp.concatenate([table[s], jnp.zeros((96, 128), F32)], axis=0).T
        groups.append([full[8 * g : 8 * g + 8] for g in range(9)])
    edges = []
    for s in range(4):
        e = groups[s][4]
        edges.append([along(e, v - 1, 1) for v in range(3)])
    d_low, d_high, totals, shares, whole = [], [], [], [], []
    for s in range(4):
        f_low, f_high, t, c, _, w_low, w_high, o_low, o_high = groups[s]
        for u in range(3):
            for v in range(3):
                if s > 0:
                    weight = kernels[9 * u + 3 * v, :, 128 * s : 128 * s + 128][:, 0:1]
                    f_low = f_low + weight * edges[s - 1][v][3 + u : 4 + u, :]
                if s < 3:
                    weight = kernels[9 * u + 3 * v + 2, :, 128 * s : 128 * s + 128][:, 127:128]
                    f_high = f_high + weight * edges[s + 1][v][u : u + 1, :]
        a, b = jnp.exp(f_low), jnp.exp(f_high)
        d_low.append(a)
        d_high.append(b)
        both = a + b
        totals.append(t + both + swap(both))
        both = a * w_low + b * w_high
        shares.append(c + step * (both + swap(both)))
        whole.append(jnp.where(even, w_low, swap(w_low)))
    zero = jnp.zeros((8, 128), F32)
    nearer = [zero]
    for s in range(3):
        nearer.append(nearer[s] + totals[s])
    nearer = [step * x for x in nearer]
    sums = [shares[s] + nearer[s] * whole[s] for s in range(4)]
    farther = [zero]
    for s in (3, 2, 1):
        farther.insert(0, farther[0] + sums[s])

    def low_edge(s):
        _, _, _, _, _, w, _, o, _ = groups[s]
        first = (nearer[s] + step * swap(d_low[s])) * (swap(w) - w) - (swap(o) - o)
        suffix = sums[s] - jnp.where(even, 0.0, first)
        return d_low[s] * step * (farther[s] + suffix)

    def high_edge(s):
        _, _, _, _, _, _, w, _, o = groups[s]
        last = step * swap(d_high[s]) * (w - swap(w))
        suffix = (nearer[s] + step * totals[s]) * w - o - jnp.where(even, last, 0.0)
        return d_high[s] * step * (farther[s] + suffix)

    def mine(values):
        out = values[0]
        for s in range(1, 4):
            out = jnp.where(shard == s, values[s], out)
        return out

    columns = [mine(d_low), mine(d_high), mine(nearer), mine(farther),
               mine([zero, high_edge(0), high_edge(1), high_edge(2)]),
               mine([low_edge(1), low_edge(2), low_edge(3), zero])]
    columns = jnp.concatenate(columns + [jnp.zeros((80, 128), F32)], axis=0).T[0:32]

    def column(group, q):
        return columns[:, 8 * group + q : 8 * group + q + 1]

    lane = lanes((32, 128))
    plus, minus, here = [], [], []
    for p in range(4):
        a0, a1 = column(0, 2 * p), column(0, 2 * p + 1)
        b0, b1 = column(1, 2 * p), column(1, 2 * p + 1)
        rel = rel_in[p]
        reach = local[p] + jnp.where(rel >= 0, a0, 0.0) + jnp.where(rel >= 1, a1, 0.0)
        reach = reach + jnp.where(rel >= 254, b0, 0.0) + jnp.where(rel >= 255, b1, 0.0)
        term = w_in[p] * (column(2, 2 * p) + step * reach) - o_in[p]
        s0 = jnp.broadcast_to(column(3, 2 * p), (32, 128))
        s1 = s0
        for m in range(16):
            at = rel[:, m : m + 1]
            value = term[:, m : m + 1]
            s0 = s0 + jnp.where(at >= 2 * lane, value, 0.0)
            s1 = s1 + jnp.where(at > 2 * lane, value, 0.0)
        for k, s in ((0, s0), (1, s1)):
            q = 2 * p + k
            d = jnp.where(lane == 0, column(0, q), dens[q])
            d = jnp.where(lane == 127, column(1, q), d)
            g = d * step * s
            grad[q] = g
            here.append(g)
            plus.append(jnp.where(lane == 127, column(4, q), g))
            minus.append(jnp.where(lane == 0, column(5, q), g))
    at = pl.ds(pl.multiple_of(shard * 128, 128), 128)
    prev = pl.ds(pl.multiple_of(jnp.maximum(shard - 1, 0) * 128, 128), 128)
    after = pl.ds(pl.multiple_of(jnp.minimum(shard + 1, 3) * 128, 128), 128)
    lane8 = lanes((8, 128))
    for u, out in enumerate((to_low, own, to_high)):
        total = None
        for w, field in enumerate((minus, here, plus)):
            part = None
            for v in range(3):
                t = 9 * u + 3 * v + w
                block = kernels[t, :, at]
                if w == 0:
                    block = jnp.where(lane8 == 0, kernels[t, :, after], block)
                if w == 2:
                    block = jnp.where(lane8 == 127, kernels[t, :, prev], block)
                piece = block[0:1, :] * field[0]
                for q in range(1, 8):
                    piece = piece + block[q : q + 1, :] * field[q]
                piece = along(piece, 1 - v, 0)
                part = piece if part is None else part + piece
            if w != 1:
                part = pltpu.roll(part, (w - 1) % 128, 1)
            total = part if total is None else total + part
        out[...] = total


def finish(grad, fields, mixing, out, halves):
    shard = lax.axis_index("rad")
    at = pl.ds(pl.multiple_of(shard * 128, 128), 128)
    lane = lanes((32, 128))
    acc = [fields[p] for p in range(8)]
    for q in range(8):
        block = mixing[q, :, at]
        g = grad[q]
        for p in range(8):
            acc[p] = acc[p] + block[p : p + 1, :] * g
    for i in range(2):
        for j in range(2):
            pair = acc[4 * i + 2 * j : 4 * i + 2 * j + 2]
            half = pl.ds(j, 32, stride=2)
            for side in range(2):
                index = (lane >> 1) + 64 * side
                value = jnp.where((lane & 1) == 0, pick(pair[0], index), pick(pair[1], index))
                halves[side, half, :] = value
        for side in range(2):
            out[i, :, 128 * side : 128 * side + 128] = halves[side]


def call(body, name, ins, outs, flops, scratch=()):
    shapes = tuple(jax.ShapeDtypeStruct(s, d) for s, d in outs)
    size = sum(x.size * 4 for x in ins) + sum(x.size * 4 for x in shapes)
    return pl.pallas_call(
        body,
        name=name,
        out_shape=shapes,
        in_specs=[VMEM] * len(ins),
        out_specs=tuple([VMEM] * len(shapes)),
        scratch_shapes=list(scratch),
        cost_estimate=pl.CostEstimate(flops=flops, bytes_accessed=size, transcendentals=0),
        compiler_params=pltpu.CompilerParams(vmem_limit_bytes=16 << 20),
    )(*ins)


def per_device(coarse, excite, kernels, mixing, star_bin, star_count, star_obs, star_isig):
    count = lax.axis_size("ang")
    up = [(i, i + 1) for i in range(count - 1)]
    down = [(i + 1, i) for i in range(count - 1)]
    own = coarse[0, 0]
    low = lax.ppermute(own, "ang", up)
    high = lax.ppermute(own, "ang", down)
    block = ((8, 32, 128), F32)
    stars = ((4, 32, 128), F32)
    row = ((32, 128), F32)
    base, fields, rel, w, o, sums = call(
        prepare, "prepare",
        (own, excite[0], kernels, mixing, star_bin, star_count, star_obs, star_isig),
        (block, block, ((4, 32, 128), jnp.int32), stars, stars, row), 4_000_000,
        [pltpu.VMEM((128, 128), F32), pltpu.VMEM((2, 2, 64, 128), F32),
         pltpu.VMEM((2, 2, 64, 128), F32), pltpu.VMEM((2, 64, 128), jnp.int32)],
    )
    dens, local, table = call(
        forward, "forward", (own, low, high, base, kernels, rel, w, o, sums),
        (block, stars, row), 6_000_000,
    )
    tables = lax.all_gather(table, "rad")
    grad, to_low, here, to_high = call(
        backward, "backward", (tables, dens, local, kernels, rel, w, o),
        (block, row, row, row), 8_000_000,
    )
    from_high = lax.ppermute(to_low, "ang", down)
    from_low = lax.ppermute(to_high, "ang", up)
    (grad_excite,) = call(
        finish, "finish", (grad, fields, mixing), (((2, 64, 256), F32),), 4_000_000,
        [pltpu.VMEM((2, 64, 128), F32)],
    )
    grad_coarse = here + from_high + from_low
    return grad_excite[None], grad_coarse[None, None]


def solution(mesh):
    in_specs = (
        P(None, "ang", None, "rad"),
        P(None, "ang", None, "rad"),
        P(),
        P(),
        P("ang", None, None),
        P("ang", None),
        P("ang", None, None),
        P("ang", None, None),
    )
    out_specs = (P(None, "ang", None, "rad"), P(None, "ang", None, "rad"))
    return jax.shard_map(
        per_device, mesh=mesh, in_specs=in_specs, out_specs=out_specs, check_vma=False
    )
```

time: 225 us -> 47.8 us (0.21)
  the two profiles are of different devices: /device:TPU:7 before, /device:TPU:6 now
where the time goes in v1:
time: 47.8 us; the launch traced here: 47.3 us
  starting transfers between devices  20.2 us (42%)
  waiting for transfers between devices  12 us (25%)
  blocking collectives  5.24 us (11%)
  local copies, waits for them, and re-layouts  4.3 us (9%)
  Pallas kernels  4.23 us (9%)
  between operations  0.72 us (2%)
  other arithmetic  0.61 us (1%)
    ppermute x1, starting transfers between devices, per_device(): high = lax.ppermute(own, 'ang', down)  11.1 us
    ppermute x1, waiting for transfers between devices, per_device(): from_low = lax.ppermute(to_high, 'ang', up)  7.95 us
    ppermute x1, starting transfers between devices, per_device(): from_high = lax.ppermute(to_low, 'ang', down)  5.33 us
    all_gather x1, blocking collectives, per_device(): tables = lax.all_gather(table, 'rad')  5.24 us
    unnamed x17, local copies, waits for them, and re-layouts  4.3 us
    pallas_call x4, Pallas kernels, call(): pl.pallas_call(body, name=name, out_shape=shapes, in_specs=[VMEM] * len(i...  4.23 us
    ppermute x1, waiting for transfers between devices, per_device(): low = lax.ppermute(own, 'ang', up)  4.02 us
    ppermute x1, starting transfers between devices, per_device(): low = lax.ppermute(own, 'ang', up)  1.92 us
  transfers between devices with their start and end apart: 4, of which 2 were waited for; matrix products, arithmetic and copies ran while one was open for 4% of the time, Pallas kernels for 3%

profile of v1, /device:TPU:6, one launch (start us, length us, event | category | flops | bytes accessed | tf_op | source)
XLA Modules:
  0.0 47.3 jit_solution(100211161115642045)
XLA Ops:
  0.6 0.0 copy-start.2
  0.6 11.1 %collective-permute-start.1 = (f32[32,128]{1,0:T(8,128)}, f32[32,128]{1,0:T(8,128)S(1)}, u32[]{:S(2)}, u32[]{:S(2)}) collective-permute-start(f32[32,128]{1,0:T(8,128)} %bitcast.8), channel_id=1, source_target_pairs={{4,0},{8,4},{12,8},{16,12},{20,16},{24,20},{28,24},{32,28},{36,32}... | collective-permute-start | bytes 49160 | tf_op jit(solution)/shard_map/ppermute | solution.py:321
  11.7 1.9 %collective-permute-start = (f32[32,128]{1,0:T(8,128)}, f32[32,128]{1,0:T(8,128)S(1)}, u32[]{:S(2)}, u32[]{:S(2)}) collective-permute-start(f32[32,128]{1,0:T(8,128)} %bitcast.9), channel_id=1, source_target_pairs={{0,4},{4,8},{8,12},{12,16},{16,20},{20,24},{24,28},{28,32},{32,36}... | collective-permute-start | bytes 49160 | tf_op jit(solution)/shard_map/ppermute | solution.py:320
  13.6 0.8 %copy.10.star_bin = s32[2,64,16]{2,1,0:T(8,128)S(1)} copy(s32[2,64,16]{1,2,0:T(8,128)} %param.12) | data formatting | bytes 16384 | tf_op args[4]
  14.4 0.8 %copy.11.star_obs = f32[2,64,16]{2,1,0:T(8,128)S(1)} copy(f32[2,64,16]{1,2,0:T(8,128)} %param.14) | data formatting | bytes 16384 | tf_op args[6]
  15.3 0.0 copy-done.6
  15.3 0.0 copy-start.4
  15.3 0.1 copy.12.star_isig
  15.4 0.6 %copy-done.4 = f32[1,1,32,128]{3,2,1,0:T(8,128)S(1)} copy-done((f32[1,1,32,128]{3,2,1,0:T(8,128)S(1)}, f32[1,1,32,128]{3,2,1,0:T(8,128)}, u32[]{:S(2)}) %copy-start.4) | copy-done | bytes 16408
  16.0 0.1 copy-done.5
  16.0 1.0 %copy-done = f32[27,8,512]{2,1,0:T(8,128)S(1)} copy-done((f32[27,8,512]{2,1,0:T(8,128)S(1)}, f32[27,8,512]{2,1,0:T(8,128)}, u32[]{:S(2)}) %copy-start) | copy-done | bytes 442392
  17.0 0.9 %copy-done.3 = f32[1,2,64,256]{3,2,1,0:T(8,128)S(1)} copy-done((f32[1,2,64,256]{3,2,1,0:T(8,128)S(1)}, f32[1,2,64,256]{3,2,1,0:T(8,128)}, u32[]{:S(2)}) %copy-start.3) | copy-done | bytes 131096
  18.0 0.7 %prepare.1 = (f32[8,32,128]{2,1,0:T(8,128)S(1)}, f32[8,32,128]{2,1,0:T(8,128)S(1)}, s32[4,32,128]{2,1,0:T(8,128)S(1)}, f32[4,32,128]{2,1,0:T(8,128)S(1)}, f32[4,...) custom-call(f32[32,128]{1,0:T(8,128)S(1)} %bitcast.10, f32[2,64,256]{2,1,0:T(8,128)S(1)} %bitcast.7, ...), custom_call_target="tpu_custom_call" | custom-call | flops 4000000 | bytes 1221120 | tf_op jit(solution)/shard_map/prepare/pallas_call | solution.py:303
  18.6 0.0 collective-permute-done.1.high
  18.6 4.0 %collective-permute-done.low = f32[32,128]{1,0:T(8,128)S(1)} collective-permute-done((f32[32,128]{1,0:T(8,128)}, f32[32,128]{1,0:T(8,128)S(1)}, u32[]{:S(2)}, u32[]{:S(2)}) %collective-permute-start) | collective-permute-done | bytes 16416 | tf_op jit(solution)/shard_map/ppermute | solution.py:320
  22.7 0.7 %forward.1 = (f32[8,32,128]{2,1,0:T(8,128)S(1)}, f32[4,32,128]{2,1,0:T(8,128)S(1)}, f32[32,128]{1,0:T(8,128)S(1)}) custom-call(f32[32,128]{1,0:T(8,128)S(1)} %bitcast.11, f32[32,128]{1,0:T(8,128)S(1)} %collective-permute-done.low, f32[32,128]{1,0:T(8,128)S(1)} %collective-permute-done.1.high, f32[8,32,128]{2,1,0:T(8,128)S(1)} %get-tuple-element.15.base, ...), custom_call_target="tpu_custom_call" | custom-call | flops 6000000 | bytes 1048576 | tf_op jit(solution)/shard_map/forward/pallas_call | solution.py:303
  23.4 5.2 %all-gather = f32[128,128]{1,0:T(8,128)S(1)} all-gather(f32[32,128]{1,0:T(8,128)S(1)} %get-tuple-element.20), channel_id=2, replica_groups=mesh['ang'=64,'rad'=4] {'rad'}, dimensions={0}, use_global_device_ids=true | all-gather | bytes 81920 | tf_op jit(solution)/shard_map/all_gather | solution.py:336
  28.6 2.0 %backward.1 = (f32[8,32,128]{2,1,0:T(8,128)S(1)}, f32[32,128]{1,0:T(8,128)S(1)}, f32[32,128]{1,0:T(8,128)S(1)}, f32[32,128]{1,0:T(8,128)S(1)}) custom-call(f32[4,32,128]{2,1,0:T(8,128)S(1)} %bitcast.6, f32[8,32,128]{2,1,0:T(8,128)S(1)} %get-tuple-element.21.dens, f32[4,32,128]{2,1,0:T(8,128)S(1)} %get-tuple-element.22.local, f32[27,8,512]{2,1,0:T(8,128)S(1)} %copy-done.1, ...), custom_call_target="tpu_custom_call" | custom-call | flops 8000000 | bytes 1081344 | tf_op jit(solution)/shard_map/backward/pallas_call | solution.py:303
  30.6 5.3 %collective-permute-start.2 = (f32[32,128]{1,0:T(8,128)S(1)}, f32[32,128]{1,0:T(8,128)S(1)}, u32[]{:S(2)}, u32[]{:S(2)}) collective-permute-start(f32[32,128]{1,0:T(8,128)S(1)} %get-tuple-element.26), channel_id=1, source_target_pairs={{4,0},{8,4},{12,8},{16,12},{20,16},{24,20},{28,24},{32,28},{36,32}... | collective-permute-start | bytes 49160 | tf_op jit(solution)/shard_map/ppermute | solution.py:341
  36.0 1.9 %collective-permute-start.3 = (f32[32,128]{1,0:T(8,128)S(1)}, f32[32,128]{1,0:T(8,128)S(1)}, u32[]{:S(2)}, u32[]{:S(2)}) collective-permute-start(f32[32,128]{1,0:T(8,128)S(1)} %get-tuple-element.27), channel_id=1, source_target_pairs={{0,4},{4,8},{8,12},{12,16},{16,20},{20,24},{24,28},{28,32},{32,36}... | collective-permute-start | bytes 49160 | tf_op jit(solution)/shard_map/ppermute | solution.py:342
  37.9 0.9 %finish.1 = f32[2,64,256]{2,1,0:T(8,128)} custom-call(f32[8,32,128]{2,1,0:T(8,128)S(1)} %get-tuple-element.23.grad, f32[8,32,128]{2,1,0:T(8,128)S(1)} %get-tuple-element.24.fields, f32[8,8,512]{2,1,0:T(8,128)S(1)} %copy-done.2), custom_call_target="tpu_custom_call" | custom-call | flops 4000000 | bytes 524288 | tf_op jit(solution)/shard_map/finish/pallas_call | solution.py:303
  38.7 0.0 collective-permute-done.2
  38.7 8.0 %collective-permute-done.3 = f32[32,128]{1,0:T(8,128)S(1)} collective-permute-done((f32[32,128]{1,0:T(8,128)S(1)}, f32[32,128]{1,0:T(8,128)S(1)}, u32[]{:S(2)}, u32[]{:S(2)}) %collective-permute-start.3) | collective-permute-done | bytes 16416 | tf_op jit(solution)/shard_map/ppermute | solution.py:342
  46.7 0.6 %add_bitcast_fusion = f32[1,1,32,128]{3,2,1,0:T(8,128)} fusion(f32[32,128]{1,0:T(8,128)S(1)} %collective-permute-done.3, f32[32,128]{1,0:T(8,128)S(1)} %get-tuple-element.25, f32[32,128]{1,0:T(8,128)S(1)} %collective-permute-done.2), kind=kLoop, calls=%fused_computation | loop fusion | flops 8192 | bytes 65536 | tf_op jit(solution)/shard_map/broadcast_in_dim | solution.py:348
  (7 shorter events, 0.0 us)
Async XLA Ops:
  0.6 14.7 %copy-start.2 = (f32[8,8,512]{2,1,0:T(8,128)S(1)}, f32[8,8,512]{2,1,0:T(8,128)}, u32[]{:S(2)}) copy-start(f32[8,8,512]{2,1,0:T(8,128)} %mixing.3) | copy-start | bytes 393220
  0.6 18.0 %collective-permute-start.1 = (f32[32,128]{1,0:T(8,128)}, f32[32,128]{1,0:T(8,128)S(1)}, u32[]{:S(2)}, u32[]{:S(2)}) collective-permute-start(f32[32,128]{1,0:T(8,128)} %bitcast.8), channel_id=1, source_target_pairs={{4,0},{8,4},{12,8},{16,12},{20,16},{24,20},{28,24},{32,28},{36,32}... | collective-permute-start | bytes 49160 | tf_op jit(solution)/shard_map/ppermute | solution.py:321
  11.7 11.0 %collective-permute-start = (f32[32,128]{1,0:T(8,128)}, f32[32,128]{1,0:T(8,128)S(1)}, u32[]{:S(2)}, u32[]{:S(2)}) collective-permute-start(f32[32,128]{1,0:T(8,128)} %bitcast.9), channel_id=1, source_target_pairs={{0,4},{4,8},{8,12},{12,16},{16,20},{20,24},{24,28},{28,32},{32,36}... | collective-permute-start | bytes 49160 | tf_op jit(solution)/shard_map/ppermute | solution.py:320
  14.4 0.8 %copy-start.6 = (f32[2,64,16]{1,2,0:T(8,128)S(1)}, f32[2,64,16]{1,2,0:T(8,128)}, u32[]{:S(2)}) copy-start(f32[2,64,16]{1,2,0:T(8,128)} %param.15) | copy-start | bytes 24580
  15.3 0.7 %copy-start.4 = (f32[1,1,32,128]{3,2,1,0:T(8,128)S(1)}, f32[1,1,32,128]{3,2,1,0:T(8,128)}, u32[]{:S(2)}) copy-start(f32[1,1,32,128]{3,2,1,0:T(8,128)} %param.8) | copy-start | bytes 49156
  15.3 0.7 %copy-start.5 = (s32[2,64]{1,0:T(2,128)S(1)}, s32[2,64]{1,0:T(2,128)}, u32[]{:S(2)}) copy-start(s32[2,64]{1,0:T(2,128)} %star_count.1) | copy-start | bytes 1540
  16.0 1.0 %copy-start = (f32[27,8,512]{2,1,0:T(8,128)S(1)}, f32[27,8,512]{2,1,0:T(8,128)}, u32[]{:S(2)}) copy-start(f32[27,8,512]{2,1,0:T(8,128)} %kernels.5) | copy-start | bytes 1327108
  17.0 0.9 %copy-start.3 = (f32[1,2,64,256]{3,2,1,0:T(8,128)S(1)}, f32[1,2,64,256]{3,2,1,0:T(8,128)}, u32[]{:S(2)}) copy-start(f32[1,2,64,256]{3,2,1,0:T(8,128)} %param.9) | copy-start | bytes 393220
  18.0 4.7 %copy-start.1 = (f32[27,8,512]{2,1,0:T(8,128)S(1)}, f32[27,8,512]{2,1,0:T(8,128)}, u32[]{:S(2)}) copy-start(f32[27,8,512]{2,1,0:T(8,128)} %kernels.5) | copy-start | bytes 1327108
  30.6 8.1 %collective-permute-start.2 = (f32[32,128]{1,0:T(8,128)S(1)}, f32[32,128]{1,0:T(8,128)S(1)}, u32[]{:S(2)}, u32[]{:S(2)}) collective-permute-start(f32[32,128]{1,0:T(8,128)S(1)} %get-tuple-element.26), channel_id=1, source_target_pairs={{4,0},{8,4},{12,8},{16,12},{20,16},{24,20},{28,24},{32,28},{36,32}... | collective-permute-start | bytes 49160 | tf_op jit(solution)/shard_map/ppermute | solution.py:341
  36.0 10.8 %collective-permute-start.3 = (f32[32,128]{1,0:T(8,128)S(1)}, f32[32,128]{1,0:T(8,128)S(1)}, u32[]{:S(2)}, u32[]{:S(2)}) collective-permute-start(f32[32,128]{1,0:T(8,128)S(1)} %get-tuple-element.27), channel_id=1, source_target_pairs={{0,4},{4,8},{8,12},{12,16},{16,20},{20,24},{24,28},{28,32},{32,36}... | collective-permute-start | bytes 49160 | tf_op jit(solution)/shard_map/ppermute | solution.py:342

commit v2 on v1

v2 whole, which is shorter than its diff:
```python
import jax
import jax.numpy as jnp
from jax import lax
from jax.experimental import pallas as pl
from jax.experimental.pallas import tpu as pltpu
from jax.sharding import PartitionSpec as P


F32 = jnp.float32
HI = lax.Precision.HIGHEST
VMEM = pl.BlockSpec(memory_space=pltpu.VMEM)


def lanes(shape):
    return lax.broadcasted_iota(jnp.int32, shape, 1)


def rows(shape):
    return lax.broadcasted_iota(jnp.int32, shape, 0)


def along(x, k, axis):
    if k == 0:
        return x
    n = x.shape[axis]
    at = lax.broadcasted_iota(jnp.int32, x.shape, axis)
    inside = at < n - k if k > 0 else at >= -k
    return jnp.where(inside, pltpu.roll(x, (-k) % n, axis), 0.0)


def pick(x, index):
    return jnp.take_along_axis(x, index, axis=1, mode="promise_in_bounds")


def split_pixels(ref, j):
    half = pl.ds(j, 32, stride=2)
    low, high = ref[0, half, :], ref[1, half, :]
    lane = lanes((32, 128))
    out = []
    for k in range(2):
        index = (2 * lane + k) & 127
        out.append(jnp.where(lane < 64, pick(low, index), pick(high, index)))
    return out


def taps(acc, row, weights):
    for w in range(3):
        moved = along(row, w - 1, 1)
        for v in range(3):
            window = along(moved, v - 1, 0)
            block = weights[3 * v + w]
            for q in range(8):
                acc[q] = acc[q] + block[q : q + 1, :] * window


def prepare(coarse_in, excite_in, kernels_in, mixing_in, bin_in, count_in, obs_in, isig_in,
            base, fields, hits_w, deep_w, deep_o, sums, mixing,
            slots, halves, coarse, kernels, star_bin, star_count, star_obs, star_isig, arrived):
    shard = lax.axis_index("rad")
    here = pl.ds(pl.multiple_of(shard * 128, 128), 128)
    moves = [(bin_in, star_bin), (count_in, star_count), (obs_in, star_obs), (isig_in, star_isig)]
    for i in range(2):
        for side in range(2):
            moves.append((excite_in.at[i, :, 128 * side : 128 * side + 128], halves.at[i, side]))
    moves += [(mixing_in.at[:, :, here], mixing), (coarse_in, coarse), (kernels_in.at[9:18, :, here], kernels)]
    moves = [pltpu.make_async_copy(a, b, arrived.at[n]) for n, (a, b) in enumerate(moves)]
    for move in moves:
        move.start()
    for move in moves[:4]:
        move.wait()
    slot = rows((16, 64)).astype(F32)
    stack = []
    for i in range(2):
        count = star_count[i : i + 1, :].astype(F32)
        rel = (star_bin[i] - 256 * shard).astype(F32)
        live = (slot < count) & (rel >= 0.0) & (rel < 256.0)
        isig = star_isig[i]
        w = jnp.where(live, isig * isig, 0.0)
        stack += [jnp.where(live, rel, -1.0), w, w * star_obs[i]]
    stack = jnp.concatenate(stack + [jnp.zeros((32, 64), F32)], axis=0)
    slots[...] = jnp.concatenate([stack, jnp.zeros((128, 64), F32)], axis=1).T
    for move in moves[4:]:
        move.wait()
    parts = []
    for i in range(2):
        for j in range(2):
            parts += split_pixels(halves.at[i], j)
    for p in range(8):
        fields[p] = parts[p]
    acc = []
    for q in range(8):
        block = mixing[q]
        total = block[0:1, :] * parts[0]
        for p in range(1, 8):
            total = total + block[p : p + 1, :] * parts[p]
        acc.append(total)
    taps(acc, coarse[...], [kernels[t] for t in range(9)])
    for q in range(8):
        base[q] = acc[q]
    lane = lanes((32, 128))
    bin0 = 2.0 * lane.astype(F32)
    bin1 = bin0 + 1.0
    zero = jnp.zeros((32, 128), F32)
    hits = [[zero] * 8, [zero] * 8]
    for j in range(2):
        stars = slots[pl.ds(j, 32, stride=2), :]
        for i in range(2):
            q = 4 * i + 2 * j
            for m in range(16):
                at = 48 * i + m
                rel = stars[:, at : at + 1]
                is0, is1 = rel == bin0, rel == bin1
                for f in range(2):
                    value = stars[:, at + 16 + 16 * f : at + 17 + 16 * f]
                    hits[f][q] = hits[f][q] + jnp.where(is0, value, 0.0)
                    hits[f][q + 1] = hits[f][q + 1] + jnp.where(is1, value, 0.0)
    pairs = jnp.concatenate([hits[f][2 * p] + hits[f][2 * p + 1] for f in range(2) for p in range(4)], axis=0)
    beyond = (rows((128, 128)) > lanes((128, 128))).astype(F32)
    after = jnp.dot(pairs, beyond, precision=HI, preferred_element_type=F32)
    table = zero
    for f, out in ((0, deep_w), (1, deep_o)):
        for p in range(4):
            second = after[128 * f + 32 * p : 128 * f + 32 * p + 32] + hits[f][2 * p + 1]
            first = second + hits[f][2 * p]
            for k, value in ((0, first), (1, second)):
                q = 2 * p + k
                out[q] = value
                table = jnp.where(lane == 40 + 16 * f + q, value[:, 0:1], table)
                table = jnp.where(lane == 48 + 16 * f + q, value[:, 127:128], table)
    for q in range(8):
        hits_w[q] = hits[0][q]
    sums[...] = table


def sides(odd, even):
    first = (lax.axis_index("ang") & 1) == 0
    return jnp.where(first, odd, even), jnp.where(first, even, odd)


def forward(coarse, odd, even, base, kernels, hits_w, sums, dens, prod, table):
    shard = lax.axis_index("rad")
    step = 1.0 / 1024
    acc = [base[q] for q in range(8)]
    low, high = sides(odd[...], even[...])
    here = pl.ds(pl.multiple_of(shard * 128, 128), 128)
    taps(acc, low, [kernels[t, :, here] for t in range(9)])
    taps(acc, high, [kernels[t, :, here] for t in range(18, 27)])
    lane = lanes((32, 128))
    out = sums[...]
    for q in range(8):
        out = jnp.where(lane == q, acc[q][:, 0:1], out)
        out = jnp.where(lane == 8 + q, acc[q][:, 127:128], out)
    for u, value in enumerate((low, coarse[...], high)):
        out = jnp.where(lane == 32 + u, value[:, 0:1], out)
        out = jnp.where(lane == 35 + u, value[:, 127:128], out)
    inner = (lane > 0) & (lane < 127)
    density = []
    for q in range(8):
        d = jnp.exp(acc[q])
        dens[q] = d
        density.append(jnp.where(inner, d, 0.0))
    pairs = jnp.concatenate([density[2 * p] + density[2 * p + 1] for p in range(4)], axis=0)
    strict = (rows((128, 128)) < lanes((128, 128))).astype(F32)
    before = jnp.dot(pairs, strict, precision=HI, preferred_element_type=F32)
    for p in range(4):
        first = before[32 * p : 32 * p + 32] + density[2 * p]
        second = first + density[2 * p + 1]
        first = weighed(step * first, hits_w[2 * p])
        total = second[:, 127:128]
        second = weighed(step * second, hits_w[2 * p + 1])
        prod[2 * p] = first
        prod[2 * p + 1] = second
        share = jnp.sum(first + second, axis=1, keepdims=True)
        for k in range(2):
            out = jnp.where(lane == 16 + 2 * p + k, total, out)
            out = jnp.where(lane == 24 + 2 * p + k, share, out)
    table[...] = out


def weighed(x, w):
    return jnp.where(w != 0.0, x * w, 0.0)


def swap(x):
    even = (rows(x.shape) & 1) == 0
    return jnp.where(even, pltpu.roll(x, x.shape[0] - 1, 0), pltpu.roll(x, 1, 0))


def spread(grad, columns):
    lane = lanes((32, 128))
    plus, minus = [], []
    for q in range(8):
        plus.append(jnp.where(lane == 127, columns[:, 32 + q : 33 + q], grad[q]))
        minus.append(jnp.where(lane == 0, columns[:, 40 + q : 41 + q], grad[q]))
    return minus, grad, plus


def to_row(u, fields, kernels, shard):
    at = pl.ds(pl.multiple_of(shard * 128, 128), 128)
    prev = pl.ds(pl.multiple_of(jnp.maximum(shard - 1, 0) * 128, 128), 128)
    after = pl.ds(pl.multiple_of(jnp.minimum(shard + 1, 3) * 128, 128), 128)
    lane = lanes((8, 128))
    total = None
    for w, field in enumerate(fields):
        part = None
        for v in range(3):
            t = 9 * u + 3 * v + w
            block = kernels[t, :, at]
            if w == 0:
                block = jnp.where(lane == 0, kernels[t, :, after], block)
            if w == 2:
                block = jnp.where(lane == 127, kernels[t, :, prev], block)
            piece = block[0:1, :] * field[0]
            for q in range(1, 8):
                piece = piece + block[q : q + 1, :] * field[q]
            piece = along(piece, 1 - v, 0)
            part = piece if part is None else part + piece
        if w != 1:
            part = pltpu.roll(part, (w - 1) % 128, 1)
        total = part if total is None else total + part
    return total


def backward(table, dens, prod, kernels, deep_w, deep_o, grad, edges_out, odd_out, even_out):
    shard = lax.axis_index("rad")
    step = 1.0 / 1024
    even = (rows((8, 128)) & 1) == 0
    pairs = jnp.concatenate([prod[2 * p] + prod[2 * p + 1] for p in range(4)], axis=0)
    beyond = (rows((128, 128)) > lanes((128, 128))).astype(F32)
    after = jnp.dot(pairs, beyond, precision=HI, preferred_element_type=F32)
    groups = []
    for s in range(4):
        full = jnp.concatenate([table[s], jnp.zeros((96, 128), F32)], axis=0).T
        groups.append([full[8 * g : 8 * g + 8] for g in range(9)])
    edges = []
    for s in range(4):
        e = groups[s][4]
        edges.append([along(e, v - 1, 1) for v in range(3)])
    d_low, d_high, totals, shares, whole, tails = [], [], [], [], [], []
    for s in range(4):
        f_low, f_high, t, c, _, w_low, w_high, o_low, _ = groups[s]
        for u in range(3):
            for v in range(3):
                if s > 0:
                    weight = kernels[9 * u + 3 * v, :, 128 * s : 128 * s + 128][:, 0:1]
                    f_low = f_low + weight * edges[s - 1][v][3 + u : 4 + u, :]
                if s < 3:
                    weight = kernels[9 * u + 3 * v + 2, :, 128 * s : 128 * s + 128][:, 127:128]
                    f_high = f_high + weight * edges[s + 1][v][u : u + 1, :]
        a, b = jnp.exp(f_low), jnp.exp(f_high)
        d_low.append(a)
        d_high.append(b)
        both = a + b
        totals.append(t + both + swap(both))
        tail = step * b * w_high
        tail = tail + swap(tail)
        tails.append(tail)
        head = step * a * w_low
        o_all = jnp.where(even, o_low, swap(o_low))
        shares.append(c - o_all + head + swap(head) + tail)
        whole.append(jnp.where(even, w_low, swap(w_low)))
    zero = jnp.zeros((8, 128), F32)
    nearer = [zero]
    for s in range(3):
        nearer.append(nearer[s] + totals[s])
    nearer = [step * x for x in nearer]
    sums = [shares[s] + weighed(nearer[s], whole[s]) for s in range(4)]
    farther = [zero]
    for s in (3, 2, 1):
        farther.insert(0, farther[0] + sums[s])

    def low_edge(s):
        w, o = groups[s][5], groups[s][7]
        first = weighed(nearer[s] + step * swap(d_low[s]), swap(w) - w) - (swap(o) - o)
        suffix = sums[s] - jnp.where(even, 0.0, first)
        return d_low[s] * step * (farther[s] + suffix)

    def high_edge(s):
        w, o = groups[s][6], groups[s][8]
        last = step * swap(d_high[s]) * (w - swap(w))
        suffix = weighed(nearer[s] + step * totals[s], w) - o - jnp.where(even, last, 0.0)
        return d_high[s] * step * (farther[s] + suffix)

    def mine(values):
        out = values[0]
        for s in range(1, 4):
            out = jnp.where(shard == s, values[s], out)
        return out

    lows = [low_edge(s) for s in range(4)]
    highs = [high_edge(s) for s in range(4)]
    columns = [mine(lows), mine(highs),
               mine([nearer[s] + step * (d_low[s] + swap(d_low[s])) for s in range(4)]),
               mine([farther[s] + tails[s] for s in range(4)]),
               mine([zero] + highs[:3]), mine(lows[1:] + [zero])]
    columns = jnp.concatenate(columns + [jnp.zeros((80, 128), F32)], axis=0).T[0:32]
    edges_out[...] = columns
    lane = lanes((32, 128))
    grads = []
    for p in range(4):
        near, far = columns[:, 16 + 2 * p : 17 + 2 * p], columns[:, 24 + 2 * p : 25 + 2 * p]
        second = after[32 * p : 32 * p + 32] + prod[2 * p + 1]
        first = second + prod[2 * p]
        for k, share in ((0, first), (1, second)):
            q = 2 * p + k
            suffix = far + weighed(near, deep_w[q]) + (share - deep_o[q])
            g = step * dens[q] * suffix
            g = jnp.where(lane == 0, columns[:, q : q + 1], g)
            g = jnp.where(lane == 127, columns[:, 8 + q : 9 + q], g)
            grad[q] = g
            grads.append(g)
    fields = spread(grads, columns)
    odd, even_row = sides(to_row(0, fields, kernels, shard), to_row(2, fields, kernels, shard))
    odd_out[...] = odd
    even_out[...] = even_row


def finish(grad, columns, fields, kernels, mixing, out, own, halves):
    shard = lax.axis_index("rad")
    lane = lanes((32, 128))
    grads = [grad[q] for q in range(8)]
    acc = [fields[p] for p in range(8)]
    for q in range(8):
        block = mixing[q]
        for p in range(8):
            acc[p] = acc[p] + block[p : p + 1, :] * grads[q]
    for i in range(2):
        for j in range(2):
            pair = acc[4 * i + 2 * j : 4 * i + 2 * j + 2]
            half = pl.ds(j, 32, stride=2)
            for side in range(2):
                index = (lane >> 1) + 64 * side
                value = jnp.where((lane & 1) == 0, pick(pair[0], index), pick(pair[1], index))
                halves[side, half, :] = value
        for side in range(2):
            out[i, :, 128 * side : 128 * side + 128] = halves[side]
    own[...] = to_row(1, spread(grads, columns[...]), kernels, shard)


def call(body, ins, outs, flops, scratch=(), space=pltpu.VMEM):
    shapes = tuple(jax.ShapeDtypeStruct(s, d) for s, d in outs)
    size = sum(x.size * 4 for x in ins) + sum(x.size * 4 for x in shapes)
    return pl.pallas_call(
        body,
        out_shape=shapes,
        in_specs=[pl.BlockSpec(memory_space=space)] * len(ins),
        out_specs=tuple([VMEM] * len(shapes)),
        scratch_shapes=list(scratch),
        cost_estimate=pl.CostEstimate(flops=flops, bytes_accessed=size, transcendentals=0),
        compiler_params=pltpu.CompilerParams(vmem_limit_bytes=16 << 20),
    )(*ins)


def per_device(coarse, excite, kernels, mixing, star_bin, star_count, star_obs, star_isig):
    count = lax.axis_size("ang")
    pairs = [[], []]
    for i in range(count - 1):
        pairs[i % 2] += [(i, i + 1), (i + 1, i)]

    def exchange(odd, even):
        even = lax.ppermute(even, "ang", pairs[0])
        odd = lax.ppermute(odd, "ang", pairs[1])
        return odd, even

    own = coarse[0, 0]
    odd = lax.ppermute(own, "ang", pairs[1])
    even = lax.ppermute(own, "ang", pairs[0])
    block = ((8, 32, 128), F32)
    row = ((32, 128), F32)
    stars = [x.transpose(0, 2, 1) for x in (star_bin, star_obs, star_isig)]
    base, fields, hits_w, deep_w, deep_o, sums, mixing_here = call(
        prepare,
        [pltpu.with_memory_space_constraint(x, pltpu.HBM) for x in
         (own, excite[0], kernels, mixing, stars[0], star_count, stars[1], stars[2])],
        (block, block, block, block, block, row, ((8, 8, 128), F32)), 4_000_000,
        [pltpu.VMEM((128, 128), F32), pltpu.VMEM((2, 2, 64, 128), F32), pltpu.VMEM((32, 128), F32),
         pltpu.VMEM((9, 8, 128), F32), pltpu.VMEM((2, 16, 64), jnp.int32), pltpu.VMEM((2, 64), jnp.int32),
         pltpu.VMEM((2, 16, 64), F32), pltpu.VMEM((2, 16, 64), F32), pltpu.SemaphoreType.DMA((11,))],
        pltpu.HBM,
    )
    dens, prod, table = call(
        forward, (own, odd, even, base, kernels, hits_w, sums),
        (block, block, row), 6_000_000,
    )
    tables = lax.all_gather(table, "rad")
    grad, columns, odd, even = call(
        backward, (tables, dens, prod, kernels, deep_w, deep_o),
        (block, row, row, row), 8_000_000,
    )
    odd, even = exchange(odd, even)
    grad_excite, here = call(
        finish, (grad, columns, fields, kernels, mixing_here),
        (((2, 64, 256), F32), row), 4_000_000,
        [pltpu.VMEM((2, 64, 128), F32)],
    )
    grad_coarse = here + odd + even
    return grad_excite[None], grad_coarse[None, None]


def solution(mesh):
    in_specs = (
        P(None, "ang", None, "rad"),
        P(None, "ang", None, "rad"),
        P(),
        P(),
        P("ang", None, None),
        P("ang", None),
        P("ang", None, None),
        P("ang", None, None),
    )
    out_specs = (P(None, "ang", None, "rad"), P(None, "ang", None, "rad"))
    return jax.shard_map(
        per_device, mesh=mesh, in_specs=in_specs, out_specs=out_specs, check_vma=False
    )
```

time: 47.8 us -> 36.2 us (0.76)
  waiting for transfers between devices: 12 us -> 3.75 us
  local copies, waits for them, and re-layouts: 4.3 us -> 0.01 us
  Pallas kernels: 4.23 us -> 5.05 us
    ppermute x4, waiting for transfers between devices: 12 us -> 3.75 us  [the longest x1 2.05 us: exchange(): even = lax.ppermute(even, 'ang', pairs[0])]
    unnamed x17 -> x4, local copies, waits for them, and re-layouts: 4.3 us -> 0.01 us
    pallas_call x4, Pallas kernels: 4.23 us -> 5.05 us  [call(): pl.pallas_call(body, out_shape=shapes, in_specs=[pl.BlockSpec(memory_spac...]
  transfers between devices with their start and end apart: 4 -> 4, of which waited for: 2 -> 2; matrix products, arithmetic and copies ran while one was open for 4% -> 0% of each run, Pallas kernels for 3% -> 10%
where the time goes in v2:
time: 36.2 us; the launch traced here: 36 us
  starting transfers between devices  20.6 us (57%)
  blocking collectives  5.24 us (14%)
  Pallas kernels  5.05 us (14%)
  waiting for transfers between devices  3.75 us (10%)
  between operations  0.73 us (2%)
  other arithmetic  0.61 us (2%)
    ppermute x1, starting transfers between devices, per_device(): odd = lax.ppermute(own, 'ang', pairs[1])  9.09 us
    ppermute x1, starting transfers between devices, exchange(): odd = lax.ppermute(odd, 'ang', pairs[1])  8.06 us
    all_gather x1, blocking collectives, per_device(): tables = lax.all_gather(table, 'rad')  5.24 us
    pallas_call x4, Pallas kernels, call(): pl.pallas_call(body, out_shape=shapes, in_specs=[pl.BlockSpec(memory_spac...  5.05 us
    ppermute x1, starting transfers between devices, per_device(): even = lax.ppermute(own, 'ang', pairs[0])  3.36 us
    ppermute x1, waiting for transfers between devices, exchange(): even = lax.ppermute(even, 'ang', pairs[0])  2.05 us
    ppermute x1, waiting for transfers between devices, exchange(): odd = lax.ppermute(odd, 'ang', pairs[1])  1.69 us
  transfers between devices with their start and end apart: 4, of which 2 were waited for; matrix products, arithmetic and copies ran while one was open for 0% of the time, Pallas kernels for 10%

profile of v2, /device:TPU:6, one launch (start us, length us, event | category | flops | bytes accessed | tf_op | source)
XLA Modules:
  0.0 36.0 jit_solution(17567931812510545676)
XLA Ops:
  0.6 0.0 copy-start
  0.6 3.4 %collective-permute-start.1 = (f32[32,128]{1,0:T(8,128)}, f32[32,128]{1,0:T(8,128)S(1)}, u32[]{:S(2)}, u32[]{:S(2)}) collective-permute-start(f32[32,128]{1,0:T(8,128)} %bitcast.10), channel_id=1, source_target_pairs={{0,4},{4,0},{8,12},{12,8},{16,20},{20,16},{24,28},{28,24},{32,36},... | collective-permute-start | bytes 49160 | tf_op jit(solution)/shard_map/ppermute | solution.py:367
  4.0 9.1 %collective-permute-start = (f32[32,128]{1,0:T(8,128)}, f32[32,128]{1,0:T(8,128)S(1)}, u32[]{:S(2)}, u32[]{:S(2)}) collective-permute-start(f32[32,128]{1,0:T(8,128)} %bitcast.11), channel_id=1, source_target_pairs={{4,8},{8,4},{12,16},{16,12},{20,24},{24,20},{28,32},{32,28},{36,40... | collective-permute-start | bytes 49160 | tf_op jit(solution)/shard_map/ppermute | solution.py:366
  13.1 0.0 copy-start.1
  13.1 2.8 %shard_map.95 = (f32[8,32,128]{2,1,0:T(8,128)S(1)}, f32[8,32,128]{2,1,0:T(8,128)S(1)}, f32[8,32,128]{2,1,0:T(8,128)S(1)}, f32[8,32,128]{2,1,0:T(8,128)S(1)}, f32...) custom-call(f32[32,128]{1,0:T(8,128)} %bitcast.12, f32[2,64,256]{2,1,0:T(8,128)} %bitcast.14, ...), custom_call_target="tpu_custom_call" | custom-call | flops 4000000 | bytes 1450496 | tf_op jit(solution)/shard_map/pallas_call | solution.py:343
  16.0 0.0 collective-permute-done.1.even
  16.0 0.0 collective-permute-done.odd
  16.0 0.0 copy-done
  16.0 0.0 copy-done.1
  16.0 0.6 %shard_map.96 = (f32[8,32,128]{2,1,0:T(8,128)S(1)}, f32[8,32,128]{2,1,0:T(8,128)S(1)}, f32[32,128]{1,0:T(8,128)S(1)}) custom-call(f32[32,128]{1,0:T(8,128)S(1)} %bitcast.13, f32[32,128]{1,0:T(8,128)S(1)} %collective-permute-done.odd, f32[32,128]{1,0:T(8,128)S(1)} %collective-permute-done.1.even, f32[8,32,128]{2,1,0:T(8,128)S(1)} %get-tuple-element.18.base, ...), custom_call_target="tpu_custom_call" | custom-call | flops 6000000 | bytes 1048576 | tf_op jit(solution)/shard_map/pallas_call | solution.py:343
  16.6 5.2 %all-gather = f32[128,128]{1,0:T(8,128)S(1)} all-gather(f32[32,128]{1,0:T(8,128)S(1)} %get-tuple-element.21), channel_id=2, replica_groups=mesh['ang'=64,'rad'=4] {'rad'}, dimensions={0}, use_global_device_ids=true | all-gather | bytes 81920 | tf_op jit(solution)/shard_map/all_gather | solution.py:385
  21.8 0.7 %shard_map.97 = (f32[8,32,128]{2,1,0:T(8,128)S(1)}, f32[32,128]{1,0:T(8,128)S(1)}, f32[32,128]{1,0:T(8,128)S(1)}, f32[32,128]{1,0:T(8,128)S(1)}) custom-call(f32[4,32,128]{2,1,0:T(8,128)S(1)} %bitcast.9, f32[8,32,128]{2,1,0:T(8,128)S(1)} %get-tuple-element.22.dens, f32[8,32,128]{2,1,0:T(8,128)S(1)} %get-tuple-element.23.prod, f32[27,8,512]{2,1,0:T(8,128)S(1)} %copy-done, ...), custom_call_target="tpu_custom_call" | custom-call | flops 8000000 | bytes 1212416 | tf_op jit(solution)/shard_map/pallas_call | solution.py:343
  22.6 8.1 %collective-permute-start.2 = (f32[32,128]{1,0:T(8,128)S(1)}, f32[32,128]{1,0:T(8,128)S(1)}, u32[]{:S(2)}, u32[]{:S(2)}) collective-permute-start(f32[32,128]{1,0:T(8,128)S(1)} %get-tuple-element.32), channel_id=1, source_target_pairs={{4,8},{8,4},{12,16},{16,12},{20,24},{24,20},{28,32},{32,28},{36,40... | collective-permute-start | bytes 49160 | tf_op jit(solution)/shard_map/ppermute | solution.py:362
  30.7 0.1 collective-permute-start.3
  30.8 0.9 %shard_map.98 = (f32[2,64,256]{2,1,0:T(8,128)}, f32[32,128]{1,0:T(8,128)S(1)}) custom-call(f32[8,32,128]{2,1,0:T(8,128)S(1)} %get-tuple-element.26.grad, f32[32,128]{1,0:T(8,128)S(1)} %get-tuple-element.27.columns, f32[8,32,128]{2,1,0:T(8,128)S(1)} %get-tuple-element.28.fields, f32[27,8,512]{2,1,0:T(8,128)S(1)} %copy-done, ...), custom_call_target="tpu_custom_call" | custom-call | flops 4000000 | bytes 901120 | tf_op jit(solution)/shard_map/pallas_call | solution.py:343
  31.6 1.7 %collective-permute-done.2 = f32[32,128]{1,0:T(8,128)S(1)} collective-permute-done((f32[32,128]{1,0:T(8,128)S(1)}, f32[32,128]{1,0:T(8,128)S(1)}, u32[]{:S(2)}, u32[]{:S(2)}) %collective-permute-start.2) | collective-permute-done | bytes 16416 | tf_op jit(solution)/shard_map/ppermute | solution.py:362
  33.3 2.0 %collective-permute-done.3 = f32[32,128]{1,0:T(8,128)S(1)} collective-permute-done((f32[32,128]{1,0:T(8,128)S(1)}, f32[32,128]{1,0:T(8,128)S(1)}, u32[]{:S(2)}, u32[]{:S(2)}) %collective-permute-start.3) | collective-permute-done | bytes 16416 | tf_op jit(solution)/shard_map/ppermute | solution.py:361
  35.4 0.6 %add_bitcast_fusion = f32[1,1,32,128]{3,2,1,0:T(8,128)} fusion(f32[32,128]{1,0:T(8,128)S(1)} %collective-permute-done.3, f32[32,128]{1,0:T(8,128)S(1)} %get-tuple-element.31, f32[32,128]{1,0:T(8,128)S(1)} %collective-permute-done.2), kind=kLoop, calls=%fused_computation | loop fusion | flops 8192 | bytes 65536 | tf_op jit(solution)/shard_map/broadcast_in_dim | solution.py:397
Async XLA Ops:
  0.6 15.3 %copy-start = (f32[27,8,512]{2,1,0:T(8,128)S(1)}, f32[27,8,512]{2,1,0:T(8,128)}, u32[]{:S(2)}) copy-start(f32[27,8,512]{2,1,0:T(8,128)} %kernels.5) | copy-start | bytes 1327108
  0.6 15.3 %collective-permute-start.1 = (f32[32,128]{1,0:T(8,128)}, f32[32,128]{1,0:T(8,128)S(1)}, u32[]{:S(2)}, u32[]{:S(2)}) collective-permute-start(f32[32,128]{1,0:T(8,128)} %bitcast.10), channel_id=1, source_target_pairs={{0,4},{4,0},{8,12},{12,8},{16,20},{20,16},{24,28},{28,24},{32,36},... | collective-permute-start | bytes 49160 | tf_op jit(solution)/shard_map/ppermute | solution.py:367
  4.0 12.0 %collective-permute-start = (f32[32,128]{1,0:T(8,128)}, f32[32,128]{1,0:T(8,128)S(1)}, u32[]{:S(2)}, u32[]{:S(2)}) collective-permute-start(f32[32,128]{1,0:T(8,128)} %bitcast.11), channel_id=1, source_target_pairs={{4,8},{8,4},{12,16},{16,12},{20,24},{24,20},{28,32},{32,28},{36,40... | collective-permute-start | bytes 49160 | tf_op jit(solution)/shard_map/ppermute | solution.py:366
  13.1 2.9 %copy-start.1 = (f32[1,1,32,128]{3,2,1,0:T(8,128)S(1)}, f32[1,1,32,128]{3,2,1,0:T(8,128)}, u32[]{:S(2)}) copy-start(f32[1,1,32,128]{3,2,1,0:T(8,128)} %param.8) | copy-start | bytes 49156
  22.6 10.8 %collective-permute-start.2 = (f32[32,128]{1,0:T(8,128)S(1)}, f32[32,128]{1,0:T(8,128)S(1)}, u32[]{:S(2)}, u32[]{:S(2)}) collective-permute-start(f32[32,128]{1,0:T(8,128)S(1)} %get-tuple-element.32), channel_id=1, source_target_pairs={{4,8},{8,4},{12,16},{16,12},{20,24},{24,20},{28,32},{32,28},{36,40... | collective-permute-start | bytes 49160 | tf_op jit(solution)/shard_map/ppermute | solution.py:362
  30.7 4.7 %collective-permute-start.3 = (f32[32,128]{1,0:T(8,128)S(1)}, f32[32,128]{1,0:T(8,128)S(1)}, u32[]{:S(2)}, u32[]{:S(2)}) collective-permute-start(f32[32,128]{1,0:T(8,128)S(1)} %get-tuple-element.33), channel_id=1, source_target_pairs={{0,4},{4,0},{8,12},{12,8},{16,20},{20,16},{24,28},{28,24},{32,36},... | collective-permute-start | bytes 49160 | tf_op jit(solution)/shard_map/ppermute | solution.py:361

commit v3 on v2

--- a/solution.py
+++ b/solution.py
@@ -43,6 +43,10 @@
     return out
 
 
+def pixels(p):
+    return pl.ds(64 * (p // 2) + p % 2, 32, stride=2)
+
+
 def taps(acc, row, weights):
     for w in range(3):
         moved = along(row, w - 1, 1)
@@ -54,8 +58,8 @@
 
 
 def prepare(coarse_in, excite_in, kernels_in, mixing_in, bin_in, count_in, obs_in, isig_in,
-            base, fields, hits_w, deep_w, deep_o, sums, mixing,
-            slots, halves, coarse, kernels, star_bin, star_count, star_obs, star_isig, arrived):
+            base, fields, stars, sums, mixing,
+            turned, halves, coarse, kernels, star_bin, star_count, star_obs, star_isig, arrived):
     shard = lax.axis_index("rad")
     here = pl.ds(pl.multiple_of(shard * 128, 128), 128)
     moves = [(bin_in, star_bin), (count_in, star_count), (obs_in, star_obs), (isig_in, star_isig)]
@@ -68,17 +72,54 @@
         move.start()
     for move in moves[:4]:
         move.wait()
-    slot = rows((16, 64)).astype(F32)
-    stack = []
-    for i in range(2):
-        count = star_count[i : i + 1, :].astype(F32)
-        rel = (star_bin[i] - 256 * shard).astype(F32)
-        live = (slot < count) & (rel >= 0.0) & (rel < 256.0)
-        isig = star_isig[i]
-        w = jnp.where(live, isig * isig, 0.0)
-        stack += [jnp.where(live, rel, -1.0), w, w * star_obs[i]]
-    stack = jnp.concatenate(stack + [jnp.zeros((32, 64), F32)], axis=0)
-    slots[...] = jnp.concatenate([stack, jnp.zeros((128, 64), F32)], axis=1).T
+
+    def joined(x):
+        return jnp.concatenate([x[0], x[1]], axis=1)
+
+    count = jnp.concatenate([star_count[0:1, :], star_count[1:2, :]], axis=1)
+    rel = joined(star_bin) - 256 * shard
+    live = (rows((16, 128)) < count) & (rel >= 0) & (rel < 256)
+    isig = joined(star_isig)
+    w = jnp.where(live, isig * isig, 0.0)
+    o = w * joined(star_obs)
+    rel = jnp.where(live, rel, -1)
+    hits = [[[], []], [[], []]]
+    for tile in range(16):
+        bin0 = 2 * (rows((8, 128)) + 8 * tile)
+        bin1 = bin0 + 1
+        total = [[jnp.zeros((8, 128), F32)] * 2 for _ in range(2)]
+        for m in range(16):
+            at = rel[m : m + 1, :]
+            for k, bins in ((0, bin0), (1, bin1)):
+                here_now = at == bins
+                for f, value in ((0, w), (1, o)):
+                    total[f][k] = total[f][k] + jnp.where(here_now, value[m : m + 1, :], 0.0)
+        for f in range(2):
+            for k in range(2):
+                hits[f][k].append(total[f][k])
+    hits = [[jnp.concatenate(hits[f][k], axis=0) for k in range(2)] for f in range(2)]
+    pairs = jnp.concatenate([hits[f][0] + hits[f][1] for f in range(2)], axis=1)
+    beyond = (lanes((128, 128)) > rows((128, 128))).astype(F32)
+    after = jnp.dot(beyond, pairs, precision=HI, preferred_element_type=F32)
+    ends = []
+    for f in range(2):
+        second = after[:, 128 * f : 128 * f + 128] + hits[f][1]
+        first = second + hits[f][0]
+        for k, value in ((0, first), (1, second)):
+            stars[2 + 2 * f + k] = value.T
+            ends.append((40 + 16 * f + k, value[0:1, :]))
+            ends.append((48 + 16 * f + k, value[127:128, :]))
+    for k in range(2):
+        stars[k] = hits[0][k].T
+    row = rows((8, 128))
+    groups = [jnp.zeros((8, 128), F32)] * 16
+    for at, value in ends:
+        groups[at // 8] = jnp.where(row == at % 8, value, groups[at // 8])
+    turned[...] = jnp.concatenate(groups, axis=0).T
+    table = jnp.zeros((32, 128), F32)
+    for p in range(4):
+        table = table + pltpu.roll(turned[pixels(p), :], 2 * p, 1)
+    sums[...] = table
     for move in moves[4:]:
         move.wait()
     parts = []
@@ -97,39 +138,6 @@
     taps(acc, coarse[...], [kernels[t] for t in range(9)])
     for q in range(8):
         base[q] = acc[q]
-    lane = lanes((32, 128))
-    bin0 = 2.0 * lane.astype(F32)
-    bin1 = bin0 + 1.0
-    zero = jnp.zeros((32, 128), F32)
-    hits = [[zero] * 8, [zero] * 8]
-    for j in range(2):
-        stars = slots[pl.ds(j, 32, stride=2), :]
-        for i in range(2):
-            q = 4 * i + 2 * j
-            for m in range(16):
-                at = 48 * i + m
-                rel = stars[:, at : at + 1]
-                is0, is1 = rel == bin0, rel == bin1
-                for f in range(2):
-                    value = stars[:, at + 16 + 16 * f : at + 17 + 16 * f]
-                    hits[f][q] = hits[f][q] + jnp.where(is0, value, 0.0)
-                    hits[f][q + 1] = hits[f][q + 1] + jnp.where(is1, value, 0.0)
-    pairs = jnp.concatenate([hits[f][2 * p] + hits[f][2 * p + 1] for f in range(2) for p in range(4)], axis=0)
-    beyond = (rows((128, 128)) > lanes((128, 128))).astype(F32)
-    after = jnp.dot(pairs, beyond, precision=HI, preferred_element_type=F32)
-    table = zero
-    for f, out in ((0, deep_w), (1, deep_o)):
-        for p in range(4):
-            second = after[128 * f + 32 * p : 128 * f + 32 * p + 32] + hits[f][2 * p + 1]
-            first = second + hits[f][2 * p]
-            for k, value in ((0, first), (1, second)):
-                q = 2 * p + k
-                out[q] = value
-                table = jnp.where(lane == 40 + 16 * f + q, value[:, 0:1], table)
-                table = jnp.where(lane == 48 + 16 * f + q, value[:, 127:128], table)
-    for q in range(8):
-        hits_w[q] = hits[0][q]
-    sums[...] = table
 
 
 def sides(odd, even):
@@ -137,7 +145,7 @@
     return jnp.where(first, odd, even), jnp.where(first, even, odd)
 
 
-def forward(coarse, odd, even, base, kernels, hits_w, sums, dens, prod, table):
+def forward(coarse, odd, even, base, kernels, stars, sums, dens, prod, table):
     shard = lax.axis_index("rad")
     step = 1.0 / 1024
     acc = [base[q] for q in range(8)]
@@ -165,9 +173,9 @@
     for p in range(4):
         first = before[32 * p : 32 * p + 32] + density[2 * p]
         second = first + density[2 * p + 1]
-        first = weighed(step * first, hits_w[2 * p])
+        first = weighed(step * first, stars[0, pixels(p), :])
         total = second[:, 127:128]
-        second = weighed(step * second, hits_w[2 * p + 1])
+        second = weighed(step * second, stars[1, pixels(p), :])
         prod[2 * p] = first
         prod[2 * p + 1] = second
         share = jnp.sum(first + second, axis=1, keepdims=True)
@@ -221,16 +229,20 @@
     return total
 
 
-def backward(table, dens, prod, kernels, deep_w, deep_o, grad, edges_out, odd_out, even_out):
+def backward(own, by1, by2, by3, dens, prod, kernels, stars, grad, edges_out, odd_out, even_out):
     shard = lax.axis_index("rad")
     step = 1.0 / 1024
     even = (rows((8, 128)) & 1) == 0
     pairs = jnp.concatenate([prod[2 * p] + prod[2 * p + 1] for p in range(4)], axis=0)
     beyond = (rows((128, 128)) > lanes((128, 128))).astype(F32)
     after = jnp.dot(pairs, beyond, precision=HI, preferred_element_type=F32)
+    held = [own[...], by1[...], by2[...], by3[...]]
     groups = []
     for s in range(4):
-        full = jnp.concatenate([table[s], jnp.zeros((96, 128), F32)], axis=0).T
+        table = held[0]
+        for k in range(1, 4):
+            table = jnp.where(shard == (s ^ k), held[k], table)
+        full = jnp.concatenate([table, jnp.zeros((96, 128), F32)], axis=0).T
         groups.append([full[8 * g : 8 * g + 8] for g in range(9)])
     edges = []
     for s in range(4):
@@ -303,7 +315,7 @@
         first = second + prod[2 * p]
         for k, share in ((0, first), (1, second)):
             q = 2 * p + k
-            suffix = far + weighed(near, deep_w[q]) + (share - deep_o[q])
+            suffix = far + weighed(near, stars[2 + k, pixels(p), :]) + (share - stars[4 + k, pixels(p), :])
             g = step * dens[q] * suffix
             g = jnp.where(lane == 0, columns[:, q : q + 1], g)
             g = jnp.where(lane == 127, columns[:, 8 + q : 9 + q], g)
@@ -315,7 +327,7 @@
     even_out[...] = even_row
 
 
-def finish(grad, columns, fields, kernels, mixing, out, own, halves):
+def finish(grad, columns, fields, kernels, mixing, even, odd, out, own, halves):
     shard = lax.axis_index("rad")
     lane = lanes((32, 128))
     grads = [grad[q] for q in range(8)]
@@ -334,7 +346,11 @@
                 halves[side, half, :] = value
         for side in range(2):
             out[i, :, 128 * side : 128 * side + 128] = halves[side]
-    own[...] = to_row(1, spread(grads, columns[...]), kernels, shard)
+    place = lax.axis_index("ang")
+    other = jnp.where((place & 1) == 0, odd[0:32], odd[32:64])
+    met = (place > 0) & (place < lax.axis_size("ang") - 1)
+    total = to_row(1, spread(grads, columns[...]), kernels, shard) + even[...]
+    own[...] = total + jnp.where(met, other, 0.0)
 
 
 def call(body, ins, outs, flops, scratch=(), space=pltpu.VMEM):
@@ -357,43 +373,39 @@
     for i in range(count - 1):
         pairs[i % 2] += [(i, i + 1), (i + 1, i)]
 
-    def exchange(odd, even):
-        even = lax.ppermute(even, "ang", pairs[0])
-        odd = lax.ppermute(odd, "ang", pairs[1])
-        return odd, even
-
     own = coarse[0, 0]
     odd = lax.ppermute(own, "ang", pairs[1])
     even = lax.ppermute(own, "ang", pairs[0])
     block = ((8, 32, 128), F32)
     row = ((32, 128), F32)
     stars = [x.transpose(0, 2, 1) for x in (star_bin, star_obs, star_isig)]
-    base, fields, hits_w, deep_w, deep_o, sums, mixing_here = call(
+    base, fields, stars, sums, mixing_here = call(
         prepare,
         [pltpu.with_memory_space_constraint(x, pltpu.HBM) for x in
          (own, excite[0], kernels, mixing, stars[0], star_count, stars[1], stars[2])],
-        (block, block, block, block, block, row, ((8, 8, 128), F32)), 4_000_000,
+        (block, block, ((6, 128, 128), F32), row, ((8, 8, 128), F32)), 4_000_000,
         [pltpu.VMEM((128, 128), F32), pltpu.VMEM((2, 2, 64, 128), F32), pltpu.VMEM((32, 128), F32),
          pltpu.VMEM((9, 8, 128), F32), pltpu.VMEM((2, 16, 64), jnp.int32), pltpu.VMEM((2, 64), jnp.int32),
          pltpu.VMEM((2, 16, 64), F32), pltpu.VMEM((2, 16, 64), F32), pltpu.SemaphoreType.DMA((11,))],
         pltpu.HBM,
     )
     dens, prod, table = call(
-        forward, (own, odd, even, base, kernels, hits_w, sums),
+        forward, (own, odd, even, base, kernels, stars, sums),
         (block, block, row), 6_000_000,
     )
-    tables = lax.all_gather(table, "rad")
+    others = [lax.ppermute(table, "rad", [(i, i ^ k) for i in range(4)]) for k in (1, 2, 3)]
     grad, columns, odd, even = call(
-        backward, (tables, dens, prod, kernels, deep_w, deep_o),
+        backward, (table, *others, dens, prod, kernels, stars),
         (block, row, row, row), 8_000_000,
     )
-    odd, even = exchange(odd, even)
-    grad_excite, here = call(
-        finish, (grad, columns, fields, kernels, mixing_here),
+    even = lax.ppermute(even, "ang", pairs[0])
+    groups = [[i, (i + 1) % count] for i in range(1, count, 2)]
+    odd = lax.all_gather(odd, "ang", axis_index_groups=groups, tiled=True)
+    grad_excite, grad_coarse = call(
+        finish, (grad, columns, fields, kernels, mixing_here, even, odd),
         (((2, 64, 256), F32), row), 4_000_000,
         [pltpu.VMEM((2, 64, 128), F32)],
     )
-    grad_coarse = here + odd + even
     return grad_excite[None], grad_coarse[None, None]
 
 

time: 36.2 us -> 31.5 us (0.87)
  the two profiles are of different devices: /device:TPU:6 before, /device:TPU:1 now
where the time goes in v3:
time: 31.5 us; the launch traced here: 31.3 us
  starting transfers between devices  13.6 us (43%)
  blocking collectives  9.98 us (32%)
  Pallas kernels  4.49 us (14%)
  waiting for transfers between devices  2.55 us (8%)
  between operations  0.71 us (2%)
    all_gather x1, blocking collectives, per_device(): odd = lax.all_gather(odd, 'ang', axis_index_groups=groups, tiled=True)  9.98 us
    ppermute x1, starting transfers between devices, per_device(): even = lax.ppermute(even, 'ang', pairs[0])  5.95 us
    pallas_call x4, Pallas kernels, call(): pl.pallas_call(body, out_shape=shapes, in_specs=[pl.BlockSpec(memory_spac...  4.49 us
    ppermute x1, starting transfers between devices, per_device(): even = lax.ppermute(own, 'ang', pairs[0])  3.9 us
    ppermute x3, starting transfers between devices, per_device(): lax.ppermute(table, 'rad', [(i, i ^ k) for i in range(4)])  3.06 us
    ppermute x3, waiting for transfers between devices, per_device(): lax.ppermute(table, 'rad', [(i, i ^ k) for i in range(4)])  2.54 us
    ppermute x1, starting transfers between devices, per_device(): odd = lax.ppermute(own, 'ang', pairs[1])  0.65 us
  transfers between devices with their start and end apart: 6, of which 2 were waited for; matrix products, arithmetic and copies ran while one was open for 0% of the time, Pallas kernels for 7%

profile of v3, /device:TPU:1, one launch (start us, length us, event | category | flops | bytes accessed | tf_op | source)
XLA Modules:
  0.0 31.3 jit_solution(13560273317274995144)
XLA Ops:
  0.6 0.0 copy-start
  0.6 3.9 %collective-permute-start.1 = (f32[32,128]{1,0:T(8,128)}, f32[32,128]{1,0:T(8,128)S(1)}, u32[]{:S(2)}, u32[]{:S(2)}) collective-permute-start(f32[32,128]{1,0:T(8,128)} %bitcast.7), channel_id=1, source_target_pairs={{0,4},{4,0},{8,12},{12,8},{16,20},{20,16},{24,28},{28,24},{32,36},... | collective-permute-start | bytes 49160 | tf_op jit(solution)/shard_map/ppermute | solution.py:378
  4.5 0.7 %collective-permute-start = (f32[32,128]{1,0:T(8,128)}, f32[32,128]{1,0:T(8,128)S(1)}, u32[]{:S(2)}, u32[]{:S(2)}) collective-permute-start(f32[32,128]{1,0:T(8,128)} %bitcast.8), channel_id=1, source_target_pairs={{4,8},{8,4},{12,16},{16,12},{20,24},{24,20},{28,32},{32,28},{36,40... | collective-permute-start | bytes 49160 | tf_op jit(solution)/shard_map/ppermute | solution.py:377
  5.2 0.0 copy-start.1
  5.2 2.1 %shard_map.95 = (f32[8,32,128]{2,1,0:T(8,128)S(1)}, f32[8,32,128]{2,1,0:T(8,128)S(1)}, f32[6,128,128]{2,1,0:T(8,128)S(1)}, f32[32,128]{1,0:T(8,128)S(1)}, f32[8,8,128]{2,1,0:T(8,128)S(1)}) custom-call(f32[32,128]{1,0:T(8,128)} %bitcast.9, f32[2,64,256]{2,1,0:T(8,128)} %bitcast.11, f32[27,8,512]{2,1,0:T(8,128)} %kernels.5, f32[8,8,512]{2,1,0:T(8,128)} %mixing_in.1, ...), custom_call_target="tpu_custom_call" | custom-call | flops 4000000 | bytes 1450496 | tf_op jit(solution)/shard_map/pallas_call | solution.py:359
  7.3 0.0 collective-permute-done.1.even
  7.4 0.0 collective-permute-done.odd
  7.4 0.0 copy-done
  7.4 0.0 copy-done.1
  7.4 0.6 %shard_map.96 = (f32[8,32,128]{2,1,0:T(8,128)S(1)}, f32[8,32,128]{2,1,0:T(8,128)S(1)}, f32[32,128]{1,0:T(8,128)S(1)}) custom-call(f32[32,128]{1,0:T(8,128)S(1)} %bitcast.10, f32[32,128]{1,0:T(8,128)S(1)} %collective-permute-done.odd, f32[32,128]{1,0:T(8,128)S(1)} %collective-permute-done.1.even, f32[8,32,128]{2,1,0:T(8,128)S(1)} %get-tuple-element.16.base, ...), custom_call_target="tpu_custom_call" | custom-call | flops 6000000 | bytes 1310720 | tf_op jit(solution)/shard_map/pallas_call | solution.py:359
  8.0 2.6 %collective-permute-start.4 = (f32[32,128]{1,0:T(8,128)S(1)}, f32[32,128]{1,0:T(8,128)S(1)}, u32[]{:S(2)}, u32[]{:S(2)}) collective-permute-start(f32[32,128]{1,0:T(8,128)S(1)} %get-tuple-element.19.own), channel_id=1, source_target_pairs={{0,3},{1,2},{2,1},{3,0},{4,7},{5,6},{6,5},{7,4},{8,11},{9,10},{10,... | collective-permute-start | bytes 49160 | tf_op jit(solution)/shard_map/ppermute | solution.py:396
  10.6 0.4 %collective-permute-start.3 = (f32[32,128]{1,0:T(8,128)S(1)}, f32[32,128]{1,0:T(8,128)S(1)}, u32[]{:S(2)}, u32[]{:S(2)}) collective-permute-start(f32[32,128]{1,0:T(8,128)S(1)} %get-tuple-element.19.own), channel_id=1, source_target_pairs={{0,2},{1,3},{2,0},{3,1},{4,6},{5,7},{6,4},{7,5},{8,10},{9,11},{10,... | collective-permute-start | bytes 49160 | tf_op jit(solution)/shard_map/ppermute | solution.py:396
  11.0 0.1 collective-permute-start.2
  11.1 1.3 %collective-permute-done.4.by3 = f32[32,128]{1,0:T(8,128)S(1)} collective-permute-done((f32[32,128]{1,0:T(8,128)S(1)}, f32[32,128]{1,0:T(8,128)S(1)}, u32[]{:S(2)}, u32[]{:S(2)}) %collective-permute-start.4) | collective-permute-done | bytes 16416 | tf_op jit(solution)/shard_map/ppermute | solution.py:396
  12.4 1.3 %collective-permute-done.3.by2 = f32[32,128]{1,0:T(8,128)S(1)} collective-permute-done((f32[32,128]{1,0:T(8,128)S(1)}, f32[32,128]{1,0:T(8,128)S(1)}, u32[]{:S(2)}, u32[]{:S(2)}) %collective-permute-start.3) | collective-permute-done | bytes 16416 | tf_op jit(solution)/shard_map/ppermute | solution.py:396
  13.6 0.0 collective-permute-done.2.by1
  13.6 0.7 %shard_map.97 = (f32[8,32,128]{2,1,0:T(8,128)S(1)}, f32[32,128]{1,0:T(8,128)S(1)}, f32[32,128]{1,0:T(8,128)S(1)}, f32[32,128]{1,0:T(8,128)S(1)}) custom-call(f32[32,128]{1,0:T(8,128)S(1)} %get-tuple-element.19.own, f32[32,128]{1,0:T(8,128)S(1)} %collective-permute-done.2.by1, f32[32,128]{1,0:T(8,128)S(1)} %collective-permute-done.3.by2, ...), custom_call_target="tpu_custom_call" | custom-call | flops 8000000 | bytes 1343488 | tf_op jit(solution)/shard_map/pallas_call | solution.py:359
  14.4 6.0 %collective-permute-start.5 = (f32[32,128]{1,0:T(8,128)S(1)}, f32[32,128]{1,0:T(8,128)S(1)}, u32[]{:S(2)}, u32[]{:S(2)}) collective-permute-start(f32[32,128]{1,0:T(8,128)S(1)} %get-tuple-element.26), channel_id=1, source_target_pairs={{0,4},{4,0},{8,12},{12,8},{16,20},{20,16},{24,28},{28,24},{32,36},... | collective-permute-start | bytes 49160 | tf_op jit(solution)/shard_map/ppermute | solution.py:401
  20.3 10.0 %all_gather.3.odd = f32[64,128]{1,0:T(8,128)S(1)} all-gather(f32[32,128]{1,0:T(8,128)S(1)} %get-tuple-element.27), channel_id=1, replica_groups={{4,8},{12,16},{20,24},{28,32},{36,40},{44,48},{52,56},{60,64},{68,72},{..., dimensions={0}, use_global_device_ids=true | all-gather | bytes 49152 | tf_op jit(solution)/shard_map/all_gather | solution.py:403
  30.3 0.0 collective-permute-done.5.even
  30.3 1.0 %shard_map.98 = (f32[2,64,256]{2,1,0:T(8,128)}, f32[32,128]{1,0:T(8,128)}) custom-call(f32[8,32,128]{2,1,0:T(8,128)S(1)} %get-tuple-element.22.grad, f32[32,128]{1,0:T(8,128)S(1)} %get-tuple-element.23.columns, f32[8,32,128]{2,1,0:T(8,128)S(1)} %get-tuple-element.24.fields, f32[27,8,512]{2,1,0:T(8,128)S(1)} %copy-done, ...), custom_call_target="tpu_custom_call" | custom-call | flops 4000000 | bytes 950272 | tf_op jit(solution)/shard_map/pallas_call | solution.py:359
Async XLA Ops:
  0.6 6.7 %copy-start = (f32[27,8,512]{2,1,0:T(8,128)S(1)}, f32[27,8,512]{2,1,0:T(8,128)}, u32[]{:S(2)}) copy-start(f32[27,8,512]{2,1,0:T(8,128)} %kernels.5) | copy-start | bytes 1327108
  0.6 6.7 %collective-permute-start.1 = (f32[32,128]{1,0:T(8,128)}, f32[32,128]{1,0:T(8,128)S(1)}, u32[]{:S(2)}, u32[]{:S(2)}) collective-permute-start(f32[32,128]{1,0:T(8,128)} %bitcast.7), channel_id=1, source_target_pairs={{0,4},{4,0},{8,12},{12,8},{16,20},{20,16},{24,28},{28,24},{32,36},... | collective-permute-start | bytes 49160 | tf_op jit(solution)/shard_map/ppermute | solution.py:378
  4.5 2.8 %collective-permute-start = (f32[32,128]{1,0:T(8,128)}, f32[32,128]{1,0:T(8,128)S(1)}, u32[]{:S(2)}, u32[]{:S(2)}) collective-permute-start(f32[32,128]{1,0:T(8,128)} %bitcast.8), channel_id=1, source_target_pairs={{4,8},{8,4},{12,16},{16,12},{20,24},{24,20},{28,32},{32,28},{36,40... | collective-permute-start | bytes 49160 | tf_op jit(solution)/shard_map/ppermute | solution.py:377
  5.2 2.2 %copy-start.1 = (f32[1,1,32,128]{3,2,1,0:T(8,128)S(1)}, f32[1,1,32,128]{3,2,1,0:T(8,128)}, u32[]{:S(2)}) copy-start(f32[1,1,32,128]{3,2,1,0:T(8,128)} %param.8) | copy-start | bytes 49156
  8.0 4.3 %collective-permute-start.4 = (f32[32,128]{1,0:T(8,128)S(1)}, f32[32,128]{1,0:T(8,128)S(1)}, u32[]{:S(2)}, u32[]{:S(2)}) collective-permute-start(f32[32,128]{1,0:T(8,128)S(1)} %get-tuple-element.19.own), channel_id=1, source_target_pairs={{0,3},{1,2},{2,1},{3,0},{4,7},{5,6},{6,5},{7,4},{8,11},{9,10},{10,... | collective-permute-start | bytes 49160 | tf_op jit(solution)/shard_map/ppermute | solution.py:396
  10.6 3.0 %collective-permute-start.3 = (f32[32,128]{1,0:T(8,128)S(1)}, f32[32,128]{1,0:T(8,128)S(1)}, u32[]{:S(2)}, u32[]{:S(2)}) collective-permute-start(f32[32,128]{1,0:T(8,128)S(1)} %get-tuple-element.19.own), channel_id=1, source_target_pairs={{0,2},{1,3},{2,0},{3,1},{4,6},{5,7},{6,4},{7,5},{8,10},{9,11},{10,... | collective-permute-start | bytes 49160 | tf_op jit(solution)/shard_map/ppermute | solution.py:396
  11.0 2.6 %collective-permute-start.2 = (f32[32,128]{1,0:T(8,128)S(1)}, f32[32,128]{1,0:T(8,128)S(1)}, u32[]{:S(2)}, u32[]{:S(2)}) collective-permute-start(f32[32,128]{1,0:T(8,128)S(1)} %get-tuple-element.19.own), channel_id=1, source_target_pairs={{0,1},{1,0},{2,3},{3,2},{4,5},{5,4},{6,7},{7,6},{8,9},{9,8},{10,11... | collective-permute-start | bytes 49160 | tf_op jit(solution)/shard_map/ppermute | solution.py:396
  14.4 15.9 %collective-permute-start.5 = (f32[32,128]{1,0:T(8,128)S(1)}, f32[32,128]{1,0:T(8,128)S(1)}, u32[]{:S(2)}, u32[]{:S(2)}) collective-permute-start(f32[32,128]{1,0:T(8,128)S(1)} %get-tuple-element.26), channel_id=1, source_target_pairs={{0,4},{4,0},{8,12},{12,8},{16,20},{20,16},{24,28},{28,24},{32,36},... | collective-permute-start | bytes 49160 | tf_op jit(solution)/shard_map/ppermute | solution.py:401

commit v4 on v3

--- a/solution.py
+++ b/solution.py
@@ -229,13 +229,26 @@
     return total
 
 
-def backward(own, by1, by2, by3, dens, prod, kernels, stars, grad, edges_out, odd_out, even_out):
+def middle(prod, stars, kernels, share, weights):
+    pairs = jnp.concatenate([prod[2 * p] + prod[2 * p + 1] for p in range(4)], axis=0)
+    beyond = (rows((128, 128)) > lanes((128, 128))).astype(F32)
+    after = jnp.dot(pairs, beyond, precision=HI, preferred_element_type=F32)
+    for p in range(4):
+        second = after[32 * p : 32 * p + 32] + prod[2 * p + 1]
+        first = second + prod[2 * p]
+        for k, value in ((0, first), (1, second)):
+            share[2 * p + k] = value - stars[4 + k, pixels(p), :]
+    for s in range(4):
+        for n in range(9):
+            for side in range(2):
+                block = kernels[3 * n + 2 * side, :, 128 * s : 128 * s + 128]
+                weights[s, side, n] = jnp.broadcast_to(block[:, 127 * side : 127 * side + 1], (8, 128))
+
+
+def backward(own, by1, by2, by3, dens, share, weights, kernels, stars, grad, edges_out, odd_out, even_out):
     shard = lax.axis_index("rad")
     step = 1.0 / 1024
     even = (rows((8, 128)) & 1) == 0
-    pairs = jnp.concatenate([prod[2 * p] + prod[2 * p + 1] for p in range(4)], axis=0)
-    beyond = (rows((128, 128)) > lanes((128, 128))).astype(F32)
-    after = jnp.dot(pairs, beyond, precision=HI, preferred_element_type=F32)
     held = [own[...], by1[...], by2[...], by3[...]]
     groups = []
     for s in range(4):
@@ -254,11 +267,9 @@
         for u in range(3):
             for v in range(3):
                 if s > 0:
-                    weight = kernels[9 * u + 3 * v, :, 128 * s : 128 * s + 128][:, 0:1]
-                    f_low = f_low + weight * edges[s - 1][v][3 + u : 4 + u, :]
+                    f_low = f_low + weights[s, 0, 3 * u + v] * edges[s - 1][v][3 + u : 4 + u, :]
                 if s < 3:
-                    weight = kernels[9 * u + 3 * v + 2, :, 128 * s : 128 * s + 128][:, 127:128]
-                    f_high = f_high + weight * edges[s + 1][v][u : u + 1, :]
+                    f_high = f_high + weights[s, 1, 3 * u + v] * edges[s + 1][v][u : u + 1, :]
         a, b = jnp.exp(f_low), jnp.exp(f_high)
         d_low.append(a)
         d_high.append(b)
@@ -311,11 +322,9 @@
     grads = []
     for p in range(4):
         near, far = columns[:, 16 + 2 * p : 17 + 2 * p], columns[:, 24 + 2 * p : 25 + 2 * p]
-        second = after[32 * p : 32 * p + 32] + prod[2 * p + 1]
-        first = second + prod[2 * p]
-        for k, share in ((0, first), (1, second)):
+        for k in range(2):
             q = 2 * p + k
-            suffix = far + weighed(near, stars[2 + k, pixels(p), :]) + (share - stars[4 + k, pixels(p), :])
+            suffix = far + weighed(near, stars[2 + k, pixels(p), :]) + share[q]
             g = step * dens[q] * suffix
             g = jnp.where(lane == 0, columns[:, q : q + 1], g)
             g = jnp.where(lane == 127, columns[:, 8 + q : 9 + q], g)
@@ -394,13 +403,18 @@
         (block, block, row), 6_000_000,
     )
     others = [lax.ppermute(table, "rad", [(i, i ^ k) for i in range(4)]) for k in (1, 2, 3)]
+    share, weights = call(
+        middle, (prod, stars, kernels), (block, ((4, 2, 9, 8, 128), F32)), 1_000_000,
+    )
     grad, columns, odd, even = call(
-        backward, (table, *others, dens, prod, kernels, stars),
+        backward, (table, *others, dens, share, weights, kernels, stars),
         (block, row, row, row), 8_000_000,
     )
     even = lax.ppermute(even, "ang", pairs[0])
-    groups = [[i, (i + 1) % count] for i in range(1, count, 2)]
-    odd = lax.all_gather(odd, "ang", axis_index_groups=groups, tiled=True)
+    near = lax.axis_size("rad")
+    groups = [[i * near + r, (i + 1) * near + r] for i in range(1, count - 1, 2) for r in range(near)]
+    groups += [[i * near + r, i * near + r + 1] for i in (0, count - 1) for r in range(0, near, 2)]
+    odd = lax.all_gather(odd, ("ang", "rad"), axis_index_groups=groups, tiled=True)
     grad_excite, grad_coarse = call(
         finish, (grad, columns, fields, kernels, mixing_here, even, odd),
         (((2, 64, 256), F32), row), 4_000_000,

time: 31.5 us -> 31.3 us (level)
  the two profiles are of different devices: /device:TPU:1 before, /device:TPU:6 now
where the time goes in v4:
time: 31.3 us; the launch traced here: 31.1 us
  starting transfers between devices  14.5 us (46%)
  blocking collectives  9.53 us (30%)
  Pallas kernels  4.61 us (15%)
  waiting for transfers between devices  1.78 us (6%)
  between operations  0.74 us (2%)
    all_gather x1, blocking collectives, per_device(): lax.all_gather(odd, ('ang', 'rad'), axis_index_groups=groups, tiled=True)  9.53 us
    ppermute x1, starting transfers between devices, per_device(): odd = lax.ppermute(own, 'ang', pairs[1])  9.09 us
    pallas_call x5, Pallas kernels, call(): pl.pallas_call(body, out_shape=shapes, in_specs=[pl.BlockSpec(memory_spac...  4.61 us
    ppermute x1, starting transfers between devices, per_device(): even = lax.ppermute(own, 'ang', pairs[0])  3.36 us
    ppermute x3, starting transfers between devices, per_device(): lax.ppermute(table, 'rad', [(i, i ^ k) for i in range(4)])  1.94 us
    ppermute x3, waiting for transfers between devices, per_device(): lax.ppermute(table, 'rad', [(i, i ^ k) for i in range(4)])  1.77 us
  transfers between devices with their start and end apart: 6, of which 2 were waited for; matrix products, arithmetic and copies ran while one was open for 0% of the time, Pallas kernels for 8%

profile of v4, /device:TPU:6, one launch (start us, length us, event | category | flops | bytes accessed | tf_op | source)
XLA Modules:
  0.0 31.1 jit_solution(1431475005442726795)
XLA Ops:
  0.6 0.0 copy-start
  0.6 3.4 %collective-permute-start.1 = (f32[32,128]{1,0:T(8,128)}, f32[32,128]{1,0:T(8,128)S(1)}, u32[]{:S(2)}, u32[]{:S(2)}) collective-permute-start(f32[32,128]{1,0:T(8,128)} %bitcast.7), channel_id=1, source_target_pairs={{0,4},{4,0},{8,12},{12,8},{16,20},{20,16},{24,28},{28,24},{32,36},... | collective-permute-start | bytes 49160 | tf_op jit(solution)/shard_map/ppermute | solution.py:387
  4.0 9.1 %collective-permute-start = (f32[32,128]{1,0:T(8,128)}, f32[32,128]{1,0:T(8,128)S(1)}, u32[]{:S(2)}, u32[]{:S(2)}) collective-permute-start(f32[32,128]{1,0:T(8,128)} %bitcast.8), channel_id=1, source_target_pairs={{4,8},{8,4},{12,16},{16,12},{20,24},{24,20},{28,32},{32,28},{36,40... | collective-permute-start | bytes 49160 | tf_op jit(solution)/shard_map/ppermute | solution.py:386
  13.1 0.0 copy-start.1
  13.1 2.1 %shard_map.95 = (f32[8,32,128]{2,1,0:T(8,128)S(1)}, f32[8,32,128]{2,1,0:T(8,128)S(1)}, f32[6,128,128]{2,1,0:T(8,128)S(1)}, f32[32,128]{1,0:T(8,128)S(1)}, f32[8,8,128]{2,1,0:T(8,128)S(1)}) custom-call(f32[32,128]{1,0:T(8,128)} %bitcast.9, f32[2,64,256]{2,1,0:T(8,128)} %bitcast.11, f32[27,8,512]{2,1,0:T(8,128)} %kernels.7, f32[8,8,512]{2,1,0:T(8,128)} %mixing_in.1, ...), custom_call_target="tpu_custom_call" | custom-call | flops 4000000 | bytes 1450496 | tf_op jit(solution)/shard_map/pallas_call | solution.py:368
  15.3 0.0 collective-permute-done.1.even
  15.3 0.0 collective-permute-done.odd
  15.3 0.0 copy-done
  15.3 0.0 copy-done.1
  15.3 0.6 %shard_map.96 = (f32[8,32,128]{2,1,0:T(8,128)S(1)}, f32[8,32,128]{2,1,0:T(8,128)S(1)}, f32[32,128]{1,0:T(8,128)S(1)}) custom-call(f32[32,128]{1,0:T(8,128)S(1)} %bitcast.10, f32[32,128]{1,0:T(8,128)S(1)} %collective-permute-done.odd, f32[32,128]{1,0:T(8,128)S(1)} %collective-permute-done.1.even, f32[8,32,128]{2,1,0:T(8,128)S(1)} %get-tuple-element.18.base, ...), custom_call_target="tpu_custom_call" | custom-call | flops 6000000 | bytes 1310720 | tf_op jit(solution)/shard_map/pallas_call | solution.py:368
  15.9 0.1 collective-permute-start.4
  16.0 1.7 %collective-permute-start.3 = (f32[32,128]{1,0:T(8,128)S(1)}, f32[32,128]{1,0:T(8,128)S(1)}, u32[]{:S(2)}, u32[]{:S(2)}) collective-permute-start(f32[32,128]{1,0:T(8,128)S(1)} %get-tuple-element.21.own), channel_id=1, source_target_pairs={{0,2},{1,3},{2,0},{3,1},{4,6},{5,7},{6,4},{7,5},{8,10},{9,11},{10,... | collective-permute-start | bytes 49160 | tf_op jit(solution)/shard_map/ppermute | solution.py:405
  17.7 0.2 collective-permute-start.2
  17.9 0.2 shard_map.97
  18.1 1.1 %collective-permute-done.4.by3 = f32[32,128]{1,0:T(8,128)S(1)} collective-permute-done((f32[32,128]{1,0:T(8,128)S(1)}, f32[32,128]{1,0:T(8,128)S(1)}, u32[]{:S(2)}, u32[]{:S(2)}) %collective-permute-start.4) | collective-permute-done | bytes 16416 | tf_op jit(solution)/shard_map/ppermute | solution.py:405
  19.2 0.7 %collective-permute-done.3.by2 = f32[32,128]{1,0:T(8,128)S(1)} collective-permute-done((f32[32,128]{1,0:T(8,128)S(1)}, f32[32,128]{1,0:T(8,128)S(1)}, u32[]{:S(2)}, u32[]{:S(2)}) %collective-permute-start.3) | collective-permute-done | bytes 16416 | tf_op jit(solution)/shard_map/ppermute | solution.py:405
  19.8 0.0 collective-permute-done.2.by1
  19.8 0.7 %shard_map.98 = (f32[8,32,128]{2,1,0:T(8,128)S(1)}, f32[32,128]{1,0:T(8,128)S(1)}, f32[32,128]{1,0:T(8,128)S(1)}, f32[32,128]{1,0:T(8,128)S(1)}) custom-call(f32[32,128]{1,0:T(8,128)S(1)} %get-tuple-element.21.own, f32[32,128]{1,0:T(8,128)S(1)} %collective-permute-done.2.by1, f32[32,128]{1,0:T(8,128)S(1)} %collective-permute-done.3.by2, ...), custom_call_target="tpu_custom_call" | custom-call | flops 8000000 | bytes 1638400 | tf_op jit(solution)/shard_map/pallas_call | solution.py:368
  20.5 0.1 collective-permute-start.5
  20.6 9.5 %all_gather.3.odd = f32[64,128]{1,0:T(8,128)S(1)} all-gather(f32[32,128]{1,0:T(8,128)S(1)} %get-tuple-element.31), channel_id=1, replica_groups={{4,8},{5,9},{6,10},{7,11},{12,16},{13,17},{14,18},{15,19},{20,24},{21,2..., dimensions={0}, use_global_device_ids=true | all-gather | bytes 49152 | tf_op jit(solution)/shard_map/all_gather | solution.py:417
  30.2 0.0 collective-permute-done.5.even
  30.2 1.0 %shard_map.99 = (f32[2,64,256]{2,1,0:T(8,128)}, f32[32,128]{1,0:T(8,128)}) custom-call(f32[8,32,128]{2,1,0:T(8,128)S(1)} %get-tuple-element.26.grad, f32[32,128]{1,0:T(8,128)S(1)} %get-tuple-element.27.columns, f32[8,32,128]{2,1,0:T(8,128)S(1)} %get-tuple-element.28.fields, f32[27,8,512]{2,1,0:T(8,128)S(1)} %copy-done, ...), custom_call_target="tpu_custom_call" | custom-call | flops 4000000 | bytes 950272 | tf_op jit(solution)/shard_map/pallas_call | solution.py:368
Async XLA Ops:
  0.6 14.6 %copy-start = (f32[27,8,512]{2,1,0:T(8,128)S(1)}, f32[27,8,512]{2,1,0:T(8,128)}, u32[]{:S(2)}) copy-start(f32[27,8,512]{2,1,0:T(8,128)} %kernels.7) | copy-start | bytes 1327108
  0.6 14.6 %collective-permute-start.1 = (f32[32,128]{1,0:T(8,128)}, f32[32,128]{1,0:T(8,128)S(1)}, u32[]{:S(2)}, u32[]{:S(2)}) collective-permute-start(f32[32,128]{1,0:T(8,128)} %bitcast.7), channel_id=1, source_target_pairs={{0,4},{4,0},{8,12},{12,8},{16,20},{20,16},{24,28},{28,24},{32,36},... | collective-permute-start | bytes 49160 | tf_op jit(solution)/shard_map/ppermute | solution.py:387
  4.0 11.3 %collective-permute-start = (f32[32,128]{1,0:T(8,128)}, f32[32,128]{1,0:T(8,128)S(1)}, u32[]{:S(2)}, u32[]{:S(2)}) collective-permute-start(f32[32,128]{1,0:T(8,128)} %bitcast.8), channel_id=1, source_target_pairs={{4,8},{8,4},{12,16},{16,12},{20,24},{24,20},{28,32},{32,28},{36,40... | collective-permute-start | bytes 49160 | tf_op jit(solution)/shard_map/ppermute | solution.py:386
  13.1 2.2 %copy-start.1 = (f32[1,1,32,128]{3,2,1,0:T(8,128)S(1)}, f32[1,1,32,128]{3,2,1,0:T(8,128)}, u32[]{:S(2)}) copy-start(f32[1,1,32,128]{3,2,1,0:T(8,128)} %param.8) | copy-start | bytes 49156
  15.9 3.3 %collective-permute-start.4 = (f32[32,128]{1,0:T(8,128)S(1)}, f32[32,128]{1,0:T(8,128)S(1)}, u32[]{:S(2)}, u32[]{:S(2)}) collective-permute-start(f32[32,128]{1,0:T(8,128)S(1)} %get-tuple-element.21.own), channel_id=1, source_target_pairs={{0,3},{1,2},{2,1},{3,0},{4,7},{5,6},{6,5},{7,4},{8,11},{9,10},{10,... | collective-permute-start | bytes 49160 | tf_op jit(solution)/shard_map/ppermute | solution.py:405
  16.0 3.8 %collective-permute-start.3 = (f32[32,128]{1,0:T(8,128)S(1)}, f32[32,128]{1,0:T(8,128)S(1)}, u32[]{:S(2)}, u32[]{:S(2)}) collective-permute-start(f32[32,128]{1,0:T(8,128)S(1)} %get-tuple-element.21.own), channel_id=1, source_target_pairs={{0,2},{1,3},{2,0},{3,1},{4,6},{5,7},{6,4},{7,5},{8,10},{9,11},{10,... | collective-permute-start | bytes 49160 | tf_op jit(solution)/shard_map/ppermute | solution.py:405
  17.7 2.1 %collective-permute-start.2 = (f32[32,128]{1,0:T(8,128)S(1)}, f32[32,128]{1,0:T(8,128)S(1)}, u32[]{:S(2)}, u32[]{:S(2)}) collective-permute-start(f32[32,128]{1,0:T(8,128)S(1)} %get-tuple-element.21.own), channel_id=1, source_target_pairs={{0,1},{1,0},{2,3},{3,2},{4,5},{5,4},{6,7},{7,6},{8,9},{9,8},{10,11... | collective-permute-start | bytes 49160 | tf_op jit(solution)/shard_map/ppermute | solution.py:405
  20.5 9.6 %collective-permute-start.5 = (f32[32,128]{1,0:T(8,128)S(1)}, f32[32,128]{1,0:T(8,128)S(1)}, u32[]{:S(2)}, u32[]{:S(2)}) collective-permute-start(f32[32,128]{1,0:T(8,128)S(1)} %get-tuple-element.30), channel_id=1, source_target_pairs={{0,4},{4,0},{8,12},{12,8},{16,20},{20,16},{24,28},{28,24},{32,36},... | collective-permute-start | bytes 49160 | tf_op jit(solution)/shard_map/ppermute | solution.py:413

commit v5 on v4

--- a/solution.py
+++ b/solution.py
@@ -149,7 +149,9 @@
     shard = lax.axis_index("rad")
     step = 1.0 / 1024
     acc = [base[q] for q in range(8)]
-    low, high = sides(odd[...], even[...])
+    place = lax.axis_index("ang")
+    met = (place > 0) & (place < lax.axis_size("ang") - 1)
+    low, high = sides(jnp.where(met, odd[...], 0.0), even[...])
     here = pl.ds(pl.multiple_of(shard * 128, 128), 128)
     taps(acc, low, [kernels[t, :, here] for t in range(9)])
     taps(acc, high, [kernels[t, :, here] for t in range(18, 27)])
@@ -383,7 +385,10 @@
         pairs[i % 2] += [(i, i + 1), (i + 1, i)]
 
     own = coarse[0, 0]
-    odd = lax.ppermute(own, "ang", pairs[1])
+    near = lax.axis_size("rad")
+    hops = [(a * near + r, b * near + r) for a, b in pairs[1] for r in range(near)]
+    hops += [(a * near + r, a * near + (r ^ 1)) for a in (0, count - 1) for r in range(near)]
+    odd = lax.ppermute(own, ("ang", "rad"), hops)
     even = lax.ppermute(own, "ang", pairs[0])
     block = ((8, 32, 128), F32)
     row = ((32, 128), F32)

time: 31.3 us -> 29.4 us (0.939)
  starting transfers between devices: 14.5 us -> 12.6 us
    ppermute x1, starting transfers between devices: 9.09 us -> 7.2 us  [per_device(): odd = lax.ppermute(own, ('ang', 'rad'), hops)]
where the time goes in v5:
time: 29.4 us; the launch traced here: 29.2 us
  starting transfers between devices  12.6 us (43%)
  blocking collectives  9.53 us (32%)
  Pallas kernels  4.61 us (16%)
  waiting for transfers between devices  1.78 us (6%)
  between operations  0.72 us (2%)
    all_gather x1, blocking collectives, per_device(): lax.all_gather(odd, ('ang', 'rad'), axis_index_groups=groups, tiled=True)  9.53 us
    ppermute x1, starting transfers between devices, per_device(): odd = lax.ppermute(own, ('ang', 'rad'), hops)  7.2 us
    pallas_call x5, Pallas kernels, call(): pl.pallas_call(body, out_shape=shapes, in_specs=[pl.BlockSpec(memory_spac...  4.61 us
    ppermute x1, starting transfers between devices, per_device(): even = lax.ppermute(own, 'ang', pairs[0])  3.36 us
    ppermute x3, starting transfers between devices, per_device(): lax.ppermute(table, 'rad', [(i, i ^ k) for i in range(4)])  1.94 us
    ppermute x3, waiting for transfers between devices, per_device(): lax.ppermute(table, 'rad', [(i, i ^ k) for i in range(4)])  1.77 us
  transfers between devices with their start and end apart: 6, of which 2 were waited for; matrix products, arithmetic and copies ran while one was open for 0% of the time, Pallas kernels for 8%

profile of v5, /device:TPU:6, one launch (start us, length us, event | category | flops | bytes accessed | tf_op | source)
XLA Modules:
  0.0 29.2 jit_solution(9447049982313737286)
XLA Ops:
  0.6 0.0 copy-start
  0.6 3.4 %collective-permute-start.1 = (f32[32,128]{1,0:T(8,128)}, f32[32,128]{1,0:T(8,128)S(1)}, u32[]{:S(2)}, u32[]{:S(2)}) collective-permute-start(f32[32,128]{1,0:T(8,128)} %bitcast.7), channel_id=1, source_target_pairs={{0,4},{4,0},{8,12},{12,8},{16,20},{20,16},{24,28},{28,24},{32,36},... | collective-permute-start | bytes 49160 | tf_op jit(solution)/shard_map/ppermute | solution.py:392
  4.0 7.2 %collective-permute-start = (f32[32,128]{1,0:T(8,128)}, f32[32,128]{1,0:T(8,128)S(1)}, u32[]{:S(2)}, u32[]{:S(2)}) collective-permute-start(f32[32,128]{1,0:T(8,128)} %bitcast.8), channel_id=1, source_target_pairs={{4,8},{5,9},{6,10},{7,11},{8,4},{9,5},{10,6},{11,7},{12,16},{13,17... | collective-permute-start | bytes 49160 | tf_op jit(solution)/shard_map/ppermute | solution.py:391
  11.2 0.0 copy-start.1
  11.2 2.1 %shard_map.95 = (f32[8,32,128]{2,1,0:T(8,128)S(1)}, f32[8,32,128]{2,1,0:T(8,128)S(1)}, f32[6,128,128]{2,1,0:T(8,128)S(1)}, f32[32,128]{1,0:T(8,128)S(1)}, f32[8,8,128]{2,1,0:T(8,128)S(1)}) custom-call(f32[32,128]{1,0:T(8,128)} %bitcast.9, f32[2,64,256]{2,1,0:T(8,128)} %bitcast.11, f32[27,8,512]{2,1,0:T(8,128)} %kernels.7, f32[8,8,512]{2,1,0:T(8,128)} %mixing_in.1, ...), custom_call_target="tpu_custom_call" | custom-call | flops 4000000 | bytes 1450496 | tf_op jit(solution)/shard_map/pallas_call | solution.py:370
  13.3 0.0 collective-permute-done.1.even
  13.4 0.0 collective-permute-done.odd
  13.4 0.0 copy-done
  13.4 0.0 copy-done.1
  13.4 0.6 %shard_map.96 = (f32[8,32,128]{2,1,0:T(8,128)S(1)}, f32[8,32,128]{2,1,0:T(8,128)S(1)}, f32[32,128]{1,0:T(8,128)S(1)}) custom-call(f32[32,128]{1,0:T(8,128)S(1)} %bitcast.10, f32[32,128]{1,0:T(8,128)S(1)} %collective-permute-done.odd, f32[32,128]{1,0:T(8,128)S(1)} %collective-permute-done.1.even, f32[8,32,128]{2,1,0:T(8,128)S(1)} %get-tuple-element.18.base, ...), custom_call_target="tpu_custom_call" | custom-call | flops 6000000 | bytes 1310720 | tf_op jit(solution)/shard_map/pallas_call | solution.py:370
  14.0 0.1 collective-permute-start.4
  14.1 1.7 %collective-permute-start.3 = (f32[32,128]{1,0:T(8,128)S(1)}, f32[32,128]{1,0:T(8,128)S(1)}, u32[]{:S(2)}, u32[]{:S(2)}) collective-permute-start(f32[32,128]{1,0:T(8,128)S(1)} %get-tuple-element.21.own), channel_id=1, source_target_pairs={{0,2},{1,3},{2,0},{3,1},{4,6},{5,7},{6,4},{7,5},{8,10},{9,11},{10,... | collective-permute-start | bytes 49160 | tf_op jit(solution)/shard_map/ppermute | solution.py:410
  15.8 0.1 collective-permute-start.2
  15.9 0.2 shard_map.97
  16.2 1.1 %collective-permute-done.4.by3 = f32[32,128]{1,0:T(8,128)S(1)} collective-permute-done((f32[32,128]{1,0:T(8,128)S(1)}, f32[32,128]{1,0:T(8,128)S(1)}, u32[]{:S(2)}, u32[]{:S(2)}) %collective-permute-start.4) | collective-permute-done | bytes 16416 | tf_op jit(solution)/shard_map/ppermute | solution.py:410
  17.3 0.7 %collective-permute-done.3.by2 = f32[32,128]{1,0:T(8,128)S(1)} collective-permute-done((f32[32,128]{1,0:T(8,128)S(1)}, f32[32,128]{1,0:T(8,128)S(1)}, u32[]{:S(2)}, u32[]{:S(2)}) %collective-permute-start.3) | collective-permute-done | bytes 16416 | tf_op jit(solution)/shard_map/ppermute | solution.py:410
  17.9 0.0 collective-permute-done.2.by1
  17.9 0.7 %shard_map.98 = (f32[8,32,128]{2,1,0:T(8,128)S(1)}, f32[32,128]{1,0:T(8,128)S(1)}, f32[32,128]{1,0:T(8,128)S(1)}, f32[32,128]{1,0:T(8,128)S(1)}) custom-call(f32[32,128]{1,0:T(8,128)S(1)} %get-tuple-element.21.own, f32[32,128]{1,0:T(8,128)S(1)} %collective-permute-done.2.by1, f32[32,128]{1,0:T(8,128)S(1)} %collective-permute-done.3.by2, ...), custom_call_target="tpu_custom_call" | custom-call | flops 8000000 | bytes 1638400 | tf_op jit(solution)/shard_map/pallas_call | solution.py:370
  18.6 0.1 collective-permute-start.5
  18.7 9.5 %all_gather.3.odd = f32[64,128]{1,0:T(8,128)S(1)} all-gather(f32[32,128]{1,0:T(8,128)S(1)} %get-tuple-element.31), channel_id=1, replica_groups={{4,8},{5,9},{6,10},{7,11},{12,16},{13,17},{14,18},{15,19},{20,24},{21,2..., dimensions={0}, use_global_device_ids=true | all-gather | bytes 49152 | tf_op jit(solution)/shard_map/all_gather | solution.py:422
  28.2 0.0 collective-permute-done.5.even
  28.3 1.0 %shard_map.99 = (f32[2,64,256]{2,1,0:T(8,128)}, f32[32,128]{1,0:T(8,128)}) custom-call(f32[8,32,128]{2,1,0:T(8,128)S(1)} %get-tuple-element.26.grad, f32[32,128]{1,0:T(8,128)S(1)} %get-tuple-element.27.columns, f32[8,32,128]{2,1,0:T(8,128)S(1)} %get-tuple-element.28.fields, f32[27,8,512]{2,1,0:T(8,128)S(1)} %copy-done, ...), custom_call_target="tpu_custom_call" | custom-call | flops 4000000 | bytes 950272 | tf_op jit(solution)/shard_map/pallas_call | solution.py:370
Async XLA Ops:
  0.6 12.7 %copy-start = (f32[27,8,512]{2,1,0:T(8,128)S(1)}, f32[27,8,512]{2,1,0:T(8,128)}, u32[]{:S(2)}) copy-start(f32[27,8,512]{2,1,0:T(8,128)} %kernels.7) | copy-start | bytes 1327108
  0.6 12.7 %collective-permute-start.1 = (f32[32,128]{1,0:T(8,128)}, f32[32,128]{1,0:T(8,128)S(1)}, u32[]{:S(2)}, u32[]{:S(2)}) collective-permute-start(f32[32,128]{1,0:T(8,128)} %bitcast.7), channel_id=1, source_target_pairs={{0,4},{4,0},{8,12},{12,8},{16,20},{20,16},{24,28},{28,24},{32,36},... | collective-permute-start | bytes 49160 | tf_op jit(solution)/shard_map/ppermute | solution.py:392
  4.0 9.4 %collective-permute-start = (f32[32,128]{1,0:T(8,128)}, f32[32,128]{1,0:T(8,128)S(1)}, u32[]{:S(2)}, u32[]{:S(2)}) collective-permute-start(f32[32,128]{1,0:T(8,128)} %bitcast.8), channel_id=1, source_target_pairs={{4,8},{5,9},{6,10},{7,11},{8,4},{9,5},{10,6},{11,7},{12,16},{13,17... | collective-permute-start | bytes 49160 | tf_op jit(solution)/shard_map/ppermute | solution.py:391
  11.2 2.2 %copy-start.1 = (f32[1,1,32,128]{3,2,1,0:T(8,128)S(1)}, f32[1,1,32,128]{3,2,1,0:T(8,128)}, u32[]{:S(2)}) copy-start(f32[1,1,32,128]{3,2,1,0:T(8,128)} %param.8) | copy-start | bytes 49156
  14.0 3.3 %collective-permute-start.4 = (f32[32,128]{1,0:T(8,128)S(1)}, f32[32,128]{1,0:T(8,128)S(1)}, u32[]{:S(2)}, u32[]{:S(2)}) collective-permute-start(f32[32,128]{1,0:T(8,128)S(1)} %get-tuple-element.21.own), channel_id=1, source_target_pairs={{0,3},{1,2},{2,1},{3,0},{4,7},{5,6},{6,5},{7,4},{8,11},{9,10},{10,... | collective-permute-start | bytes 49160 | tf_op jit(solution)/shard_map/ppermute | solution.py:410
  14.1 3.8 %collective-permute-start.3 = (f32[32,128]{1,0:T(8,128)S(1)}, f32[32,128]{1,0:T(8,128)S(1)}, u32[]{:S(2)}, u32[]{:S(2)}) collective-permute-start(f32[32,128]{1,0:T(8,128)S(1)} %get-tuple-element.21.own), channel_id=1, source_target_pairs={{0,2},{1,3},{2,0},{3,1},{4,6},{5,7},{6,4},{7,5},{8,10},{9,11},{10,... | collective-permute-start | bytes 49160 | tf_op jit(solution)/shard_map/ppermute | solution.py:410
  15.8 2.1 %collective-permute-start.2 = (f32[32,128]{1,0:T(8,128)S(1)}, f32[32,128]{1,0:T(8,128)S(1)}, u32[]{:S(2)}, u32[]{:S(2)}) collective-permute-start(f32[32,128]{1,0:T(8,128)S(1)} %get-tuple-element.21.own), channel_id=1, source_target_pairs={{0,1},{1,0},{2,3},{3,2},{4,5},{5,4},{6,7},{7,6},{8,9},{9,8},{10,11... | collective-permute-start | bytes 49160 | tf_op jit(solution)/shard_map/ppermute | solution.py:410
  18.6 9.6 %collective-permute-start.5 = (f32[32,128]{1,0:T(8,128)S(1)}, f32[32,128]{1,0:T(8,128)S(1)}, u32[]{:S(2)}, u32[]{:S(2)}) collective-permute-start(f32[32,128]{1,0:T(8,128)S(1)} %get-tuple-element.30), channel_id=1, source_target_pairs={{0,4},{4,0},{8,12},{12,8},{16,20},{20,16},{24,28},{28,24},{32,36},... | collective-permute-start | bytes 49160 | tf_op jit(solution)/shard_map/ppermute | solution.py:418

commit v6 on v5

--- a/solution.py
+++ b/solution.py
@@ -338,7 +338,7 @@
     even_out[...] = even_row
 
 
-def finish(grad, columns, fields, kernels, mixing, even, odd, out, own, halves):
+def finish(grad, columns, fields, kernels, mixing, out, own, halves):
     shard = lax.axis_index("rad")
     lane = lanes((32, 128))
     grads = [grad[q] for q in range(8)]
@@ -357,11 +357,13 @@
                 halves[side, half, :] = value
         for side in range(2):
             out[i, :, 128 * side : 128 * side + 128] = halves[side]
+    own[...] = to_row(1, spread(grads, columns[...]), kernels, shard)
+
+
+def total(own, even, odd, out):
     place = lax.axis_index("ang")
-    other = jnp.where((place & 1) == 0, odd[0:32], odd[32:64])
     met = (place > 0) & (place < lax.axis_size("ang") - 1)
-    total = to_row(1, spread(grads, columns[...]), kernels, shard) + even[...]
-    own[...] = total + jnp.where(met, other, 0.0)
+    out[...] = own[...] + even[...] + jnp.where(met, odd[...], 0.0)
 
 
 def call(body, ins, outs, flops, scratch=(), space=pltpu.VMEM):
@@ -384,10 +386,10 @@
     for i in range(count - 1):
         pairs[i % 2] += [(i, i + 1), (i + 1, i)]
 
-    own = coarse[0, 0]
     near = lax.axis_size("rad")
     hops = [(a * near + r, b * near + r) for a, b in pairs[1] for r in range(near)]
     hops += [(a * near + r, a * near + (r ^ 1)) for a in (0, count - 1) for r in range(near)]
+    own = coarse[0, 0]
     odd = lax.ppermute(own, ("ang", "rad"), hops)
     even = lax.ppermute(own, "ang", pairs[0])
     block = ((8, 32, 128), F32)
@@ -416,15 +418,13 @@
         (block, row, row, row), 8_000_000,
     )
     even = lax.ppermute(even, "ang", pairs[0])
-    near = lax.axis_size("rad")
-    groups = [[i * near + r, (i + 1) * near + r] for i in range(1, count - 1, 2) for r in range(near)]
-    groups += [[i * near + r, i * near + r + 1] for i in (0, count - 1) for r in range(0, near, 2)]
-    odd = lax.all_gather(odd, ("ang", "rad"), axis_index_groups=groups, tiled=True)
-    grad_excite, grad_coarse = call(
-        finish, (grad, columns, fields, kernels, mixing_here, even, odd),
+    odd = lax.ppermute(odd, ("ang", "rad"), hops)
+    grad_excite, here = call(
+        finish, (grad, columns, fields, kernels, mixing_here),
         (((2, 64, 256), F32), row), 4_000_000,
         [pltpu.VMEM((2, 64, 128), F32)],
     )
+    (grad_coarse,) = call(total, (here, even, odd), (row,), 10_000)
     return grad_excite[None], grad_coarse[None, None]
 
 

time: 29.4 us -> 28.4 us (0.966)
  blocking collectives: 9.53 us -> 0 us
  starting transfers between devices: 12.6 us -> 19.6 us
  waiting for transfers between devices: 1.78 us -> 2.79 us
  Pallas kernels: 4.61 us -> 5.12 us
    all_gather x1 -> x0, blocking collectives: 9.53 us -> none  [per_device(): lax.all_gather(odd, ('ang', 'rad'), axis_index_groups=groups, tiled=True)]
    ppermute x0 -> x1, starting transfers between devices: none -> 7.05 us  [per_device(): odd = lax.ppermute(odd, ('ang', 'rad'), hops)]
    ppermute x0 -> x1, waiting for transfers between devices: none -> 1.01 us  [per_device(): odd = lax.ppermute(odd, ('ang', 'rad'), hops)]
    pallas_call x5 -> x6, Pallas kernels: 4.61 us -> 5.12 us  [call(): pl.pallas_call(body, out_shape=shapes, in_specs=[pl.BlockSpec(memory_spac...]
  transfers between devices with their start and end apart: 6 -> 7, of which waited for: 2 -> 3; matrix products, arithmetic and copies ran while one was open for 0% -> 0% of each run, Pallas kernels for 8% -> 11%
where the time goes in v6:
time: 28.4 us; the launch traced here: 28.3 us
  starting transfers between devices  19.6 us (69%)
  Pallas kernels  5.12 us (18%)
  waiting for transfers between devices  2.79 us (10%)
  between operations  0.73 us (3%)
    ppermute x1, starting transfers between devices, per_device(): odd = lax.ppermute(own, ('ang', 'rad'), hops)  7.2 us
    ppermute x1, starting transfers between devices, per_device(): odd = lax.ppermute(odd, ('ang', 'rad'), hops)  7.05 us
    pallas_call x6, Pallas kernels, call(): pl.pallas_call(body, out_shape=shapes, in_specs=[pl.BlockSpec(memory_spac...  5.12 us
    ppermute x1, starting transfers between devices, per_device(): even = lax.ppermute(own, 'ang', pairs[0])  3.36 us
    ppermute x3, starting transfers between devices, per_device(): lax.ppermute(table, 'rad', [(i, i ^ k) for i in range(4)])  1.94 us
    ppermute x3, waiting for transfers between devices, per_device(): lax.ppermute(table, 'rad', [(i, i ^ k) for i in range(4)])  1.77 us
    ppermute x1, waiting for transfers between devices, per_device(): odd = lax.ppermute(odd, ('ang', 'rad'), hops)  1.01 us
  transfers between devices with their start and end apart: 7, of which 3 were waited for; matrix products, arithmetic and copies ran while one was open for 0% of the time, Pallas kernels for 11%

profile of v6, /device:TPU:6, one launch (start us, length us, event | category | flops | bytes accessed | tf_op | source)
XLA Modules:
  0.0 28.3 jit_solution(5307866175674573383)
XLA Ops:
  0.6 0.0 copy-start
  0.6 3.4 %collective-permute-start.1 = (f32[32,128]{1,0:T(8,128)}, f32[32,128]{1,0:T(8,128)S(1)}, u32[]{:S(2)}, u32[]{:S(2)}) collective-permute-start(f32[32,128]{1,0:T(8,128)} %bitcast.7), channel_id=1, source_target_pairs={{0,4},{4,0},{8,12},{12,8},{16,20},{20,16},{24,28},{28,24},{32,36},... | collective-permute-start | bytes 49160 | tf_op jit(solution)/shard_map/ppermute | solution.py:394
  4.0 7.2 %collective-permute-start = (f32[32,128]{1,0:T(8,128)}, f32[32,128]{1,0:T(8,128)S(1)}, u32[]{:S(2)}, u32[]{:S(2)}) collective-permute-start(f32[32,128]{1,0:T(8,128)} %bitcast.8), channel_id=1, source_target_pairs={{4,8},{5,9},{6,10},{7,11},{8,4},{9,5},{10,6},{11,7},{12,16},{13,17... | collective-permute-start | bytes 49160 | tf_op jit(solution)/shard_map/ppermute | solution.py:393
  11.2 0.0 copy-start.1
  11.2 2.1 %shard_map.95 = (f32[8,32,128]{2,1,0:T(8,128)S(1)}, f32[8,32,128]{2,1,0:T(8,128)S(1)}, f32[6,128,128]{2,1,0:T(8,128)S(1)}, f32[32,128]{1,0:T(8,128)S(1)}, f32[8,8,128]{2,1,0:T(8,128)S(1)}) custom-call(f32[32,128]{1,0:T(8,128)} %bitcast.9, f32[2,64,256]{2,1,0:T(8,128)} %bitcast.11, f32[27,8,512]{2,1,0:T(8,128)} %kernels.7, f32[8,8,512]{2,1,0:T(8,128)} %mixing_in.1, ...), custom_call_target="tpu_custom_call" | custom-call | flops 4000000 | bytes 1450496 | tf_op jit(solution)/shard_map/pallas_call | solution.py:372
  13.3 0.0 collective-permute-done.1.even
  13.4 0.0 collective-permute-done.odd
  13.4 0.0 copy-done
  13.4 0.0 copy-done.1
  13.4 0.6 %shard_map.96 = (f32[8,32,128]{2,1,0:T(8,128)S(1)}, f32[8,32,128]{2,1,0:T(8,128)S(1)}, f32[32,128]{1,0:T(8,128)S(1)}) custom-call(f32[32,128]{1,0:T(8,128)S(1)} %bitcast.10, f32[32,128]{1,0:T(8,128)S(1)} %collective-permute-done.odd, f32[32,128]{1,0:T(8,128)S(1)} %collective-permute-done.1.even, f32[8,32,128]{2,1,0:T(8,128)S(1)} %get-tuple-element.18.base, ...), custom_call_target="tpu_custom_call" | custom-call | flops 6000000 | bytes 1310720 | tf_op jit(solution)/shard_map/pallas_call | solution.py:372
  14.0 0.1 collective-permute-start.4
  14.1 1.7 %collective-permute-start.3 = (f32[32,128]{1,0:T(8,128)S(1)}, f32[32,128]{1,0:T(8,128)S(1)}, u32[]{:S(2)}, u32[]{:S(2)}) collective-permute-start(f32[32,128]{1,0:T(8,128)S(1)} %get-tuple-element.21.own), channel_id=1, source_target_pairs={{0,2},{1,3},{2,0},{3,1},{4,6},{5,7},{6,4},{7,5},{8,10},{9,11},{10,... | collective-permute-start | bytes 49160 | tf_op jit(solution)/shard_map/ppermute | solution.py:412
  15.8 0.1 collective-permute-start.2
  15.9 0.2 shard_map.97
  16.2 1.1 %collective-permute-done.4.by3 = f32[32,128]{1,0:T(8,128)S(1)} collective-permute-done((f32[32,128]{1,0:T(8,128)S(1)}, f32[32,128]{1,0:T(8,128)S(1)}, u32[]{:S(2)}, u32[]{:S(2)}) %collective-permute-start.4) | collective-permute-done | bytes 16416 | tf_op jit(solution)/shard_map/ppermute | solution.py:412
  17.3 0.7 %collective-permute-done.3.by2 = f32[32,128]{1,0:T(8,128)S(1)} collective-permute-done((f32[32,128]{1,0:T(8,128)S(1)}, f32[32,128]{1,0:T(8,128)S(1)}, u32[]{:S(2)}, u32[]{:S(2)}) %collective-permute-start.3) | collective-permute-done | bytes 16416 | tf_op jit(solution)/shard_map/ppermute | solution.py:412
  17.9 0.0 collective-permute-done.2.by1
  17.9 0.7 %shard_map.98 = (f32[8,32,128]{2,1,0:T(8,128)S(1)}, f32[32,128]{1,0:T(8,128)S(1)}, f32[32,128]{1,0:T(8,128)S(1)}, f32[32,128]{1,0:T(8,128)S(1)}) custom-call(f32[32,128]{1,0:T(8,128)S(1)} %get-tuple-element.21.own, f32[32,128]{1,0:T(8,128)S(1)} %collective-permute-done.2.by1, f32[32,128]{1,0:T(8,128)S(1)} %collective-permute-done.3.by2, ...), custom_call_target="tpu_custom_call" | custom-call | flops 8000000 | bytes 1638400 | tf_op jit(solution)/shard_map/pallas_call | solution.py:372
  18.6 0.1 collective-permute-start.5
  18.7 7.1 %collective-permute-start.6 = (f32[32,128]{1,0:T(8,128)S(1)}, f32[32,128]{1,0:T(8,128)S(1)}, u32[]{:S(2)}, u32[]{:S(2)}) collective-permute-start(f32[32,128]{1,0:T(8,128)S(1)} %get-tuple-element.33), channel_id=1, source_target_pairs={{4,8},{5,9},{6,10},{7,11},{8,4},{9,5},{10,6},{11,7},{12,16},{13,17... | collective-permute-start | bytes 49160 | tf_op jit(solution)/shard_map/ppermute | solution.py:421
  25.8 0.9 %shard_map.99 = (f32[2,64,256]{2,1,0:T(8,128)}, f32[32,128]{1,0:T(8,128)S(1)}) custom-call(f32[8,32,128]{2,1,0:T(8,128)S(1)} %get-tuple-element.26.grad, f32[32,128]{1,0:T(8,128)S(1)} %get-tuple-element.27.columns, f32[8,32,128]{2,1,0:T(8,128)S(1)} %get-tuple-element.28.fields, f32[27,8,512]{2,1,0:T(8,128)S(1)} %copy-done, ...), custom_call_target="tpu_custom_call" | custom-call | flops 4000000 | bytes 901120 | tf_op jit(solution)/shard_map/pallas_call | solution.py:372
  26.7 0.0 collective-permute-done.5.even
  26.7 1.0 %collective-permute-done.6.odd = f32[32,128]{1,0:T(8,128)S(1)} collective-permute-done((f32[32,128]{1,0:T(8,128)S(1)}, f32[32,128]{1,0:T(8,128)S(1)}, u32[]{:S(2)}, u32[]{:S(2)}) %collective-permute-start.6) | collective-permute-done | bytes 16416 | tf_op jit(solution)/shard_map/ppermute | solution.py:421
  27.7 0.6 %shard_map.100 = f32[32,128]{1,0:T(8,128)} custom-call(f32[32,128]{1,0:T(8,128)S(1)} %get-tuple-element.31.own, f32[32,128]{1,0:T(8,128)S(1)} %collective-permute-done.5.even, f32[32,128]{1,0:T(8,128)S(1)} %collective-permute-done.6.odd), custom_call_target="tpu_custom_call" | custom-call | flops 10000 | bytes 65536 | tf_op jit(solution)/shard_map/pallas_call | solution.py:372
Async XLA Ops:
  0.6 12.7 %copy-start = (f32[27,8,512]{2,1,0:T(8,128)S(1)}, f32[27,8,512]{2,1,0:T(8,128)}, u32[]{:S(2)}) copy-start(f32[27,8,512]{2,1,0:T(8,128)} %kernels.7) | copy-start | bytes 1327108
  0.6 12.7 %collective-permute-start.1 = (f32[32,128]{1,0:T(8,128)}, f32[32,128]{1,0:T(8,128)S(1)}, u32[]{:S(2)}, u32[]{:S(2)}) collective-permute-start(f32[32,128]{1,0:T(8,128)} %bitcast.7), channel_id=1, source_target_pairs={{0,4},{4,0},{8,12},{12,8},{16,20},{20,16},{24,28},{28,24},{32,36},... | collective-permute-start | bytes 49160 | tf_op jit(solution)/shard_map/ppermute | solution.py:394
  4.0 9.4 %collective-permute-start = (f32[32,128]{1,0:T(8,128)}, f32[32,128]{1,0:T(8,128)S(1)}, u32[]{:S(2)}, u32[]{:S(2)}) collective-permute-start(f32[32,128]{1,0:T(8,128)} %bitcast.8), channel_id=1, source_target_pairs={{4,8},{5,9},{6,10},{7,11},{8,4},{9,5},{10,6},{11,7},{12,16},{13,17... | collective-permute-start | bytes 49160 | tf_op jit(solution)/shard_map/ppermute | solution.py:393
  11.2 2.2 %copy-start.1 = (f32[1,1,32,128]{3,2,1,0:T(8,128)S(1)}, f32[1,1,32,128]{3,2,1,0:T(8,128)}, u32[]{:S(2)}) copy-start(f32[1,1,32,128]{3,2,1,0:T(8,128)} %param.8) | copy-start | bytes 49156
  14.0 3.3 %collective-permute-start.4 = (f32[32,128]{1,0:T(8,128)S(1)}, f32[32,128]{1,0:T(8,128)S(1)}, u32[]{:S(2)}, u32[]{:S(2)}) collective-permute-start(f32[32,128]{1,0:T(8,128)S(1)} %get-tuple-element.21.own), channel_id=1, source_target_pairs={{0,3},{1,2},{2,1},{3,0},{4,7},{5,6},{6,5},{7,4},{8,11},{9,10},{10,... | collective-permute-start | bytes 49160 | tf_op jit(solution)/shard_map/ppermute | solution.py:412
  14.1 3.8 %collective-permute-start.3 = (f32[32,128]{1,0:T(8,128)S(1)}, f32[32,128]{1,0:T(8,128)S(1)}, u32[]{:S(2)}, u32[]{:S(2)}) collective-permute-start(f32[32,128]{1,0:T(8,128)S(1)} %get-tuple-element.21.own), channel_id=1, source_target_pairs={{0,2},{1,3},{2,0},{3,1},{4,6},{5,7},{6,4},{7,5},{8,10},{9,11},{10,... | collective-permute-start | bytes 49160 | tf_op jit(solution)/shard_map/ppermute | solution.py:412
  15.8 2.1 %collective-permute-start.2 = (f32[32,128]{1,0:T(8,128)S(1)}, f32[32,128]{1,0:T(8,128)S(1)}, u32[]{:S(2)}, u32[]{:S(2)}) collective-permute-start(f32[32,128]{1,0:T(8,128)S(1)} %get-tuple-element.21.own), channel_id=1, source_target_pairs={{0,1},{1,0},{2,3},{3,2},{4,5},{5,4},{6,7},{7,6},{8,9},{9,8},{10,11... | collective-permute-start | bytes 49160 | tf_op jit(solution)/shard_map/ppermute | solution.py:412
  18.6 8.0 %collective-permute-start.5 = (f32[32,128]{1,0:T(8,128)S(1)}, f32[32,128]{1,0:T(8,128)S(1)}, u32[]{:S(2)}, u32[]{:S(2)}) collective-permute-start(f32[32,128]{1,0:T(8,128)S(1)} %get-tuple-element.32), channel_id=1, source_target_pairs={{0,4},{4,0},{8,12},{12,8},{16,20},{20,16},{24,28},{28,24},{32,36},... | collective-permute-start | bytes 49160 | tf_op jit(solution)/shard_map/ppermute | solution.py:420
  18.7 8.9 %collective-permute-start.6 = (f32[32,128]{1,0:T(8,128)S(1)}, f32[32,128]{1,0:T(8,128)S(1)}, u32[]{:S(2)}, u32[]{:S(2)}) collective-permute-start(f32[32,128]{1,0:T(8,128)S(1)} %get-tuple-element.33), channel_id=1, source_target_pairs={{4,8},{5,9},{6,10},{7,11},{8,4},{9,5},{10,6},{11,7},{12,16},{13,17... | collective-permute-start | bytes 49160 | tf_op jit(solution)/shard_map/ppermute | solution.py:421

commit v7 on v6

--- a/solution.py
+++ b/solution.py
@@ -145,7 +145,7 @@
     return jnp.where(first, odd, even), jnp.where(first, even, odd)
 
 
-def forward(coarse, odd, even, base, kernels, stars, sums, dens, prod, table):
+def forward(coarse, odd, even, base, kernels, stars, sums, dens, table):
     shard = lax.axis_index("rad")
     step = 1.0 / 1024
     acc = [base[q] for q in range(8)]
@@ -169,18 +169,11 @@
         d = jnp.exp(acc[q])
         dens[q] = d
         density.append(jnp.where(inner, d, 0.0))
-    pairs = jnp.concatenate([density[2 * p] + density[2 * p + 1] for p in range(4)], axis=0)
-    strict = (rows((128, 128)) < lanes((128, 128))).astype(F32)
-    before = jnp.dot(pairs, strict, precision=HI, preferred_element_type=F32)
     for p in range(4):
-        first = before[32 * p : 32 * p + 32] + density[2 * p]
-        second = first + density[2 * p + 1]
-        first = weighed(step * first, stars[0, pixels(p), :])
-        total = second[:, 127:128]
-        second = weighed(step * second, stars[1, pixels(p), :])
-        prod[2 * p] = first
-        prod[2 * p + 1] = second
-        share = jnp.sum(first + second, axis=1, keepdims=True)
+        first, second = density[2 * p], density[2 * p + 1]
+        share = weighed(first, stars[2, pixels(p), :]) + weighed(second, stars[3, pixels(p), :])
+        total = jnp.sum(first + second, axis=1, keepdims=True)
+        share = step * jnp.sum(share, axis=1, keepdims=True)
         for k in range(2):
             out = jnp.where(lane == 16 + 2 * p + k, total, out)
             out = jnp.where(lane == 24 + 2 * p + k, share, out)
@@ -231,7 +224,20 @@
     return total
 
 
-def middle(prod, stars, kernels, share, weights):
+def middle(dens, stars, kernels, share, weights):
+    step = 1.0 / 1024
+    lane = lanes((32, 128))
+    inner = (lane > 0) & (lane < 127)
+    density = [jnp.where(inner, dens[q], 0.0) for q in range(8)]
+    pairs = jnp.concatenate([density[2 * p] + density[2 * p + 1] for p in range(4)], axis=0)
+    strict = (rows((128, 128)) < lanes((128, 128))).astype(F32)
+    before = jnp.dot(pairs, strict, precision=HI, preferred_element_type=F32)
+    prod = []
+    for p in range(4):
+        first = before[32 * p : 32 * p + 32] + density[2 * p]
+        second = first + density[2 * p + 1]
+        prod.append(weighed(step * first, stars[0, pixels(p), :]))
+        prod.append(weighed(step * second, stars[1, pixels(p), :]))
     pairs = jnp.concatenate([prod[2 * p] + prod[2 * p + 1] for p in range(4)], axis=0)
     beyond = (rows((128, 128)) > lanes((128, 128))).astype(F32)
     after = jnp.dot(pairs, beyond, precision=HI, preferred_element_type=F32)
@@ -405,13 +411,13 @@
          pltpu.VMEM((2, 16, 64), F32), pltpu.VMEM((2, 16, 64), F32), pltpu.SemaphoreType.DMA((11,))],
         pltpu.HBM,
     )
-    dens, prod, table = call(
+    dens, table = call(
         forward, (own, odd, even, base, kernels, stars, sums),
-        (block, block, row), 6_000_000,
+        (block, row), 6_000_000,
     )
     others = [lax.ppermute(table, "rad", [(i, i ^ k) for i in range(4)]) for k in (1, 2, 3)]
     share, weights = call(
-        middle, (prod, stars, kernels), (block, ((4, 2, 9, 8, 128), F32)), 1_000_000,
+        middle, (dens, stars, kernels), (block, ((4, 2, 9, 8, 128), F32)), 1_000_000,
     )
     grad, columns, odd, even = call(
         backward, (table, *others, dens, share, weights, kernels, stars),

time: 28.4 us -> 28.3 us (level)
  transfers between devices with their start and end apart: 7 -> 7, of which waited for: 3 -> 3; matrix products, arithmetic and copies ran while one was open for 0% -> 0% of each run, Pallas kernels for 11% -> 12%
where the time goes in v7:
time: 28.3 us; the launch traced here: 28.1 us
  starting transfers between devices  19.6 us (69%)
  Pallas kernels  5.24 us (19%)
  waiting for transfers between devices  2.53 us (9%)
  between operations  0.72 us (3%)
    ppermute x1, starting transfers between devices, per_device(): odd = lax.ppermute(own, ('ang', 'rad'), hops)  7.2 us
    ppermute x1, starting transfers between devices, per_device(): odd = lax.ppermute(odd, ('ang', 'rad'), hops)  7.05 us
    pallas_call x6, Pallas kernels, call(): pl.pallas_call(body, out_shape=shapes, in_specs=[pl.BlockSpec(memory_spac...  5.24 us
    ppermute x1, starting transfers between devices, per_device(): even = lax.ppermute(own, 'ang', pairs[0])  3.36 us
    ppermute x3, starting transfers between devices, per_device(): lax.ppermute(table, 'rad', [(i, i ^ k) for i in range(4)])  1.94 us
    ppermute x3, waiting for transfers between devices, per_device(): lax.ppermute(table, 'rad', [(i, i ^ k) for i in range(4)])  1.51 us
    ppermute x1, waiting for transfers between devices, per_device(): odd = lax.ppermute(odd, ('ang', 'rad'), hops)  1.01 us
  transfers between devices with their start and end apart: 7, of which 3 were waited for; matrix products, arithmetic and copies ran while one was open for 0% of the time, Pallas kernels for 12%

profile of v7, /device:TPU:6, one launch (start us, length us, event | category | flops | bytes accessed | tf_op | source)
XLA Modules:
  0.0 28.1 jit_solution(3122585122875334475)
XLA Ops:
  0.6 0.0 copy-start
  0.6 3.4 %collective-permute-start.1 = (f32[32,128]{1,0:T(8,128)}, f32[32,128]{1,0:T(8,128)S(1)}, u32[]{:S(2)}, u32[]{:S(2)}) collective-permute-start(f32[32,128]{1,0:T(8,128)} %bitcast.7), channel_id=1, source_target_pairs={{0,4},{4,0},{8,12},{12,8},{16,20},{20,16},{24,28},{28,24},{32,36},... | collective-permute-start | bytes 49160 | tf_op jit(solution)/shard_map/ppermute | solution.py:400
  4.0 7.2 %collective-permute-start = (f32[32,128]{1,0:T(8,128)}, f32[32,128]{1,0:T(8,128)S(1)}, u32[]{:S(2)}, u32[]{:S(2)}) collective-permute-start(f32[32,128]{1,0:T(8,128)} %bitcast.8), channel_id=1, source_target_pairs={{4,8},{5,9},{6,10},{7,11},{8,4},{9,5},{10,6},{11,7},{12,16},{13,17... | collective-permute-start | bytes 49160 | tf_op jit(solution)/shard_map/ppermute | solution.py:399
  11.2 0.0 copy-start.1
  11.2 2.1 %shard_map.95 = (f32[8,32,128]{2,1,0:T(8,128)S(1)}, f32[8,32,128]{2,1,0:T(8,128)S(1)}, f32[6,128,128]{2,1,0:T(8,128)S(1)}, f32[32,128]{1,0:T(8,128)S(1)}, f32[8,8,128]{2,1,0:T(8,128)S(1)}) custom-call(f32[32,128]{1,0:T(8,128)} %bitcast.9, f32[2,64,256]{2,1,0:T(8,128)} %bitcast.11, f32[27,8,512]{2,1,0:T(8,128)} %kernels.7, f32[8,8,512]{2,1,0:T(8,128)} %mixing_in.1, ...), custom_call_target="tpu_custom_call" | custom-call | flops 4000000 | bytes 1450496 | tf_op jit(solution)/shard_map/pallas_call | solution.py:378
  13.3 0.0 collective-permute-done.1.even
  13.4 0.0 collective-permute-done.odd
  13.4 0.0 copy-done
  13.4 0.0 copy-done.1
  13.4 0.5 %shard_map.96 = (f32[8,32,128]{2,1,0:T(8,128)S(1)}, f32[32,128]{1,0:T(8,128)S(1)}) custom-call(f32[32,128]{1,0:T(8,128)S(1)} %bitcast.10, f32[32,128]{1,0:T(8,128)S(1)} %collective-permute-done.odd, f32[32,128]{1,0:T(8,128)S(1)} %collective-permute-done.1.even, f32[8,32,128]{2,1,0:T(8,128)S(1)} %get-tuple-element.17.base, f32[27,8,512]{2,1,0:T(8,128)S(1)} %copy-done, ...), custom_call_target="tpu_custom_call" | custom-call | flops 6000000 | bytes 1179648 | tf_op jit(solution)/shard_map/pallas_call | solution.py:378
  13.9 0.1 collective-permute-start.4
  14.0 1.7 %collective-permute-start.3 = (f32[32,128]{1,0:T(8,128)S(1)}, f32[32,128]{1,0:T(8,128)S(1)}, u32[]{:S(2)}, u32[]{:S(2)}) collective-permute-start(f32[32,128]{1,0:T(8,128)S(1)} %get-tuple-element.20.own), channel_id=1, source_target_pairs={{0,2},{1,3},{2,0},{3,1},{4,6},{5,7},{6,4},{7,5},{8,10},{9,11},{10,... | collective-permute-start | bytes 49160 | tf_op jit(solution)/shard_map/ppermute | solution.py:418
  15.7 0.1 collective-permute-start.2
  15.8 0.5 %shard_map.97 = (f32[8,32,128]{2,1,0:T(8,128)S(1)}, f32[4,2,9,8,128]{4,3,2,1,0:T(8,128)S(1)}) custom-call(f32[8,32,128]{2,1,0:T(8,128)S(1)} %get-tuple-element.21.dens, f32[6,128,128]{2,1,0:T(8,128)S(1)} %get-tuple-element.18.stars, f32[27,8,512]{2,1,0:T(8,128)S(1)} %copy-done), custom_call_target="tpu_custom_call" | custom-call | flops 1000000 | bytes 1392640 | tf_op jit(solution)/shard_map/pallas_call | solution.py:378
  16.3 0.8 %collective-permute-done.4.by3 = f32[32,128]{1,0:T(8,128)S(1)} collective-permute-done((f32[32,128]{1,0:T(8,128)S(1)}, f32[32,128]{1,0:T(8,128)S(1)}, u32[]{:S(2)}, u32[]{:S(2)}) %collective-permute-start.4) | collective-permute-done | bytes 16416 | tf_op jit(solution)/shard_map/ppermute | solution.py:418
  17.1 0.7 %collective-permute-done.3.by2 = f32[32,128]{1,0:T(8,128)S(1)} collective-permute-done((f32[32,128]{1,0:T(8,128)S(1)}, f32[32,128]{1,0:T(8,128)S(1)}, u32[]{:S(2)}, u32[]{:S(2)}) %collective-permute-start.3) | collective-permute-done | bytes 16416 | tf_op jit(solution)/shard_map/ppermute | solution.py:418
  17.8 0.0 collective-permute-done.2.by1
  17.8 0.7 %shard_map.98 = (f32[8,32,128]{2,1,0:T(8,128)S(1)}, f32[32,128]{1,0:T(8,128)S(1)}, f32[32,128]{1,0:T(8,128)S(1)}, f32[32,128]{1,0:T(8,128)S(1)}) custom-call(f32[32,128]{1,0:T(8,128)S(1)} %get-tuple-element.20.own, f32[32,128]{1,0:T(8,128)S(1)} %collective-permute-done.2.by1, f32[32,128]{1,0:T(8,128)S(1)} %collective-permute-done.3.by2, ...), custom_call_target="tpu_custom_call" | custom-call | flops 8000000 | bytes 1638400 | tf_op jit(solution)/shard_map/pallas_call | solution.py:378
  18.5 0.1 collective-permute-start.5
  18.6 7.1 %collective-permute-start.6 = (f32[32,128]{1,0:T(8,128)S(1)}, f32[32,128]{1,0:T(8,128)S(1)}, u32[]{:S(2)}, u32[]{:S(2)}) collective-permute-start(f32[32,128]{1,0:T(8,128)S(1)} %get-tuple-element.31), channel_id=1, source_target_pairs={{4,8},{5,9},{6,10},{7,11},{8,4},{9,5},{10,6},{11,7},{12,16},{13,17... | collective-permute-start | bytes 49160 | tf_op jit(solution)/shard_map/ppermute | solution.py:427
  25.6 0.9 %shard_map.99 = (f32[2,64,256]{2,1,0:T(8,128)}, f32[32,128]{1,0:T(8,128)S(1)}) custom-call(f32[8,32,128]{2,1,0:T(8,128)S(1)} %get-tuple-element.24.grad, f32[32,128]{1,0:T(8,128)S(1)} %get-tuple-element.25.columns, f32[8,32,128]{2,1,0:T(8,128)S(1)} %get-tuple-element.26.fields, f32[27,8,512]{2,1,0:T(8,128)S(1)} %copy-done, ...), custom_call_target="tpu_custom_call" | custom-call | flops 4000000 | bytes 901120 | tf_op jit(solution)/shard_map/pallas_call | solution.py:378
  26.5 0.0 collective-permute-done.5.even
  26.5 1.0 %collective-permute-done.6.odd = f32[32,128]{1,0:T(8,128)S(1)} collective-permute-done((f32[32,128]{1,0:T(8,128)S(1)}, f32[32,128]{1,0:T(8,128)S(1)}, u32[]{:S(2)}, u32[]{:S(2)}) %collective-permute-start.6) | collective-permute-done | bytes 16416 | tf_op jit(solution)/shard_map/ppermute | solution.py:427
  27.5 0.6 %shard_map.100 = f32[32,128]{1,0:T(8,128)} custom-call(f32[32,128]{1,0:T(8,128)S(1)} %get-tuple-element.29.own, f32[32,128]{1,0:T(8,128)S(1)} %collective-permute-done.5.even, f32[32,128]{1,0:T(8,128)S(1)} %collective-permute-done.6.odd), custom_call_target="tpu_custom_call" | custom-call | flops 10000 | bytes 65536 | tf_op jit(solution)/shard_map/pallas_call | solution.py:378
Async XLA Ops:
  0.6 12.7 %copy-start = (f32[27,8,512]{2,1,0:T(8,128)S(1)}, f32[27,8,512]{2,1,0:T(8,128)}, u32[]{:S(2)}) copy-start(f32[27,8,512]{2,1,0:T(8,128)} %kernels.7) | copy-start | bytes 1327108
  0.6 12.7 %collective-permute-start.1 = (f32[32,128]{1,0:T(8,128)}, f32[32,128]{1,0:T(8,128)S(1)}, u32[]{:S(2)}, u32[]{:S(2)}) collective-permute-start(f32[32,128]{1,0:T(8,128)} %bitcast.7), channel_id=1, source_target_pairs={{0,4},{4,0},{8,12},{12,8},{16,20},{20,16},{24,28},{28,24},{32,36},... | collective-permute-start | bytes 49160 | tf_op jit(solution)/shard_map/ppermute | solution.py:400
  4.0 9.4 %collective-permute-start = (f32[32,128]{1,0:T(8,128)}, f32[32,128]{1,0:T(8,128)S(1)}, u32[]{:S(2)}, u32[]{:S(2)}) collective-permute-start(f32[32,128]{1,0:T(8,128)} %bitcast.8), channel_id=1, source_target_pairs={{4,8},{5,9},{6,10},{7,11},{8,4},{9,5},{10,6},{11,7},{12,16},{13,17... | collective-permute-start | bytes 49160 | tf_op jit(solution)/shard_map/ppermute | solution.py:399
  11.2 2.2 %copy-start.1 = (f32[1,1,32,128]{3,2,1,0:T(8,128)S(1)}, f32[1,1,32,128]{3,2,1,0:T(8,128)}, u32[]{:S(2)}) copy-start(f32[1,1,32,128]{3,2,1,0:T(8,128)} %param.8) | copy-start | bytes 49156
  13.9 3.3 %collective-permute-start.4 = (f32[32,128]{1,0:T(8,128)S(1)}, f32[32,128]{1,0:T(8,128)S(1)}, u32[]{:S(2)}, u32[]{:S(2)}) collective-permute-start(f32[32,128]{1,0:T(8,128)S(1)} %get-tuple-element.20.own), channel_id=1, source_target_pairs={{0,3},{1,2},{2,1},{3,0},{4,7},{5,6},{6,5},{7,4},{8,11},{9,10},{10,... | collective-permute-start | bytes 49160 | tf_op jit(solution)/shard_map/ppermute | solution.py:418
  14.0 3.8 %collective-permute-start.3 = (f32[32,128]{1,0:T(8,128)S(1)}, f32[32,128]{1,0:T(8,128)S(1)}, u32[]{:S(2)}, u32[]{:S(2)}) collective-permute-start(f32[32,128]{1,0:T(8,128)S(1)} %get-tuple-element.20.own), channel_id=1, source_target_pairs={{0,2},{1,3},{2,0},{3,1},{4,6},{5,7},{6,4},{7,5},{8,10},{9,11},{10,... | collective-permute-start | bytes 49160 | tf_op jit(solution)/shard_map/ppermute | solution.py:418
  15.7 2.1 %collective-permute-start.2 = (f32[32,128]{1,0:T(8,128)S(1)}, f32[32,128]{1,0:T(8,128)S(1)}, u32[]{:S(2)}, u32[]{:S(2)}) collective-permute-start(f32[32,128]{1,0:T(8,128)S(1)} %get-tuple-element.20.own), channel_id=1, source_target_pairs={{0,1},{1,0},{2,3},{3,2},{4,5},{5,4},{6,7},{7,6},{8,9},{9,8},{10,11... | collective-permute-start | bytes 49160 | tf_op jit(solution)/shard_map/ppermute | solution.py:418
  18.5 8.0 %collective-permute-start.5 = (f32[32,128]{1,0:T(8,128)S(1)}, f32[32,128]{1,0:T(8,128)S(1)}, u32[]{:S(2)}, u32[]{:S(2)}) collective-permute-start(f32[32,128]{1,0:T(8,128)S(1)} %get-tuple-element.30), channel_id=1, source_target_pairs={{0,4},{4,0},{8,12},{12,8},{16,20},{20,16},{24,28},{28,24},{32,36},... | collective-permute-start | bytes 49160 | tf_op jit(solution)/shard_map/ppermute | solution.py:426
  18.6 8.9 %collective-permute-start.6 = (f32[32,128]{1,0:T(8,128)S(1)}, f32[32,128]{1,0:T(8,128)S(1)}, u32[]{:S(2)}, u32[]{:S(2)}) collective-permute-start(f32[32,128]{1,0:T(8,128)S(1)} %get-tuple-element.31), channel_id=1, source_target_pairs={{4,8},{5,9},{6,10},{7,11},{8,4},{9,5},{10,6},{11,7},{12,16},{13,17... | collective-permute-start | bytes 49160 | tf_op jit(solution)/shard_map/ppermute | solution.py:427

commit v8 on v7

--- a/solution.py
+++ b/solution.py
@@ -145,24 +145,43 @@
     return jnp.where(first, odd, even), jnp.where(first, even, odd)
 
 
-def forward(coarse, odd, even, base, kernels, stars, sums, dens, table):
+def even_side():
+    return 2 * (1 - (lax.axis_index("ang") & 1))
+
+
+def even_row(coarse, first_hop, last_hop, base, kernels, sums, base_out, sums_out):
+    u = even_side()
+    here = pl.ds(pl.multiple_of(lax.axis_index("rad") * 128, 128), 128)
+    even = jnp.where(lax.axis_index("ang") % 4 < 2, first_hop[...], last_hop[...])
+    acc = [base[q] for q in range(8)]
+    taps(acc, even, [kernels[9 * u + t, :, here] for t in range(9)])
+    for q in range(8):
+        base_out[q] = acc[q]
+    lane = lanes((32, 128))
+    out = sums[...]
+    for at, value in ((1, coarse[...]), (u, even)):
+        out = jnp.where(lane == 32 + at, value[:, 0:1], out)
+        out = jnp.where(lane == 35 + at, value[:, 127:128], out)
+    sums_out[...] = out
+
+
+def forward(odd, base, kernels, stars, sums, dens, table):
     shard = lax.axis_index("rad")
     step = 1.0 / 1024
     acc = [base[q] for q in range(8)]
     place = lax.axis_index("ang")
     met = (place > 0) & (place < lax.axis_size("ang") - 1)
-    low, high = sides(jnp.where(met, odd[...], 0.0), even[...])
+    row = jnp.where(met, odd[...], 0.0)
+    u = 2 - even_side()
     here = pl.ds(pl.multiple_of(shard * 128, 128), 128)
-    taps(acc, low, [kernels[t, :, here] for t in range(9)])
-    taps(acc, high, [kernels[t, :, here] for t in range(18, 27)])
+    taps(acc, row, [kernels[9 * u + t, :, here] for t in range(9)])
     lane = lanes((32, 128))
     out = sums[...]
     for q in range(8):
         out = jnp.where(lane == q, acc[q][:, 0:1], out)
         out = jnp.where(lane == 8 + q, acc[q][:, 127:128], out)
-    for u, value in enumerate((low, coarse[...], high)):
-        out = jnp.where(lane == 32 + u, value[:, 0:1], out)
-        out = jnp.where(lane == 35 + u, value[:, 127:128], out)
+    out = jnp.where(lane == 32 + u, row[:, 0:1], out)
+    out = jnp.where(lane == 35 + u, row[:, 127:128], out)
     inner = (lane > 0) & (lane < 127)
     density = []
     for q in range(8):
@@ -396,8 +415,17 @@
     hops = [(a * near + r, b * near + r) for a, b in pairs[1] for r in range(near)]
     hops += [(a * near + r, a * near + (r ^ 1)) for a in (0, count - 1) for r in range(near)]
     own = coarse[0, 0]
+
+    def part(keep):
+        hops = []
+        for a in range(count):
+            b = a ^ 1
+            hops += [(a * near + r, b * near + r if keep(a % 4) else a * near + (r ^ 1)) for r in range(near)]
+        return hops
+
+    first = lax.ppermute(own, ("ang", "rad"), part(lambda z: z < 2))
     odd = lax.ppermute(own, ("ang", "rad"), hops)
-    even = lax.ppermute(own, "ang", pairs[0])
+    last = lax.ppermute(own, ("ang", "rad"), part(lambda z: z >= 2))
     block = ((8, 32, 128), F32)
     row = ((32, 128), F32)
     stars = [x.transpose(0, 2, 1) for x in (star_bin, star_obs, star_isig)]
@@ -411,8 +439,9 @@
          pltpu.VMEM((2, 16, 64), F32), pltpu.VMEM((2, 16, 64), F32), pltpu.SemaphoreType.DMA((11,))],
         pltpu.HBM,
     )
+    base, sums = call(even_row, (own, first, last, base, kernels, sums), (block, row), 3_000_000)
     dens, table = call(
-        forward, (own, odd, even, base, kernels, stars, sums),
+        forward, (odd, base, kernels, stars, sums),
         (block, row), 6_000_000,
     )
     others = [lax.ppermute(table, "rad", [(i, i ^ k) for i in range(4)]) for k in (1, 2, 3)]

time: 28.3 us -> 29.1 us (1.028)
  waiting for transfers between devices: 2.53 us -> 4.09 us
  starting transfers between devices: 19.6 us -> 18.8 us
    ppermute x1, waiting for transfers between devices: 1.01 us -> 1.81 us  [per_device(): odd = lax.ppermute(odd, ('ang', 'rad'), hops)]
    ppermute x1, starting transfers between devices: 7.05 us -> 6.25 us  [per_device(): odd = lax.ppermute(odd, ('ang', 'rad'), hops)]
    ppermute x3, waiting for transfers between devices: 1.51 us -> 2.27 us  [per_device(): lax.ppermute(table, 'rad', [(i, i ^ k) for i in range(4)])]
    ppermute x1 -> x2, starting transfers between devices: 3.36 us -> 3.45 us  [the longest x1 3.36 us: per_device(): first = lax.ppermute(own, ('ang', 'rad'), part(lambda z: z < 2))]
    pallas_call x6 -> x7, Pallas kernels: 5.24 us -> 5.3 us  [call(): pl.pallas_call(body, out_shape=shapes, in_specs=[pl.BlockSpec(memory_spac...]
  transfers between devices with their start and end apart: 7 -> 8, of which waited for: 3 -> 3; matrix products, arithmetic and copies ran while one was open for 0% -> 0% of each run, Pallas kernels for 12% -> 13%
where the time goes in v8:
time: 29.1 us; the launch traced here: 29 us
  starting transfers between devices  18.8 us (65%)
  Pallas kernels  5.3 us (18%)
  waiting for transfers between devices  4.09 us (14%)
  between operations  0.74 us (3%)
    ppermute x1, starting transfers between devices, per_device(): odd = lax.ppermute(own, ('ang', 'rad'), hops)  7.1 us
    ppermute x1, starting transfers between devices, per_device(): odd = lax.ppermute(odd, ('ang', 'rad'), hops)  6.25 us
    pallas_call x7, Pallas kernels, call(): pl.pallas_call(body, out_shape=shapes, in_specs=[pl.BlockSpec(memory_spac...  5.3 us
    ppermute x1, starting transfers between devices, per_device(): first = lax.ppermute(own, ('ang', 'rad'), part(lambda z: z < 2))  3.36 us
    ppermute x3, waiting for transfers between devices, per_device(): lax.ppermute(table, 'rad', [(i, i ^ k) for i in range(4)])  2.27 us
    ppermute x3, starting transfers between devices, per_device(): lax.ppermute(table, 'rad', [(i, i ^ k) for i in range(4)])  1.95 us
    ppermute x1, waiting for transfers between devices, per_device(): odd = lax.ppermute(odd, ('ang', 'rad'), hops)  1.81 us
  transfers between devices with their start and end apart: 8, of which 3 were waited for; matrix products, arithmetic and copies ran while one was open for 0% of the time, Pallas kernels for 13%

profile of v8, /device:TPU:6, one launch (start us, length us, event | category | flops | bytes accessed | tf_op | source)
XLA Modules:
  0.0 29.0 jit_solution(12476338594994124536)
XLA Ops:
  0.6 0.0 copy-start
  0.6 0.1 collective-permute-start.2
  0.7 3.4 %collective-permute-start.1 = (f32[32,128]{1,0:T(8,128)}, f32[32,128]{1,0:T(8,128)S(1)}, u32[]{:S(2)}, u32[]{:S(2)}) collective-permute-start(f32[32,128]{1,0:T(8,128)} %bitcast.8), channel_id=1, source_target_pairs={{0,4},{1,5},{2,6},{3,7},{4,0},{5,1},{6,2},{7,3},{8,9},{9,8},{10,11... | collective-permute-start | bytes 49160 | tf_op jit(solution)/shard_map/ppermute | solution.py:426
  4.1 7.1 %collective-permute-start = (f32[32,128]{1,0:T(8,128)}, f32[32,128]{1,0:T(8,128)S(1)}, u32[]{:S(2)}, u32[]{:S(2)}) collective-permute-start(f32[32,128]{1,0:T(8,128)} %bitcast.9), channel_id=1, source_target_pairs={{4,8},{5,9},{6,10},{7,11},{8,4},{9,5},{10,6},{11,7},{12,16},{13,17... | collective-permute-start | bytes 49160 | tf_op jit(solution)/shard_map/ppermute | solution.py:427
  11.2 2.1 %shard_map.95 = (f32[8,32,128]{2,1,0:T(8,128)S(1)}, f32[8,32,128]{2,1,0:T(8,128)S(1)}, f32[6,128,128]{2,1,0:T(8,128)S(1)}, f32[32,128]{1,0:T(8,128)S(1)}, f32[8,8,128]{2,1,0:T(8,128)S(1)}) custom-call(f32[32,128]{1,0:T(8,128)} %bitcast.10, f32[2,64,256]{2,1,0:T(8,128)} %bitcast.12, f32[27,8,512]{2,1,0:T(8,128)} %kernels.9, f32[8,8,512]{2,1,0:T(8,128)} %mixing_in.1, ...), custom_call_target="tpu_custom_call" | custom-call | flops 4000000 | bytes 1450496 | tf_op jit(solution)/shard_map/pallas_call | solution.py:397
  13.4 0.0 collective-permute-done.2.last_hop
  13.4 0.0 collective-permute-done.1.first_hop
  13.4 0.2 shard_map.96
  13.6 0.0 collective-permute-done.odd
  13.6 0.4 %shard_map.97 = (f32[8,32,128]{2,1,0:T(8,128)S(1)}, f32[32,128]{1,0:T(8,128)S(1)}) custom-call(f32[32,128]{1,0:T(8,128)S(1)} %collective-permute-done.odd, f32[8,32,128]{2,1,0:T(8,128)S(1)} %get-tuple-element.21.base, f32[27,8,512]{2,1,0:T(8,128)S(1)} %copy-done, f32[6,128,128]{2,1,0:T(8,128)S(1)} %get-tuple-element.22.stars, ...), custom_call_target="tpu_custom_call" | custom-call | flops 6000000 | bytes 1146880 | tf_op jit(solution)/shard_map/pallas_call | solution.py:397
  13.9 0.9 %collective-permute-start.5 = (f32[32,128]{1,0:T(8,128)S(1)}, f32[32,128]{1,0:T(8,128)S(1)}, u32[]{:S(2)}, u32[]{:S(2)}) collective-permute-start(f32[32,128]{1,0:T(8,128)S(1)} %get-tuple-element.24.own), channel_id=1, source_target_pairs={{0,3},{1,2},{2,1},{3,0},{4,7},{5,6},{6,5},{7,4},{8,11},{9,10},{10,... | collective-permute-start | bytes 49160 | tf_op jit(solution)/shard_map/ppermute | solution.py:447
  14.9 1.0 %collective-permute-start.4 = (f32[32,128]{1,0:T(8,128)S(1)}, f32[32,128]{1,0:T(8,128)S(1)}, u32[]{:S(2)}, u32[]{:S(2)}) collective-permute-start(f32[32,128]{1,0:T(8,128)S(1)} %get-tuple-element.24.own), channel_id=1, source_target_pairs={{0,2},{1,3},{2,0},{3,1},{4,6},{5,7},{6,4},{7,5},{8,10},{9,11},{10,... | collective-permute-start | bytes 49160 | tf_op jit(solution)/shard_map/ppermute | solution.py:447
  15.9 0.0 collective-permute-start.3
  15.9 0.5 %shard_map.98 = (f32[8,32,128]{2,1,0:T(8,128)S(1)}, f32[4,2,9,8,128]{4,3,2,1,0:T(8,128)S(1)}) custom-call(f32[8,32,128]{2,1,0:T(8,128)S(1)} %get-tuple-element.25.dens, f32[6,128,128]{2,1,0:T(8,128)S(1)} %get-tuple-element.22.stars, f32[27,8,512]{2,1,0:T(8,128)S(1)} %copy-done), custom_call_target="tpu_custom_call" | custom-call | flops 1000000 | bytes 1392640 | tf_op jit(solution)/shard_map/pallas_call | solution.py:397
  16.4 0.8 %collective-permute-done.5.by3 = f32[32,128]{1,0:T(8,128)S(1)} collective-permute-done((f32[32,128]{1,0:T(8,128)S(1)}, f32[32,128]{1,0:T(8,128)S(1)}, u32[]{:S(2)}, u32[]{:S(2)}) %collective-permute-start.5) | collective-permute-done | bytes 16416 | tf_op jit(solution)/shard_map/ppermute | solution.py:447
  17.2 1.4 %collective-permute-done.4.by2 = f32[32,128]{1,0:T(8,128)S(1)} collective-permute-done((f32[32,128]{1,0:T(8,128)S(1)}, f32[32,128]{1,0:T(8,128)S(1)}, u32[]{:S(2)}, u32[]{:S(2)}) %collective-permute-start.4) | collective-permute-done | bytes 16416 | tf_op jit(solution)/shard_map/ppermute | solution.py:447
  18.6 0.0 collective-permute-done.3.by1
  18.6 0.7 %shard_map.99 = (f32[8,32,128]{2,1,0:T(8,128)S(1)}, f32[32,128]{1,0:T(8,128)S(1)}, f32[32,128]{1,0:T(8,128)S(1)}, f32[32,128]{1,0:T(8,128)S(1)}) custom-call(f32[32,128]{1,0:T(8,128)S(1)} %get-tuple-element.24.own, f32[32,128]{1,0:T(8,128)S(1)} %collective-permute-done.3.by1, f32[32,128]{1,0:T(8,128)S(1)} %collective-permute-done.4.by2, ...), custom_call_target="tpu_custom_call" | custom-call | flops 8000000 | bytes 1638400 | tf_op jit(solution)/shard_map/pallas_call | solution.py:397
  19.3 0.1 collective-permute-start.6
  19.4 6.2 %collective-permute-start.7 = (f32[32,128]{1,0:T(8,128)S(1)}, f32[32,128]{1,0:T(8,128)S(1)}, u32[]{:S(2)}, u32[]{:S(2)}) collective-permute-start(f32[32,128]{1,0:T(8,128)S(1)} %get-tuple-element.35), channel_id=1, source_target_pairs={{4,8},{5,9},{6,10},{7,11},{8,4},{9,5},{10,6},{11,7},{12,16},{13,17... | collective-permute-start | bytes 49160 | tf_op jit(solution)/shard_map/ppermute | solution.py:456
  25.7 0.9 %shard_map.100 = (f32[2,64,256]{2,1,0:T(8,128)}, f32[32,128]{1,0:T(8,128)S(1)}) custom-call(f32[8,32,128]{2,1,0:T(8,128)S(1)} %get-tuple-element.28.grad, f32[32,128]{1,0:T(8,128)S(1)} %get-tuple-element.29.columns, f32[8,32,128]{2,1,0:T(8,128)S(1)} %get-tuple-element.30.fields, f32[27,8,512]{2,1,0:T(8,128)S(1)} %copy-done, ...), custom_call_target="tpu_custom_call" | custom-call | flops 4000000 | bytes 901120 | tf_op jit(solution)/shard_map/pallas_call | solution.py:397
  26.6 0.0 collective-permute-done.6.even
  26.6 1.8 %collective-permute-done.7.odd = f32[32,128]{1,0:T(8,128)S(1)} collective-permute-done((f32[32,128]{1,0:T(8,128)S(1)}, f32[32,128]{1,0:T(8,128)S(1)}, u32[]{:S(2)}, u32[]{:S(2)}) %collective-permute-start.7) | collective-permute-done | bytes 16416 | tf_op jit(solution)/shard_map/ppermute | solution.py:456
  28.4 0.6 %shard_map.101 = f32[32,128]{1,0:T(8,128)} custom-call(f32[32,128]{1,0:T(8,128)S(1)} %get-tuple-element.33.own, f32[32,128]{1,0:T(8,128)S(1)} %collective-permute-done.6.even, f32[32,128]{1,0:T(8,128)S(1)} %collective-permute-done.7.odd), custom_call_target="tpu_custom_call" | custom-call | flops 10000 | bytes 65536 | tf_op jit(solution)/shard_map/pallas_call | solution.py:397
  (3 shorter events, 0.0 us)
Async XLA Ops:
  0.6 12.7 %copy-start = (f32[27,8,512]{2,1,0:T(8,128)S(1)}, f32[27,8,512]{2,1,0:T(8,128)}, u32[]{:S(2)}) copy-start(f32[27,8,512]{2,1,0:T(8,128)} %kernels.9) | copy-start | bytes 1327108
  0.6 12.7 %collective-permute-start.2 = (f32[32,128]{1,0:T(8,128)}, f32[32,128]{1,0:T(8,128)S(1)}, u32[]{:S(2)}, u32[]{:S(2)}) collective-permute-start(f32[32,128]{1,0:T(8,128)} %bitcast.7), channel_id=1, source_target_pairs={{0,1},{1,0},{2,3},{3,2},{4,5},{5,4},{6,7},{7,6},{8,12},{9,13},{10,... | collective-permute-start | bytes 49160 | tf_op jit(solution)/shard_map/ppermute | solution.py:428
  0.7 12.6 %collective-permute-start.1 = (f32[32,128]{1,0:T(8,128)}, f32[32,128]{1,0:T(8,128)S(1)}, u32[]{:S(2)}, u32[]{:S(2)}) collective-permute-start(f32[32,128]{1,0:T(8,128)} %bitcast.8), channel_id=1, source_target_pairs={{0,4},{1,5},{2,6},{3,7},{4,0},{5,1},{6,2},{7,3},{8,9},{9,8},{10,11... | collective-permute-start | bytes 49160 | tf_op jit(solution)/shard_map/ppermute | solution.py:426
  4.1 9.5 %collective-permute-start = (f32[32,128]{1,0:T(8,128)}, f32[32,128]{1,0:T(8,128)S(1)}, u32[]{:S(2)}, u32[]{:S(2)}) collective-permute-start(f32[32,128]{1,0:T(8,128)} %bitcast.9), channel_id=1, source_target_pairs={{4,8},{5,9},{6,10},{7,11},{8,4},{9,5},{10,6},{11,7},{12,16},{13,17... | collective-permute-start | bytes 49160 | tf_op jit(solution)/shard_map/ppermute | solution.py:427
  11.2 2.2 %copy-start.1 = (f32[1,1,32,128]{3,2,1,0:T(8,128)S(1)}, f32[1,1,32,128]{3,2,1,0:T(8,128)}, u32[]{:S(2)}) copy-start(f32[1,1,32,128]{3,2,1,0:T(8,128)} %param.8) | copy-start | bytes 49156
  13.9 3.3 %collective-permute-start.5 = (f32[32,128]{1,0:T(8,128)S(1)}, f32[32,128]{1,0:T(8,128)S(1)}, u32[]{:S(2)}, u32[]{:S(2)}) collective-permute-start(f32[32,128]{1,0:T(8,128)S(1)} %get-tuple-element.24.own), channel_id=1, source_target_pairs={{0,3},{1,2},{2,1},{3,0},{4,7},{5,6},{6,5},{7,4},{8,11},{9,10},{10,... | collective-permute-start | bytes 49160 | tf_op jit(solution)/shard_map/ppermute | solution.py:447
  14.9 3.7 %collective-permute-start.4 = (f32[32,128]{1,0:T(8,128)S(1)}, f32[32,128]{1,0:T(8,128)S(1)}, u32[]{:S(2)}, u32[]{:S(2)}) collective-permute-start(f32[32,128]{1,0:T(8,128)S(1)} %get-tuple-element.24.own), channel_id=1, source_target_pairs={{0,2},{1,3},{2,0},{3,1},{4,6},{5,7},{6,4},{7,5},{8,10},{9,11},{10,... | collective-permute-start | bytes 49160 | tf_op jit(solution)/shard_map/ppermute | solution.py:447
  15.9 2.7 %collective-permute-start.3 = (f32[32,128]{1,0:T(8,128)S(1)}, f32[32,128]{1,0:T(8,128)S(1)}, u32[]{:S(2)}, u32[]{:S(2)}) collective-permute-start(f32[32,128]{1,0:T(8,128)S(1)} %get-tuple-element.24.own), channel_id=1, source_target_pairs={{0,1},{1,0},{2,3},{3,2},{4,5},{5,4},{6,7},{7,6},{8,9},{9,8},{10,11... | collective-permute-start | bytes 49160 | tf_op jit(solution)/shard_map/ppermute | solution.py:447
  19.3 7.2 %collective-permute-start.6 = (f32[32,128]{1,0:T(8,128)S(1)}, f32[32,128]{1,0:T(8,128)S(1)}, u32[]{:S(2)}, u32[]{:S(2)}) collective-permute-start(f32[32,128]{1,0:T(8,128)S(1)} %get-tuple-element.34), channel_id=1, source_target_pairs={{0,4},{4,0},{8,12},{12,8},{16,20},{20,16},{24,28},{28,24},{32,36},... | collective-permute-start | bytes 49160 | tf_op jit(solution)/shard_map/ppermute | solution.py:455
  19.4 8.9 %collective-permute-start.7 = (f32[32,128]{1,0:T(8,128)S(1)}, f32[32,128]{1,0:T(8,128)S(1)}, u32[]{:S(2)}, u32[]{:S(2)}) collective-permute-start(f32[32,128]{1,0:T(8,128)S(1)} %get-tuple-element.35), channel_id=1, source_target_pairs={{4,8},{5,9},{6,10},{7,11},{8,4},{9,5},{10,6},{11,7},{12,16},{13,17... | collective-permute-start | bytes 49160 | tf_op jit(solution)/shard_map/ppermute | solution.py:456
